TPU v7x, 32 devices: a whole 2x2x4 slice. The times are simulated.
32 devices in a mesh: dp: 8 (over z, y), mp: 4 (over x, core).
Axes of the slice: x: 2, y: 2, z: 4, core: 2. Of those that a mesh axis runs over, the one named last changes fastest.
Arguments:
- tokens: bfloat16 [64, 64, 1024], P(('dp', 'mp')), may hold values from -6 to 6
- lengths: int32 [64], P('dp'), may hold values from 32 to 64, as said below
- grid_order: int32 [64, 256], P(('dp', 'mp')), may hold values from 0 to 255, as said below
- grid_keep: int32 [64, 256], P(('dp', 'mp')), may hold values from 0 to 1, as said below
- ground_dist: float32 [64], P(('dp', 'mp')), may hold values from 0.5 to 4
- enc_norm: float32 [1024], replicated, may hold values from 0.5 to 1.5
- enc_query: bfloat16 [1024, 1024], P(None, 'mp'), may hold values from -0.1875 to 0.1875
- enc_key: bfloat16 [1024, 1024], P(None, 'mp'), may hold values from -0.1875 to 0.1875
- enc_value: bfloat16 [1024, 1024], P(None, 'mp'), may hold values from -0.1875 to 0.1875
- enc_proj: bfloat16 [1024, 1024], P('mp'), may hold values from -0.75 to 0.75
- enc_norm2: float32 [1024], replicated, may hold values from 0.5 to 1.5
- enc_up: bfloat16 [1024, 4096], P(None, 'mp'), may hold values from -0.1875 to 0.1875
- enc_down: bfloat16 [4096, 1024], P('mp'), may hold values from -0.09375 to 0.09375
- embed_proj: bfloat16 [1024, 512], P(None, 'mp'), may hold values from -0.1875 to 0.1875
- mask_token: float32 [512], replicated, may hold values from -4 to 4
- dec_norm: float32 [512], replicated, may hold values from 0.5 to 1.5
- dec_query: bfloat16 [512, 512], replicated, may hold values from -0.25 to 0.25
- dec_key: bfloat16 [512, 512], replicated, may hold values from -0.25 to 0.25
- dec_value: bfloat16 [512, 512], replicated, may hold values from -0.25 to 0.25
- dec_proj: bfloat16 [512, 512], replicated, may hold values from -2 to 2
- dec_norm2: float32 [512], replicated, may hold values from 0.5 to 1.5
- dec_up: bfloat16 [512, 2048], replicated, may hold values from -0.25 to 0.25
- dec_down: bfloat16 [2048, 512], replicated, may hold values from -0.125 to 0.125
- pred_proj: bfloat16 [512, 768], replicated, may hold values from -0.25 to 0.25
- cotangent: bfloat16 [64, 256, 768], P(('dp', 'mp')), may hold values from -6 to 6
Outputs:
- decoded: float32 [64, 256, 768], P(('dp', 'mp'))
- grad_tokens: float32 [64, 64, 1024], P(('dp', 'mp'))
- grad_enc_norm: float32 [1024], replicated
- grad_enc_query: float32 [1024, 1024], P('dp', 'mp')
- grad_enc_key: float32 [1024, 1024], P('dp', 'mp')
- grad_enc_value: float32 [1024, 1024], P('dp', 'mp')
- grad_enc_proj: float32 [1024, 1024], P('mp', 'dp')
- grad_enc_norm2: float32 [1024], replicated
- grad_enc_up: float32 [1024, 4096], P('dp', 'mp')
- grad_enc_down: float32 [4096, 1024], P('mp', 'dp')
- grad_embed_proj: float32 [1024, 512], P('dp', 'mp')
- grad_mask_token: float32 [512], replicated
- grad_dec_norm: float32 [512], replicated
- grad_dec_query: float32 [512, 512], P('dp', 'mp')
- grad_dec_key: float32 [512, 512], P('dp', 'mp')
- grad_dec_value: float32 [512, 512], P('dp', 'mp')
- grad_dec_proj: float32 [512, 512], P('dp', 'mp')
- grad_dec_norm2: float32 [512], replicated
- grad_dec_up: float32 [512, 2048], P('dp', 'mp')
- grad_dec_down: float32 [2048, 512], P('dp', 'mp')
- grad_pred_proj: float32 [512, 768], P('dp', 'mp')
Inputs may be any that keep to these rules, and one draw needn't show every extreme that they name: Rows 0 to lengths[i] - 1 of tokens are image i's visible patches; some image has exactly 64. `grid_order`: each row, images in grid order, is a permutation of the 256 positions; its first lengths entries of the same image are the positions of that image's visible rows, in row order. `grid_keep`: 1 exactly at the positions that grid_order lists among the image's first lengths entries.
All inputs are finite; a program needn't handle non-finite values.
Results may differ from a plain program's by a relative error of at most 0.03.
Values may be sent and summed in bfloat16 or wider, within the bound.
A program may use at most 192 MiB of HBM per device.

v0:
```python
import jax
import jax.numpy as jnp
from jax import lax
from jax.sharding import PartitionSpec as P

HE = 16
HD = 16
SIDE = 16
IPD = 1


eps_norm = 1e-06
masked_score = -1e30
low_type = jnp.bfloat16
full_type = jnp.float32


def layer_norm(values, scale_gain):
    center = values - jnp.mean(values, axis=-1, keepdims=True)
    spread = jnp.mean(center * center, axis=-1, keepdims=True)
    return center * lax.rsqrt(spread + eps_norm) * scale_gain


def exact_gelu(values):
    return jax.nn.gelu(values, approximate=False)


def matmul(left_side, right_side):
    flat_rows = left_side.reshape(-1, left_side.shape[-1])
    product = jnp.dot(flat_rows, right_side, preferred_element_type=full_type)
    return product.reshape(left_side.shape[:-1] + (right_side.shape[1],))


def matmul_t(left_side, right_side):
    flat_rows = left_side.reshape(-1, left_side.shape[-1])
    product = lax.dot_general(
        flat_rows, right_side, (((1,), (1,)), ((), ())), preferred_element_type=full_type
    )
    return product.reshape(left_side.shape[:-1] + (right_side.shape[0],))


def outer_sum(left_side, right_side):
    return lax.dot_general(
        left_side.reshape(-1, left_side.shape[-1]),
        right_side.reshape(-1, right_side.shape[-1]),
        (((0,), (0,)), ((), ())),
        preferred_element_type=full_type,
    )


def spread_rows(values, tensor_split):
    if tensor_split:
        return lax.all_gather(values, "mp", axis=0, tiled=True)
    return values


def collect_rows(values, tensor_split):
    if tensor_split:
        return lax.psum_scatter(
            values.astype(jnp.bfloat16), "mp", scatter_dimension=0, tiled=True
        ).astype(jnp.float32)
    return values


def images_per_block(images, length):
    grouped = 1
    while grouped * length < 512 and grouped < images:
        grouped = grouped * 2
    return grouped


def in_blocks(blocked_array, grouped):
    return blocked_array.reshape(
        (blocked_array.shape[0] // grouped, grouped) + blocked_array.shape[1:]
    )


def with_heads(blocked_array, head_count):
    return blocked_array.reshape(
        blocked_array.shape[:2] + (head_count, blocked_array.shape[2] // head_count)
    )


def attend_forward(queries, keys_all, values_all, key_valid, head_count):
    images, length, columns = queries.shape
    grouped = images_per_block(images, length)
    scaling = float(columns // head_count) ** (-0.5)

    def one_block(pieces):
        query_b, key_b, value_b, valid_b = pieces
        scores = (
            jnp.einsum("nqhd,nkhd->nhqk", query_b, key_b, preferred_element_type=full_type)
            * scaling
        )
        scores = jnp.where(valid_b[:, None, None, :], scores, masked_score)
        row_max = jnp.max(scores, axis=-1, keepdims=True)
        weights = jnp.exp(scores - row_max)
        totals = jnp.sum(weights, axis=-1, keepdims=True)
        prob_rows = (weights / totals).astype(low_type)
        mixed_b = jnp.einsum(
            "nhqk,nkhd->nqhd", prob_rows, value_b, preferred_element_type=full_type
        )
        return (mixed_b.astype(low_type), (row_max + jnp.log(totals))[..., 0])

    pieces_in = (
        in_blocks(with_heads(queries, head_count), grouped),
        in_blocks(with_heads(keys_all, head_count), grouped),
        in_blocks(with_heads(values_all, head_count), grouped),
        in_blocks(key_valid, grouped),
    )
    mixed_rows, log_total = lax.map(one_block, pieces_in)
    return (
        mixed_rows.reshape(images, length, columns),
        log_total.reshape(images, head_count, length),
    )


def attend_backward(queries, keys_all, values_all, key_valid, log_total, grad_mixed, head_count):
    images, length, columns = queries.shape
    grouped = images_per_block(images, length)
    scaling = float(columns // head_count) ** (-0.5)

    def one_block(pieces):
        query_b, key_b, value_b, valid_b, total_b, grad_b = pieces
        scores = (
            jnp.einsum("nqhd,nkhd->nhqk", query_b, key_b, preferred_element_type=full_type)
            * scaling
        )
        scores = jnp.where(valid_b[:, None, None, :], scores, masked_score)
        prob_rows = jnp.exp(scores - total_b[..., None])
        grad_value_b = jnp.einsum(
            "nhqk,nqhd->nkhd", prob_rows.astype(low_type), grad_b, preferred_element_type=full_type
        )
        grad_probs = jnp.einsum(
            "nqhd,nkhd->nhqk", grad_b, value_b, preferred_element_type=full_type
        )
        grad_scores = prob_rows * (
            grad_probs - jnp.sum(grad_probs * prob_rows, axis=-1, keepdims=True)
        )
        grad_scores = (grad_scores * scaling).astype(low_type)
        grad_query_b = jnp.einsum(
            "nhqk,nkhd->nqhd", grad_scores, key_b, preferred_element_type=full_type
        )
        grad_key_b = jnp.einsum(
            "nhqk,nqhd->nkhd", grad_scores, query_b, preferred_element_type=full_type
        )
        return (
            grad_query_b.astype(low_type),
            grad_key_b.astype(low_type),
            grad_value_b.astype(low_type),
        )

    pieces_in = (
        in_blocks(with_heads(queries, head_count), grouped),
        in_blocks(with_heads(keys_all, head_count), grouped),
        in_blocks(with_heads(values_all, head_count), grouped),
        in_blocks(key_valid, grouped),
        in_blocks(log_total, grouped),
        in_blocks(with_heads(grad_mixed, head_count), grouped),
    )
    grad_query, grad_key, grad_value = lax.map(one_block, pieces_in)
    return (
        grad_query.reshape(images, length, columns),
        grad_key.reshape(images, length, columns),
        grad_value.reshape(images, length, columns),
    )


def block_forward(inputs, key_valid, weights, head_count, tensor_split):
    gain_attn, w_query, w_key, w_value, w_out, gain_mlp, w_up, w_down = weights
    normed = spread_rows(layer_norm(inputs, gain_attn).astype(low_type), tensor_split)
    queries = matmul(normed, w_query).astype(low_type)
    keys_all = matmul(normed, w_key).astype(low_type)
    values_all = matmul(normed, w_value).astype(low_type)
    mixed_rows, log_total = attend_forward(queries, keys_all, values_all, key_valid, head_count)
    middle = inputs + collect_rows(matmul(mixed_rows, w_out), tensor_split)
    second = spread_rows(layer_norm(middle, gain_mlp).astype(low_type), tensor_split)
    pre_act = matmul(second, w_up)
    active = exact_gelu(pre_act).astype(low_type)
    outputs = middle + collect_rows(matmul(active, w_down), tensor_split)
    kept_state = (
        inputs,
        normed,
        queries,
        keys_all,
        values_all,
        mixed_rows,
        log_total,
        middle,
        second,
        pre_act,
        active,
    )
    return (outputs, kept_state)


def block_backward(grad_out, kept_state, key_valid, weights, head_count, tensor_split):
    gain_attn, w_query, w_key, w_value, w_out, gain_mlp, w_up, w_down = weights
    (
        inputs,
        normed,
        queries,
        keys_all,
        values_all,
        mixed_rows,
        log_total,
        middle,
        second,
        pre_act,
        active,
    ) = kept_state
    grad_branch = spread_rows(grad_out.astype(low_type), tensor_split)
    grad_down = outer_sum(active, grad_branch)
    grad_active = matmul_t(grad_branch, w_down)
    grad_pre = jax.vjp(exact_gelu, pre_act)[1](grad_active)[0].astype(low_type)
    grad_up = outer_sum(second, grad_pre)
    grad_second = collect_rows(matmul_t(grad_pre, w_up), tensor_split)
    norm_grad, grad_gain_mlp = jax.vjp(layer_norm, middle, gain_mlp)[1](grad_second)
    grad_middle = grad_out + norm_grad
    grad_attn = spread_rows(grad_middle.astype(low_type), tensor_split)
    grad_w_out = outer_sum(mixed_rows, grad_attn)
    grad_mixed = matmul_t(grad_attn, w_out).astype(low_type)
    grad_query, grad_key, grad_value = attend_backward(
        queries, keys_all, values_all, key_valid, log_total, grad_mixed, head_count
    )
    grad_w_query = outer_sum(normed, grad_query)
    grad_w_key = outer_sum(normed, grad_key)
    grad_w_value = outer_sum(normed, grad_value)
    grad_normed = (
        matmul_t(grad_query, w_query) + matmul_t(grad_key, w_key) + matmul_t(grad_value, w_value)
    )
    grad_normed = collect_rows(grad_normed, tensor_split)
    input_grad, grad_gain_attn = jax.vjp(layer_norm, inputs, gain_attn)[1](grad_normed)
    return (
        grad_middle + input_grad,
        (
            grad_gain_attn,
            grad_w_query,
            grad_w_key,
            grad_w_value,
            grad_w_out,
            grad_gain_mlp,
            grad_up,
            grad_down,
        ),
    )


def grid_codes(distance, side_count, columns):
    quarter = columns // 4
    frequency = 10000.0 ** (-jnp.arange(quarter, dtype=full_type) / quarter)
    places = jnp.arange(side_count * side_count)
    row_pos = (places // side_count).astype(full_type)
    col_pos = (places % side_count).astype(full_type)
    row_angle = distance[:, None, None] * row_pos[None, :, None] * frequency[None, None, :]
    col_angle = distance[:, None, None] * col_pos[None, :, None] * frequency[None, None, :]
    return jnp.concatenate(
        [jnp.sin(row_angle), jnp.cos(row_angle), jnp.sin(col_angle), jnp.cos(col_angle)], axis=-1
    )


def placement_table(visible_order, keep_flags, visible):
    positions = jnp.arange(visible_order.shape[1])
    matches = (visible_order[:, None, :visible] == positions[None, :, None]) & (
        keep_flags[:, :, None] == 1
    )
    return matches.astype(low_type)


def owner_blocks(full_grad, data_count, model_count):
    row_count, col_count = full_grad.shape
    reshaped = full_grad.reshape(
        data_count, row_count // data_count, model_count, col_count // model_count
    )
    return jnp.transpose(reshaped, (0, 2, 1, 3)).reshape(
        data_count * model_count, row_count // data_count, col_count // model_count
    )


def per_device(
    tokens,
    lengths,
    grid_order,
    grid_keep,
    ground_dist,
    enc_norm,
    enc_query,
    enc_key,
    enc_value,
    enc_proj,
    enc_norm2,
    enc_up,
    enc_down,
    embed_proj,
    mask_token,
    dec_norm,
    dec_query,
    dec_key,
    dec_value,
    dec_proj,
    dec_norm2,
    dec_up,
    dec_down,
    pred_proj,
    cotangent,
):
    data_count = lax.axis_size("dp")
    model_count = lax.axis_size("mp")
    enc_weights = (enc_norm, enc_query, enc_key, enc_value, enc_proj, enc_norm2, enc_up, enc_down)
    dec_weights = (dec_norm, dec_query, dec_key, dec_value, dec_proj, dec_norm2, dec_up, dec_down)
    enc_heads = HE // model_count
    key_valid = jnp.arange(tokens.shape[1])[None, :] < lengths[:, None]
    enc_out, enc_saved = block_forward(
        tokens.astype(full_type), key_valid, enc_weights, enc_heads, True
    )
    enc_low = enc_out.astype(low_type)
    enc_all = spread_rows(enc_low, True)
    embedded = matmul(enc_all, embed_proj).astype(low_type)
    sectioned = embedded.reshape((data_count, -1) + embedded.shape[1:])
    arrived = lax.all_to_all(
        lax.all_to_all(sectioned, "dp", split_axis=0, concat_axis=0, tiled=True),
        "mp",
        split_axis=0,
        concat_axis=3,
        tiled=True,
    )
    arrived = arrived.reshape((-1,) + arrived.shape[2:])
    pick_table = placement_table(grid_order, grid_keep, arrived.shape[1])
    masked = (1 - grid_keep).astype(full_type)[..., None]
    dec_start = jnp.einsum("npt,ntc->npc", pick_table, arrived, preferred_element_type=full_type)
    dec_start = dec_start + masked * mask_token + grid_codes(ground_dist, SIDE, mask_token.shape[0])
    all_valid = jnp.ones(dec_start.shape[:2], jnp.bool_)
    dec_out, dec_saved = block_forward(dec_start, all_valid, dec_weights, HD, False)
    dec_low = dec_out.astype(low_type)
    decoded = matmul(dec_low, pred_proj)
    grad_pred = outer_sum(dec_low, cotangent)
    grad_dec_out = matmul_t(cotangent, pred_proj)
    grad_start, dec_grads = block_backward(
        grad_dec_out, dec_saved, all_valid, dec_weights, HD, False
    )
    grad_mask = jnp.sum(masked * grad_start, axis=(0, 1))
    grad_arrived = jnp.einsum("npt,npc->ntc", pick_table.astype(full_type), grad_start).astype(
        low_type
    )
    sent_back = grad_arrived.reshape((-1, IPD) + grad_arrived.shape[1:])
    returned = lax.all_to_all(
        lax.all_to_all(sent_back, "mp", split_axis=3, concat_axis=0, tiled=True),
        "dp",
        split_axis=0,
        concat_axis=0,
        tiled=True,
    )
    returned = returned.reshape((-1,) + returned.shape[2:])
    grad_embed = outer_sum(enc_all, returned)
    grad_enc_out = collect_rows(matmul_t(returned, embed_proj), True)
    grad_tokens, enc_grads = block_backward(
        grad_enc_out, enc_saved, key_valid, enc_weights, enc_heads, True
    )
    col_sums = (
        lax.psum_scatter(
            enc_grads[4].astype(jnp.bfloat16), "dp", scatter_dimension=1, tiled=True
        ).astype(jnp.float32),
        lax.psum_scatter(
            enc_grads[7].astype(jnp.bfloat16), "dp", scatter_dimension=1, tiled=True
        ).astype(jnp.float32),
    )
    norm_grads = lax.psum(
        (enc_grads[0], enc_grads[5], dec_grads[0], dec_grads[5], grad_mask), ("dp", "mp")
    )
    dec_list = (
        dec_grads[1],
        dec_grads[2],
        dec_grads[3],
        dec_grads[4],
        dec_grads[6],
        dec_grads[7],
        grad_pred,
    )
    row_sums = (
        lax.psum_scatter(
            enc_grads[1].astype(jnp.bfloat16), "dp", scatter_dimension=0, tiled=True
        ).astype(jnp.float32),
        lax.psum_scatter(
            enc_grads[2].astype(jnp.bfloat16), "dp", scatter_dimension=0, tiled=True
        ).astype(jnp.float32),
        lax.psum_scatter(
            enc_grads[3].astype(jnp.bfloat16), "dp", scatter_dimension=0, tiled=True
        ).astype(jnp.float32),
        lax.psum_scatter(
            enc_grads[6].astype(jnp.bfloat16), "dp", scatter_dimension=0, tiled=True
        ).astype(jnp.float32),
        lax.psum_scatter(
            grad_embed.astype(jnp.bfloat16), "dp", scatter_dimension=0, tiled=True
        ).astype(jnp.float32),
    )
    summed = (
        lax.psum_scatter(
            owner_blocks(dec_list[0], data_count, model_count),
            ("dp", "mp"),
            scatter_dimension=0,
            tiled=True,
        ),
        lax.psum_scatter(
            owner_blocks(dec_list[1], data_count, model_count),
            ("dp", "mp"),
            scatter_dimension=0,
            tiled=True,
        ),
        lax.psum_scatter(
            owner_blocks(dec_list[2], data_count, model_count),
            ("dp", "mp"),
            scatter_dimension=0,
            tiled=True,
        ),
        lax.psum_scatter(
            owner_blocks(dec_list[3], data_count, model_count),
            ("dp", "mp"),
            scatter_dimension=0,
            tiled=True,
        ),
        lax.psum_scatter(
            owner_blocks(dec_list[4], data_count, model_count),
            ("dp", "mp"),
            scatter_dimension=0,
            tiled=True,
        ),
        lax.psum_scatter(
            owner_blocks(dec_list[5], data_count, model_count),
            ("dp", "mp"),
            scatter_dimension=0,
            tiled=True,
        ),
        lax.psum_scatter(
            owner_blocks(dec_list[6], data_count, model_count),
            ("dp", "mp"),
            scatter_dimension=0,
            tiled=True,
        ),
    )
    embed_final = row_sums[4]
    dec_final = tuple((summed[index_num][0] for index_num in range(7)))
    return (
        decoded,
        grad_tokens,
        norm_grads[0],
        row_sums[0],
        row_sums[1],
        row_sums[2],
        col_sums[0],
        norm_grads[1],
        row_sums[3],
        col_sums[1],
        embed_final,
        norm_grads[4],
        norm_grads[2],
        dec_final[0],
        dec_final[1],
        dec_final[2],
        dec_final[3],
        norm_grads[3],
        dec_final[4],
        dec_final[5],
        dec_final[6],
    )


def solution(mesh):
    return jax.shard_map(
        per_device,
        mesh=mesh,
        in_specs=(
            P(("dp", "mp"), None, None),
            P("dp"),
            P(("dp", "mp"), None),
            P(("dp", "mp"), None),
            P(("dp", "mp")),
            P(),
            P(None, "mp"),
            P(None, "mp"),
            P(None, "mp"),
            P("mp", None),
            P(),
            P(None, "mp"),
            P("mp", None),
            P(None, "mp"),
            P(),
            P(),
            P(),
            P(),
            P(),
            P(),
            P(),
            P(),
            P(),
            P(),
            P(("dp", "mp"), None, None),
        ),
        out_specs=(
            P(("dp", "mp"), None, None),
            P(("dp", "mp"), None, None),
            P(),
            P("dp", "mp"),
            P("dp", "mp"),
            P("dp", "mp"),
            P("mp", "dp"),
            P(),
            P("dp", "mp"),
            P("mp", "dp"),
            P("dp", "mp"),
            P(),
            P(),
            P("dp", "mp"),
            P("dp", "mp"),
            P("dp", "mp"),
            P("dp", "mp"),
            P(),
            P("dp", "mp"),
            P("dp", "mp"),
            P("dp", "mp"),
        ),
        check_vma=False,
    )
```

profile of v0, /device:TPU:0, one launch (start us, length us, event | category | flops | bytes accessed | tf_op | source)
XLA Modules:
  0.0 1826.2 jit_solution(3336529380080165947)
XLA Ops:
  12.4 18.8 %all-gather.6.cloned.1.call-done = bf16[8,64,1024]{2,1,0:T(8,128)(2,1)} async-done(((bf16[2,64,1024]{2,1,0:T(8,128)(2,1)}), bf16[8,64,1024]{2,1,0:T(8,128)(2,1)}) %all-gather.6.cloned.1.call-update) | async-done | bytes 1048592 | tf_op jit(solution)/shard_map/all_gather | solution.py:53
  44.2 25.0 %reduce-scatter.24.cloned.1.call-done = bf16[2,64,1024]{2,1,0:T(8,128)(2,1)} async-done(((bf16[8,64,1024]{2,1,0:T(8,128)(2,1)}), bf16[2,64,1024]{2,1,0:T(8,128)(2,1)}) %reduce-scatter.24.cloned.1.call-update) | async-done | bytes 262160 | tf_op jit(solution)/shard_map/reduce_scatter | solution.py:59
  73.3 16.8 all-gather.8.cloned.1.call-done
  102.9 25.0 %reduce-scatter.26.cloned.1.call-done = bf16[2,64,1024]{2,1,0:T(8,128)(2,1)} async-done(((bf16[8,64,1024]{2,1,0:T(8,128)(2,1)}), bf16[2,64,1024]{2,1,0:T(8,128)(2,1)}) %reduce-scatter.26.cloned.1.call-update) | async-done | bytes 262160 | tf_op jit(solution)/shard_map/reduce_scatter | solution.py:59
  132.7 13.9 all-gather.10.cloned.1.call-done
  227.6 15.2 fusion.77
  282.2 21.8 %reduce-scatter.28.cloned.1.call-done = bf16[2,64,1024]{2,1,0:T(8,128)(2,1)} async-done(((bf16[8,64,1024]{2,1,0:T(8,128)(2,1)}), bf16[2,64,1024]{2,1,0:T(8,128)(2,1)}) %reduce-scatter.28.cloned.1.call-update) | async-done | bytes 262160 | tf_op jit(solution)/shard_map/reduce_scatter | solution.py:59
  304.1 18.3 %all-gather.12.cloned.1.call-done = bf16[8,64,1024]{2,1,0:T(8,128)(2,1)} async-done(((bf16[2,64,1024]{2,1,0:T(8,128)(2,1)}), bf16[8,64,1024]{2,1,0:T(8,128)(2,1)}) %all-gather.12.cloned.1.call-update) | async-done | bytes 1048592 | tf_op jit(solution)/shard_map/all_gather | solution.py:53
  330.3 25.0 %reduce-scatter.30.cloned.1.call-done = bf16[2,64,1024]{2,1,0:T(8,128)(2,1)} async-done(((bf16[8,64,1024]{2,1,0:T(8,128)(2,1)}), bf16[2,64,1024]{2,1,0:T(8,128)(2,1)}) %reduce-scatter.30.cloned.1.call-update) | async-done | bytes 262160 | tf_op jit(solution)/shard_map/reduce_scatter | solution.py:59
  446.8 64.6 %reduce-scatter.60.cloned.1.call-done = bf16[128,1024]{1,0:T(8,128)(2,1)} async-done(((bf16[1024,1024]{1,0:T(8,128)(2,1)}), bf16[128,1024]{1,0:T(8,128)(2,1)}) %reduce-scatter.60.cloned.1.call-update) | async-done | bytes 262160
  513.3 68.1 %reduce-scatter.40.cloned.1.call-done = bf16[128,1024]{1,0:T(8,128)(2,1)} async-done(((bf16[1024,1024]{1,0:T(8,128)(2,1)}), bf16[128,1024]{1,0:T(8,128)(2,1)}) %reduce-scatter.40.cloned.1.call-update) | async-done | bytes 262160 | tf_op jit(solution)/shard_map/reduce_scatter | solution.py:389
  583.2 62.5 %reduce-scatter.58.cloned.1.call-done = bf16[128,256]{1,0:T(8,128)(2,1)} async-done(((bf16[1024,256]{1,0:T(8,128)(2,1)}), bf16[128,256]{1,0:T(8,128)(2,1)}) %reduce-scatter.58.cloned.1.call-update) | async-done | bytes 65552
  647.3 62.9 %reduce-scatter.38.cloned.1.call-done = bf16[128,256]{1,0:T(8,128)(2,1)} async-done(((bf16[1024,256]{1,0:T(8,128)(2,1)}), bf16[128,256]{1,0:T(8,128)(2,1)}) %reduce-scatter.38.cloned.1.call-update) | async-done | bytes 65552 | tf_op jit(solution)/shard_map/reduce_scatter | solution.py:386
  711.7 62.7 %reduce-scatter.34.cloned.1.call-done = bf16[128,256]{1,0:T(8,128)(2,1)} async-done(((bf16[1024,256]{1,0:T(8,128)(2,1)}), bf16[128,256]{1,0:T(8,128)(2,1)}) %reduce-scatter.34.cloned.1.call-update) | async-done | bytes 65552 | tf_op jit(solution)/shard_map/reduce_scatter | solution.py:380
  775.8 63.0 %reduce-scatter.36.cloned.1.call-done = bf16[128,256]{1,0:T(8,128)(2,1)} async-done(((bf16[1024,256]{1,0:T(8,128)(2,1)}), bf16[128,256]{1,0:T(8,128)(2,1)}) %reduce-scatter.36.cloned.1.call-update) | async-done | bytes 65552 | tf_op jit(solution)/shard_map/reduce_scatter | solution.py:383
  840.3 24.8 %reduce-scatter.32.cloned.1.call-done = bf16[2,64,1024]{2,1,0:T(8,128)(2,1)} async-done(((bf16[8,64,1024]{2,1,0:T(8,128)(2,1)}), bf16[2,64,1024]{2,1,0:T(8,128)(2,1)}) %reduce-scatter.32.cloned.1.call-update) | async-done | bytes 262160 | tf_op jit(solution)/shard_map/reduce_scatter | solution.py:59
  867.6 39.7 %all-reduce = (f32[1024]{0:T(1024)}, f32[1024]{0:T(1024)}, f32[512]{0:T(512)}, f32[512]{0:T(512)}, f32[512]{0:T(512)}) all-reduce(f32[1024]{0:T(1024)S(1)} %get-tuple-element.117, f32[1024]{0:T(1024)S(1)} %get-tuple-element.115, f32[512]{0:T(512)S(1)} %get-tuple-element.134, ...), channel_id=1, replica_groups=mesh['dp'=8,'mp'=4] {'dp','mp'}, use_global_device_ids=true, to_apply=%region_28.29 | all-reduce | flops 3584 | bytes 28672 | tf_op jit(solution)/shard_map/psum | solution.py:367
  909.5 93.3 %reduce-scatter.50.cloned.1.call-done = f32[1,64,128]{2,1,0:T(8,128)} async-done(((f32[32,64,128]{2,1,0:T(8,128)}), f32[1,64,128]{2,1,0:T(8,128)}) %reduce-scatter.50.cloned.1.call-update) | async-done | bytes 32784 | tf_op jit(solution)/shard_map/reduce_scatter | solution.py:415
  1002.9 133.6 %reduce-scatter.48.cloned.1.call-done = f32[1,64,128]{2,1,0:T(8,128)} async-done(((f32[32,64,128]{2,1,0:T(8,128)}), f32[1,64,128]{2,1,0:T(8,128)}) %reduce-scatter.48.cloned.1.call-update) | async-done | bytes 32784 | tf_op jit(solution)/shard_map/reduce_scatter | solution.py:409
  1136.4 133.5 %reduce-scatter.44.cloned.1.call-done = f32[1,64,128]{2,1,0:T(8,128)} async-done(((f32[32,64,128]{2,1,0:T(8,128)}), f32[1,64,128]{2,1,0:T(8,128)}) %reduce-scatter.44.cloned.1.call-update) | async-done | bytes 32784 | tf_op jit(solution)/shard_map/reduce_scatter | solution.py:397
  1269.9 133.6 %reduce-scatter.46.cloned.1.call-done = f32[1,64,128]{2,1,0:T(8,128)} async-done(((f32[32,64,128]{2,1,0:T(8,128)}), f32[1,64,128]{2,1,0:T(8,128)}) %reduce-scatter.46.cloned.1.call-update) | async-done | bytes 32784 | tf_op jit(solution)/shard_map/reduce_scatter | solution.py:403
  1403.5 135.5 %reduce-scatter.56.cloned.1.call-done = f32[1,64,192]{2,1,0:T(8,128)} async-done(((f32[32,64,192]{2,1,0:T(8,128)}), f32[1,64,192]{2,1,0:T(8,128)}) %reduce-scatter.56.cloned.1.call-update) | async-done | bytes 49168 | tf_op jit(solution)/shard_map/reduce_scatter | solution.py:433
  1539.0 140.2 %reduce-scatter.54.cloned.1.call-done = f32[1,256,128]{2,1,0:T(8,128)} async-done(((f32[32,256,128]{2,1,0:T(8,128)}), f32[1,256,128]{2,1,0:T(8,128)}) %reduce-scatter.54.cloned.1.call-update) | async-done | bytes 131088 | tf_op jit(solution)/shard_map/reduce_scatter | solution.py:427
  1679.1 139.7 %reduce-scatter.52.cloned.1.call-done = f32[1,64,512]{2,1,0:T(8,128)} async-done(((f32[32,64,512]{2,1,0:T(8,128)}), f32[1,64,512]{2,1,0:T(8,128)}) %reduce-scatter.52.cloned.1.call-update) | async-done | bytes 131088 | tf_op jit(solution)/shard_map/reduce_scatter | solution.py:421
  (369 shorter events, 272.7 us)
Async XLA Ops:
  7.2 23.9 %all-gather.6.cloned.1.call-start = ((), (), s32[]{:S(2)}) async-start(), calls=%async_computation.23 | async-start | bytes 1310720 | tf_op jit(solution)/shard_map/all_gather | solution.py:53
  11.6 57.6 %reduce-scatter.24.cloned.1.call-start = ((), (), s32[]{:S(2)}) async-start(), calls=%async_computation.24 | async-start | bytes 1310720 | tf_op jit(solution)/shard_map/reduce_scatter | solution.py:59
  44.1 46.1 %all-gather.8.cloned.1.call-start = ((), (), s32[]{:S(2)}) async-start(), calls=%async_computation.25 | async-start | bytes 1310720 | tf_op jit(solution)/shard_map/all_gather | solution.py:53
  73.3 54.6 %reduce-scatter.26.cloned.1.call-start = ((), (), s32[]{:S(2)}) async-start(), calls=%async_computation.26 | async-start | bytes 1310720 | tf_op jit(solution)/shard_map/reduce_scatter | solution.py:59
  102.9 43.8 %all-gather.10.cloned.1.call-start = ((), (), s32[]{:S(2)}) async-start(), calls=%async_computation.27 | async-start | bytes 1310720 | tf_op jit(solution)/shard_map/all_gather | solution.py:53
  165.4 138.6 %reduce-scatter.28.cloned.1.call-start = ((), (), s32[]{:S(2)}) async-start(), calls=%async_computation.28 | async-start | bytes 1310720 | tf_op jit(solution)/shard_map/reduce_scatter | solution.py:59
  282.1 40.3 %all-gather.12.cloned.1.call-start = ((), (), s32[]{:S(2)}) async-start(), calls=%async_computation.29 | async-start | bytes 1310720 | tf_op jit(solution)/shard_map/all_gather | solution.py:53
  304.0 51.3 %reduce-scatter.30.cloned.1.call-start = ((), (), s32[]{:S(2)}) async-start(), calls=%async_computation.30 | async-start | bytes 1310720 | tf_op jit(solution)/shard_map/reduce_scatter | solution.py:59
  330.2 46.4 %all-gather.14.cloned.1.call-start = ((), (), s32[]{:S(2)}) async-start(), calls=%async_computation.31 | async-start | bytes 1310720 | tf_op jit(solution)/shard_map/all_gather | solution.py:53
  359.8 85.6 %reduce-scatter.42.cloned.1.call-start = ((), (), s32[]{:S(2)}) async-start(), calls=%async_computation.37 | async-start | bytes 294912 | tf_op jit(solution)/shard_map/reduce_scatter | solution.py:392
  361.1 150.3 %reduce-scatter.60.cloned.1.call-start = ((), (), s32[]{:S(2)}) async-start(), calls=%async_computation.46 | async-start | bytes 2359296
  366.6 214.8 %reduce-scatter.40.cloned.1.call-start = ((), (), s32[]{:S(2)}) async-start(), calls=%async_computation.36 | async-start | bytes 2359296 | tf_op jit(solution)/shard_map/reduce_scatter | solution.py:389
  371.1 274.6 %reduce-scatter.58.cloned.1.call-start = ((), (), s32[]{:S(2)}) async-start(), calls=%async_computation.45 | async-start | bytes 589824
  379.4 330.8 %reduce-scatter.38.cloned.1.call-start = ((), (), s32[]{:S(2)}) async-start(), calls=%async_computation.35 | async-start | bytes 589824 | tf_op jit(solution)/shard_map/reduce_scatter | solution.py:386
  387.7 386.6 %reduce-scatter.34.cloned.1.call-start = ((), (), s32[]{:S(2)}) async-start(), calls=%async_computation.33 | async-start | bytes 589824 | tf_op jit(solution)/shard_map/reduce_scatter | solution.py:380
  396.3 442.5 %reduce-scatter.36.cloned.1.call-start = ((), (), s32[]{:S(2)}) async-start(), calls=%async_computation.34 | async-start | bytes 589824 | tf_op jit(solution)/shard_map/reduce_scatter | solution.py:383
  402.5 462.6 %reduce-scatter.32.cloned.1.call-start = ((), (), s32[]{:S(2)}) async-start(), calls=%async_computation.32 | async-start | bytes 1310720 | tf_op jit(solution)/shard_map/reduce_scatter | solution.py:59
  409.4 593.5 %reduce-scatter.50.cloned.1.call-start = ((), (), s32[]{:S(2)}) async-start(), calls=%async_computation.41 | async-start | bytes 1081344 | tf_op jit(solution)/shard_map/reduce_scatter | solution.py:415
  412.9 723.5 %reduce-scatter.48.cloned.1.call-start = ((), (), s32[]{:S(2)}) async-start(), calls=%async_computation.40 | async-start | bytes 1081344 | tf_op jit(solution)/shard_map/reduce_scatter | solution.py:409
  416.4 853.5 %reduce-scatter.44.cloned.1.call-start = ((), (), s32[]{:S(2)}) async-start(), calls=%async_computation.38 | async-start | bytes 1081344 | tf_op jit(solution)/shard_map/reduce_scatter | solution.py:397
  418.9 984.6 %reduce-scatter.46.cloned.1.call-start = ((), (), s32[]{:S(2)}) async-start(), calls=%async_computation.39 | async-start | bytes 1081344 | tf_op jit(solution)/shard_map/reduce_scatter | solution.py:403
  422.2 1116.8 %reduce-scatter.56.cloned.1.call-start = ((), (), s32[]{:S(2)}) async-start(), calls=%async_computation.44 | async-start | bytes 2162688 | tf_op jit(solution)/shard_map/reduce_scatter | solution.py:433
  428.3 1250.8 %reduce-scatter.54.cloned.1.call-start = ((), (), s32[]{:S(2)}) async-start(), calls=%async_computation.43 | async-start | bytes 4325376 | tf_op jit(solution)/shard_map/reduce_scatter | solution.py:427
  434.8 1384.1 %reduce-scatter.52.cloned.1.call-start = ((), (), s32[]{:S(2)}) async-start(), calls=%async_computation.42 | async-start | bytes 4325376 | tf_op jit(solution)/shard_map/reduce_scatter | solution.py:421
  (81 other events, 5081.8 us)
Sparse Core Ops, SparseCore 0:
  11.7 19.4 all-gather.5
  44.2 24.8 reduce-scatter.23
  73.4 16.7 all-gather.7
  103.0 24.8 reduce-scatter.25
  129.9 16.7 all-gather.9
  282.2 21.7 reduce-scatter.27
  305.6 16.7 all-gather.11
  330.4 24.8 reduce-scatter.29
  359.9 16.7 all-gather.13
  379.8 61.2 reduce-scatter.41
  444.7 66.6 reduce-scatter.59
  514.7 66.6 reduce-scatter.39
  584.8 60.8 reduce-scatter.57
  649.3 60.8 reduce-scatter.37
  713.4 60.9 reduce-scatter.33
  777.9 60.8 reduce-scatter.35
  841.2 23.8 reduce-scatter.31
  867.9 134.9 reduce-scatter.49
  1005.7 130.7 reduce-scatter.47
  1139.2 130.6 reduce-scatter.43
  1272.7 130.7 reduce-scatter.45
  1406.4 132.5 reduce-scatter.55
  1541.8 137.2 reduce-scatter.53
  1681.8 136.9 reduce-scatter.51
where the time goes:
time: 1840 us; the launch traced here: 1830 us
  waiting for transfers between devices  1490 us (81%)
  matrix products  148 us (8%)
  blocking collectives  56.6 us (3%)
  other arithmetic  55.8 us (3%)
  local copies, waits for them, and re-layouts  44.7 us (2%)
    reduce_scatter x1, waiting for transfers between devices, per_device(): lax.psum_scatter(owner_blocks(dec_list[5], data_count, model_count), ('dp...  140 us
    reduce_scatter x1, waiting for transfers between devices, per_device(): lax.psum_scatter(owner_blocks(dec_list[4], data_count, model_count), ('dp...  140 us
    reduce_scatter x1, waiting for transfers between devices, per_device(): lax.psum_scatter(owner_blocks(dec_list[6], data_count, model_count), ('dp...  136 us
    reduce_scatter x1, waiting for transfers between devices, per_device(): lax.psum_scatter(owner_blocks(dec_list[1], data_count, model_count), ('dp...  134 us
    reduce_scatter x1, waiting for transfers between devices, per_device(): lax.psum_scatter(owner_blocks(dec_list[2], data_count, model_count), ('dp...  134 us
    reduce_scatter x1, waiting for transfers between devices, per_device(): lax.psum_scatter(owner_blocks(dec_list[0], data_count, model_count), ('dp...  133 us
    unnamed x26, waiting for transfers between devices  127 us
    reduce_scatter x5, waiting for transfers between devices, collect_rows(): lax.psum_scatter(values.astype(jnp.bfloat16), 'mp', scatter_dimension=0,...  122 us
  transfers between devices with their start and end apart: 26, of which 25 were waited for; matrix products, arithmetic and copies ran while one was open for 6% of the time, Pallas kernels for 0%

commit v1 on v0

--- a/solution.py
+++ b/solution.py
@@ -1,6 +1,8 @@
 import jax
 import jax.numpy as jnp
 from jax import lax
+from jax.experimental import pallas as pl
+from jax.experimental.pallas import tpu as pltpu
 from jax.sharding import PartitionSpec as P
 
 HE = 16
@@ -210,7 +212,7 @@
         active,
     ) = kept_state
     grad_branch = spread_rows(grad_out.astype(low_type), tensor_split)
-    grad_down = outer_sum(active, grad_branch)
+    grad_down = outer_sum(grad_branch, active) if tensor_split else outer_sum(active, grad_branch)
     grad_active = matmul_t(grad_branch, w_down)
     grad_pre = jax.vjp(exact_gelu, pre_act)[1](grad_active)[0].astype(low_type)
     grad_up = outer_sum(second, grad_pre)
@@ -218,7 +220,7 @@
     norm_grad, grad_gain_mlp = jax.vjp(layer_norm, middle, gain_mlp)[1](grad_second)
     grad_middle = grad_out + norm_grad
     grad_attn = spread_rows(grad_middle.astype(low_type), tensor_split)
-    grad_w_out = outer_sum(mixed_rows, grad_attn)
+    grad_w_out = outer_sum(grad_attn, mixed_rows) if tensor_split else outer_sum(mixed_rows, grad_attn)
     grad_mixed = matmul_t(grad_attn, w_out).astype(low_type)
     grad_query, grad_key, grad_value = attend_backward(
         queries, keys_all, values_all, key_valid, log_total, grad_mixed, head_count
@@ -267,14 +269,240 @@
     return matches.astype(low_type)
 
 
-def owner_blocks(full_grad, data_count, model_count):
-    row_count, col_count = full_grad.shape
-    reshaped = full_grad.reshape(
-        data_count, row_count // data_count, model_count, col_count // model_count
-    )
-    return jnp.transpose(reshaped, (0, 2, 1, 3)).reshape(
-        data_count * model_count, row_count // data_count, col_count // model_count
-    )
+MESH = pl.DeviceIdType.MESH
+LANES = 128
+
+
+def log2_of(count):
+    bits = count.bit_length() - 1
+    assert 1 << bits == count
+    return bits
+
+
+def bit_reverse(index, bits):
+    out = 0
+    for position in range(bits):
+        out = out * 2 + ((index >> position) & 1)
+    return out
+
+
+def partner(axis, bit):
+    dp, mp = lax.axis_index("dp"), lax.axis_index("mp")
+    step = 1 << bit
+    if axis == "dp":
+        return (dp ^ step, mp), (dp >> bit) & 1
+    return (dp, mp ^ step), (mp >> bit) & 1
+
+
+def enter_barrier(partners):
+    barrier = pltpu.get_barrier_semaphore()
+    for peer in partners:
+        pl.semaphore_signal(barrier, inc=1, device_id=peer, device_id_type=MESH)
+    pl.semaphore_wait(barrier, len(partners))
+
+
+class HalvingSum:
+    def __init__(self, stages, buffers, window, send_sems, recv_sems):
+        self.stages, self.buffers, self.window = stages, buffers, window
+        self.send_sems, self.recv_sems = send_sems, recv_sems
+        self.copies = [None] * len(stages)
+
+    def view(self, index, start, size):
+        return self.buffers[index].at[(pl.ds(start, size),) + self.window]
+
+    def start(self, index):
+        peer, mine = partner(*self.stages[index])
+        half = self.buffers[index].shape[0] // 2
+        copy = pltpu.make_async_remote_copy(
+            src_ref=self.view(index, (1 - mine) * half, half),
+            dst_ref=self.view(index + 1, 0, half),
+            send_sem=self.send_sems.at[index],
+            recv_sem=self.recv_sems.at[index],
+            device_id=peer,
+            device_id_type=MESH,
+        )
+        copy.start()
+        self.copies[index] = copy
+
+    def finish(self, index):
+        self.copies[index].wait()
+        peer, mine = partner(*self.stages[index])
+        half = self.buffers[index].shape[0] // 2
+
+        def one(position, carry):
+            there = self.buffers[index + 1].at[(position,) + self.window]
+            here = self.buffers[index].at[(mine * half + position,) + self.window]
+            there[...] = there[...] + here[...]
+            return carry
+
+        lax.fori_loop(0, half, one, 0)
+
+
+def dec_pieces(data_count, model_count, shapes):
+    offset, pieces = 0, []
+    for rows, columns in shapes:
+        height, width = rows // data_count, columns // model_count
+        tiles = -(-width // LANES)
+        pieces.append((offset, height, width, tiles))
+        offset += height * tiles
+    return pieces, offset
+
+
+def pack_dec(matrices, data_count, model_count):
+    pieces, total = dec_pieces(data_count, model_count, [m.shape for m in matrices])
+    blocks = []
+    for matrix, (offset, height, width, tiles) in zip(matrices, pieces):
+        block = matrix.astype(low_type).reshape(data_count, height, model_count, width)
+        block = jnp.pad(block, ((0, 0), (0, 0), (0, 0), (0, tiles * LANES - width)))
+        block = block.reshape(data_count, height, model_count, tiles, LANES)
+        block = jnp.transpose(block, (2, 0, 3, 1, 4))
+        blocks.append(block.reshape(model_count, data_count, tiles * height, LANES))
+    packed = jnp.concatenate(blocks, axis=2)
+    packed = reversed_order(reversed_order(packed, 0), 1)
+    return packed.reshape((model_count * data_count,) + packed.shape[2:])
+
+
+def reversed_order(values, axis):
+    count = values.shape[axis]
+    bits = log2_of(count)
+    shape = values.shape
+    split = values.reshape(shape[:axis] + (2,) * bits + shape[axis + 1 :])
+    order = list(range(split.ndim))
+    order[axis : axis + bits] = order[axis : axis + bits][::-1]
+    return jnp.transpose(split, order).reshape(shape)
+
+
+def reduce_kernel(data_count, model_count, enc_cuts, dec_cuts, pieces, enc_widths, *refs):
+    data_bits, model_bits = log2_of(data_count), log2_of(model_count)
+    enc_stages = [("dp", bit) for bit in range(data_bits)]
+    dec_stages = [("mp", bit) for bit in range(model_bits)] + enc_stages
+    refs = list(refs)
+    enc_in, dec_in, norm_in = refs[:3]
+    enc_outs = refs[3 : 3 + len(enc_widths)]
+    dec_outs = refs[3 + len(enc_widths) : 3 + len(enc_widths) + len(pieces)]
+    rest = refs[3 + len(enc_widths) + len(pieces) :]
+    norm_out, rest = rest[0], rest[1:]
+    enc_bufs, rest = [enc_in] + rest[: len(enc_stages)], rest[len(enc_stages) :]
+    dec_bufs, rest = [dec_in] + rest[: len(dec_stages)], rest[len(dec_stages) :]
+    norm_acc, norm_got, enc_send, enc_recv, dec_send, dec_recv, norm_send, norm_recv = rest
+    enter_barrier([partner(*stage)[0] for stage in dec_stages])
+
+    columns = enc_in.shape[2] // enc_cuts
+    enc = [
+        HalvingSum(
+            enc_stages,
+            enc_bufs,
+            (slice(None), pl.ds(cut * columns, columns)),
+            enc_send.at[cut],
+            enc_recv.at[cut],
+        )
+        for cut in range(enc_cuts)
+    ]
+    height = dec_in.shape[1] // dec_cuts
+    dec = [
+        HalvingSum(
+            dec_stages,
+            dec_bufs,
+            (pl.ds(cut * height, height), slice(None)),
+            dec_send.at[cut],
+            dec_recv.at[cut],
+        )
+        for cut in range(dec_cuts)
+    ]
+    for one in dec + enc:
+        one.start(0)
+    norm_acc[0] = norm_in[...]
+    for index, stage in enumerate(dec_stages):
+        peer, mine = partner(*stage)
+        copy = pltpu.make_async_remote_copy(
+            src_ref=norm_acc.at[index],
+            dst_ref=norm_got.at[index],
+            send_sem=norm_send.at[index],
+            recv_sem=norm_recv.at[index],
+            device_id=peer,
+            device_id_type=MESH,
+        )
+        copy.start()
+        for one in dec + (enc if index < len(enc_stages) else []):
+            one.finish(index)
+            if index + 1 < len(one.stages):
+                one.start(index + 1)
+        copy.wait()
+        norm_acc[index + 1] = norm_acc[index] + norm_got[index]
+    norm_out[...] = norm_acc[len(dec_stages)]
+    offset = 0
+    for out, (width, flipped) in zip(enc_outs, enc_widths):
+        block = enc_bufs[-1][0, :, offset : offset + width].astype(full_type)
+        out[...] = block.T if flipped else block
+        offset += width
+    for out, (offset, rows, width, tiles) in zip(dec_outs, pieces):
+        for tile in range(tiles):
+            lanes = min(LANES, width - tile * LANES)
+            block = dec_bufs[-1][0, offset + tile * rows : offset + (tile + 1) * rows, :lanes]
+            out[:, tile * LANES : tile * LANES + lanes] = block.astype(full_type)
+
+
+def reduce_all(enc_grads, dec_grads, norm_grads):
+    data_count, model_count = lax.axis_size("dp"), lax.axis_size("mp")
+    data_bits, model_bits = log2_of(data_count), log2_of(model_count)
+    enc_widths = [(grad.shape[1], flipped) for grad, flipped in enc_grads]
+    enc_packed = jnp.concatenate([grad.astype(low_type) for grad, flipped in enc_grads], axis=1)
+    rows = enc_packed.shape[0] // data_count
+    enc_cuts = 5
+    dec_cuts = 2
+    slack = -enc_packed.shape[1] % (enc_cuts * LANES)
+    if slack:
+        enc_packed = jnp.pad(enc_packed, ((0, 0), (0, slack)))
+    enc_packed = reversed_order(enc_packed.reshape(data_count, rows, -1), 0)
+    pieces, height = dec_pieces(data_count, model_count, [grad.shape for grad in dec_grads])
+    dec_packed = pack_dec(dec_grads, data_count, model_count)
+    flat = jnp.concatenate([grad.reshape(-1) for grad in norm_grads]).reshape(-1, LANES)
+    stages = data_bits + model_bits
+    scratch = []
+    for bit in range(data_bits):
+        scratch.append(pltpu.VMEM((data_count >> (bit + 1),) + enc_packed.shape[1:], low_type))
+    for bit in range(stages):
+        scratch.append(
+            pltpu.VMEM(((data_count * model_count) >> (bit + 1), height, LANES), low_type)
+        )
+    scratch += [
+        pltpu.VMEM((stages + 1,) + flat.shape, full_type),
+        pltpu.VMEM((stages,) + flat.shape, full_type),
+        pltpu.SemaphoreType.DMA((enc_cuts, data_bits)),
+        pltpu.SemaphoreType.DMA((enc_cuts, data_bits)),
+        pltpu.SemaphoreType.DMA((dec_cuts, stages)),
+        pltpu.SemaphoreType.DMA((dec_cuts, stages)),
+        pltpu.SemaphoreType.DMA((stages,)),
+        pltpu.SemaphoreType.DMA((stages,)),
+    ]
+    out_shape = [
+        jax.ShapeDtypeStruct((width, rows) if flipped else (rows, width), full_type)
+        for width, flipped in enc_widths
+    ]
+    out_shape += [
+        jax.ShapeDtypeStruct((high, width), full_type) for offset, high, width, tiles in pieces
+    ]
+    out_shape.append(jax.ShapeDtypeStruct(flat.shape, full_type))
+
+    def kernel(*refs):
+        reduce_kernel(data_count, model_count, enc_cuts, dec_cuts, pieces, enc_widths, *refs)
+
+    outs = pl.pallas_call(
+        kernel,
+        out_shape=out_shape,
+        in_specs=[pl.BlockSpec(memory_space=pltpu.VMEM)] * 3,
+        out_specs=[pl.BlockSpec(memory_space=pltpu.VMEM)] * len(out_shape),
+        scratch_shapes=scratch,
+        compiler_params=pltpu.CompilerParams(
+            collective_id=0, has_side_effects=True, vmem_limit_bytes=56 * 2**20
+        ),
+    )(enc_packed, dec_packed, flat)
+    sums, position = [], 0
+    flat_sum = outs[-1].reshape(-1)
+    for grad in norm_grads:
+        sums.append(flat_sum[position : position + grad.shape[0]])
+        position += grad.shape[0]
+    return outs[: len(enc_grads)], outs[len(enc_grads) : -1], sums
 
 
 def per_device(
@@ -356,89 +584,30 @@
     grad_tokens, enc_grads = block_backward(
         grad_enc_out, enc_saved, key_valid, enc_weights, enc_heads, True
     )
-    col_sums = (
-        lax.psum_scatter(
-            enc_grads[4].astype(jnp.bfloat16), "dp", scatter_dimension=1, tiled=True
-        ).astype(jnp.float32),
-        lax.psum_scatter(
-            enc_grads[7].astype(jnp.bfloat16), "dp", scatter_dimension=1, tiled=True
-        ).astype(jnp.float32),
-    )
-    norm_grads = lax.psum(
-        (enc_grads[0], enc_grads[5], dec_grads[0], dec_grads[5], grad_mask), ("dp", "mp")
-    )
-    dec_list = (
-        dec_grads[1],
-        dec_grads[2],
-        dec_grads[3],
-        dec_grads[4],
-        dec_grads[6],
-        dec_grads[7],
-        grad_pred,
-    )
-    row_sums = (
-        lax.psum_scatter(
-            enc_grads[1].astype(jnp.bfloat16), "dp", scatter_dimension=0, tiled=True
-        ).astype(jnp.float32),
-        lax.psum_scatter(
-            enc_grads[2].astype(jnp.bfloat16), "dp", scatter_dimension=0, tiled=True
-        ).astype(jnp.float32),
-        lax.psum_scatter(
-            enc_grads[3].astype(jnp.bfloat16), "dp", scatter_dimension=0, tiled=True
-        ).astype(jnp.float32),
-        lax.psum_scatter(
-            enc_grads[6].astype(jnp.bfloat16), "dp", scatter_dimension=0, tiled=True
-        ).astype(jnp.float32),
-        lax.psum_scatter(
-            grad_embed.astype(jnp.bfloat16), "dp", scatter_dimension=0, tiled=True
-        ).astype(jnp.float32),
-    )
-    summed = (
-        lax.psum_scatter(
-            owner_blocks(dec_list[0], data_count, model_count),
-            ("dp", "mp"),
-            scatter_dimension=0,
-            tiled=True,
-        ),
-        lax.psum_scatter(
-            owner_blocks(dec_list[1], data_count, model_count),
-            ("dp", "mp"),
-            scatter_dimension=0,
-            tiled=True,
-        ),
-        lax.psum_scatter(
-            owner_blocks(dec_list[2], data_count, model_count),
-            ("dp", "mp"),
-            scatter_dimension=0,
-            tiled=True,
-        ),
-        lax.psum_scatter(
-            owner_blocks(dec_list[3], data_count, model_count),
-            ("dp", "mp"),
-            scatter_dimension=0,
-            tiled=True,
-        ),
-        lax.psum_scatter(
-            owner_blocks(dec_list[4], data_count, model_count),
-            ("dp", "mp"),
-            scatter_dimension=0,
-            tiled=True,
-        ),
-        lax.psum_scatter(
-            owner_blocks(dec_list[5], data_count, model_count),
-            ("dp", "mp"),
-            scatter_dimension=0,
-            tiled=True,
-        ),
-        lax.psum_scatter(
-            owner_blocks(dec_list[6], data_count, model_count),
-            ("dp", "mp"),
-            scatter_dimension=0,
-            tiled=True,
-        ),
-    )
+    enc_out_grads, dec_final, norm_grads = reduce_all(
+        [
+            (enc_grads[1], False),
+            (enc_grads[2], False),
+            (enc_grads[3], False),
+            (enc_grads[6], False),
+            (grad_embed, False),
+            (enc_grads[4], True),
+            (enc_grads[7], True),
+        ],
+        [
+            dec_grads[1],
+            dec_grads[2],
+            dec_grads[3],
+            dec_grads[4],
+            dec_grads[6],
+            dec_grads[7],
+            grad_pred,
+        ],
+        [enc_grads[0], enc_grads[5], dec_grads[0], dec_grads[5], grad_mask],
+    )
+    row_sums = enc_out_grads[:5]
+    col_sums = enc_out_grads[5:]
     embed_final = row_sums[4]
-    dec_final = tuple((summed[index_num][0] for index_num in range(7)))
     return (
         decoded,
         grad_tokens,

time: 1840 us -> 647 us (0.35)
  waiting for transfers between devices: 1490 us -> 152 us
  Pallas kernels: 0 us -> 129 us
  local copies, waits for them, and re-layouts: 44.7 us -> 126 us
  blocking collectives: 56.6 us -> 16.9 us
    reduce_scatter x12 -> x0, waiting for transfers between devices: 1170 us -> none  [the longest x1 140 us: per_device(): lax.psum_scatter(owner_blocks(dec_list[5], data_count, model_count), ('dp...]
    pallas_call x0 -> x1, Pallas kernels: none -> 129 us  [reduce_all(): pl.pallas_call(kernel, out_shape=out_shape, in_specs=[pl.BlockSpec(memory...]
    unnamed x26 -> x10, waiting for transfers between devices: 127 us -> 0.16 us
    reduce_scatter x5, waiting for transfers between devices: 122 us -> 78.3 us  [collect_rows(): lax.psum_scatter(values.astype(jnp.bfloat16), 'mp', scatter_dimension=0,...]
    psum x1 -> x0, blocking collectives: 39.7 us -> none  [per_device(): lax.psum((enc_grads[0], enc_grads[5], dec_grads[0], dec_grads[5], grad_ma...]
    another operation x0 -> x2, local copies, waits for them, and re-layouts: none -> 32.6 us  [reversed_order(): split = values.reshape(shape[:axis] + (2,) * bits + shape[axis + 1:])]
    reshape x0 -> x10, local copies, waits for them, and re-layouts: none -> 19.7 us  [the longest x9 16.2 us: pack_dec(): block = block.reshape(data_count, height, model_count, tiles, LANES)]
  transfers between devices with their start and end apart: 26 -> 12, of which waited for: 25 -> 10; matrix products, arithmetic and copies ran while one was open for 6% -> 20% of each run, Pallas kernels for 0% -> 0%
where the time goes in v1:
time: 647 us; the launch traced here: 636 us
  waiting for transfers between devices  152 us (23%)
  matrix products  140 us (22%)
  Pallas kernels  129 us (20%)
  local copies, waits for them, and re-layouts  126 us (19%)
  other arithmetic  46.7 us (7%)
  blocking collectives  16.9 us (3%)
  between operations  16.1 us (2%)
  starting transfers between devices  9.59 us (1%)
    pallas_call x1, Pallas kernels, reduce_all(): pl.pallas_call(kernel, out_shape=out_shape, in_specs=[pl.BlockSpec(memory...  129 us
    reduce_scatter x5, waiting for transfers between devices, collect_rows(): lax.psum_scatter(values.astype(jnp.bfloat16), 'mp', scatter_dimension=0,...  78.3 us
    all_gather x5, waiting for transfers between devices, spread_rows(): return lax.all_gather(values, 'mp', axis=0, tiled=True)  66.7 us
    another operation x2, local copies, waits for them, and re-layouts, reversed_order(): split = values.reshape(shape[:axis] + (2,) * bits + shape[axis + 1:])  32.6 us
    unnamed x268, local copies, waits for them, and re-layouts  31.6 us
    dot_general x14, matrix products, matmul_t(): lax.dot_general(flat_rows, right_side, (((1,), (1,)), ((), ())), preferre...  29.4 us
    dot_general x14, matrix products, matmul(): product = jnp.dot(flat_rows, right_side, preferred_element_type=full_type)  27.5 us
    dot_general x14, matrix products, outer_sum(): lax.dot_general(left_side.reshape(-1, left_side.shape[-1]), right_side.re...  23.3 us
  transfers between devices with their start and end apart: 12, of which 10 were waited for; matrix products, arithmetic and copies ran while one was open for 20% of the time, Pallas kernels for 0%

profile of v1, /device:TPU:0, one launch (start us, length us, event | category | flops | bytes accessed | tf_op | source)
XLA Modules:
  0.0 636.4 jit_solution(14169814638140088940)
XLA Ops:
  12.4 18.8 %all-gather.6.cloned.1.call-done = bf16[8,64,1024]{2,1,0:T(8,128)(2,1)} async-done(((bf16[2,64,1024]{2,1,0:T(8,128)(2,1)}), bf16[8,64,1024]{2,1,0:T(8,128)(2,1)}) %all-gather.6.cloned.1.call-update) | async-done | bytes 1048592 | tf_op jit(solution)/shard_map/all_gather | solution.py:55
  44.2 25.0 %reduce-scatter.6.cloned.1.call-done = bf16[2,64,1024]{2,1,0:T(8,128)(2,1)} async-done(((bf16[8,64,1024]{2,1,0:T(8,128)(2,1)}), bf16[2,64,1024]{2,1,0:T(8,128)(2,1)}) %reduce-scatter.6.cloned.1.call-update) | async-done | bytes 262160 | tf_op jit(solution)/shard_map/reduce_scatter | solution.py:61
  73.3 16.8 %all-gather.8.cloned.1.call-done = bf16[8,64,1024]{2,1,0:T(8,128)(2,1)} async-done(((bf16[2,64,1024]{2,1,0:T(8,128)(2,1)}), bf16[8,64,1024]{2,1,0:T(8,128)(2,1)}) %all-gather.8.cloned.1.call-update) | async-done | bytes 1048592 | tf_op jit(solution)/shard_map/all_gather | solution.py:55
  93.9 5.7 multiply_convert_fusion.2
  102.9 25.0 %reduce-scatter.8.cloned.1.call-done = bf16[2,64,1024]{2,1,0:T(8,128)(2,1)} async-done(((bf16[8,64,1024]{2,1,0:T(8,128)(2,1)}), bf16[2,64,1024]{2,1,0:T(8,128)(2,1)}) %reduce-scatter.8.cloned.1.call-update) | async-done | bytes 262160 | tf_op jit(solution)/shard_map/reduce_scatter | solution.py:61
  132.5 14.1 %all-gather.10.cloned.1.call-done = bf16[8,64,1024]{2,1,0:T(8,128)(2,1)} async-done(((bf16[2,64,1024]{2,1,0:T(8,128)(2,1)}), bf16[8,64,1024]{2,1,0:T(8,128)(2,1)}) %all-gather.10.cloned.1.call-update) | async-done | bytes 1048592 | tf_op jit(solution)/shard_map/all_gather | solution.py:55
  149.0 5.5 all-to-all-start
  191.7 5.3 fusion.71
  200.4 10.5 %multiply_convert_fusion.1 = (bf16[2,256,2048]{2,1,0:T(8,128)(2,1)}, f32[2,256,2048]{2,1,0:T(8,128)S(1)}) fusion(f32[2,256,2048]{2,1,0:T(8,128)S(1)} %get-tuple-element.189, u8[256,2048]{1,0:T(8,128)(4,1)S(1)} %get-tuple-element.148, u8[256,2048]{1,0:T(8,128)(4,1)S(1)} %get-tuple-element.147), kind=kLoop, calls=%fused_computation.29 | loop fusion | flops 73400320 | bytes 11534336 | tf_op jit(solution)/shard_map/convert_element_type | solution.py:181
  219.7 4.6 fusion.197
  224.3 5.8 fusion.80
  230.1 13.5 %fusion.86 = bf16[2,16,32,256]{3,2,1,0:T(8,128)(2,1)} fusion(bf16[2,256,16,32]{1,3,2,0:T(8,128)(2,1)S(1)} %bitcast.329, f32[2,16,256,256]{2,3,1,0:T(8,128)} %fusion.197, f32[2,16,256,256]{2,3,1,0:T(8,128)} %copy-done.2, f32[2,16,256]{2,1,0:T(8,128)S(1)} %log_add_fusion), kind=kOutput, calls=%fused_computation.128 | convolution fusion | flops 153362688 | bytes 17858560 | tf_op jit(solution)/shard_map/while/body/eval_jaxpr/nhqk,nqhd->nkhd/dot_general | solution.py:146
  243.6 14.8 %fusion.83 = bf16[2,16,32,256]{3,2,1,0:T(8,128)(2,1)S(1)} fusion(bf16[2,256,16,32]{1,3,2,0:T(8,128)(2,1)S(1)} %bitcast.331, f32[2,16,256,256]{2,3,1,0:T(8,128)} %fusion.197, f32[2,16,256,256]{2,3,1,0:T(8,128)} %copy-done.2, f32[2,16,256]{2,1,0:T(8,128)S(1)} %log_add_fusion), kind=kOutput, calls=%fused_computation.127 | convolution fusion | flops 153362688 | bytes 17858560 | tf_op jit(solution)/shard_map/while/body/eval_jaxpr/nhqk,nkhd->nqhd/dot_general | solution.py:143
  264.6 7.0 %all_to_all.43 = bf16[4,2,8192]{2,1,0:T(2,128)(2,1)S(1)} all-to-all(bf16[4,2,8192]{2,1,0:T(2,128)(2,1)S(1)} %reshape.555), channel_id=1, replica_groups=mesh['dp'=8,'mp'=4] {'mp'}, dimensions={0} | all-to-all | bytes 262144 | tf_op jit(solution)/shard_map/all_to_all | solution.py:575
  272.0 9.9 %all_to_all.44 = bf16[8,1,64,128]{3,2,1,0:T(8,128)(2,1)S(1)} all-to-all(bf16[8,1,64,128]{3,2,1,0:T(8,128)(2,1)S(1)} %bitcast.370), channel_id=1, replica_groups=mesh['dp'=8,'mp'=4] {'dp'}, dimensions={0} | all-to-all | bytes 262144 | tf_op jit(solution)/shard_map/all_to_all | solution.py:574
  284.3 21.8 %reduce-scatter.10.cloned.1.call-done = bf16[2,64,1024]{2,1,0:T(8,128)(2,1)} async-done(((bf16[8,64,1024]{2,1,0:T(8,128)(2,1)}), bf16[2,64,1024]{2,1,0:T(8,128)(2,1)}) %reduce-scatter.10.cloned.1.call-update) | async-done | bytes 262160 | tf_op jit(solution)/shard_map/reduce_scatter | solution.py:61
  307.6 16.9 %all-gather.12.cloned.1.call-done = bf16[8,64,1024]{2,1,0:T(8,128)(2,1)} async-done(((bf16[2,64,1024]{2,1,0:T(8,128)(2,1)}), bf16[8,64,1024]{2,1,0:T(8,128)(2,1)}) %all-gather.12.cloned.1.call-update) | async-done | bytes 1048592 | tf_op jit(solution)/shard_map/all_gather | solution.py:55
  324.6 5.1 add_convert_fusion.2
  342.2 4.4 bitcast_convert_fusion
  351.5 6.5 %reduce-scatter.12.cloned.1.call-done = bf16[2,64,1024]{2,1,0:T(8,128)(2,1)} async-done(((bf16[8,64,1024]{2,1,0:T(8,128)(2,1)}), bf16[2,64,1024]{2,1,0:T(8,128)(2,1)}) %reduce-scatter.12.cloned.1.call-update) | async-done | bytes 262160 | tf_op jit(solution)/shard_map/reduce_scatter | solution.py:61
  364.7 4.5 reshape.531
  446.1 15.6 %reshape_reshape.29 = bf16[2,2,2,128,3200]{3,2,1,0,4:T(2,128)(2,1)} reshape(bf16[1024,3200]{0,1:T(8,128)(2,1)} %fusion.54) | data formatting | bytes 13107200 | tf_op jit(solution)/shard_map/reshape;reshape | solution.py:369
  461.7 17.0 %copy.172 = bf16[2,2,2,128,3200]{4,3,0,1,2:T(8,128)(2,1)} copy(bf16[2,2,2,128,3200]{3,2,1,0,4:T(2,128)(2,1)} %reshape_reshape.29) | data formatting | bytes 13107200 | tf_op jit(solution)/shard_map/reshape;reshape | solution.py:369
  481.9 129.1 %shard_map.400 = (f32[128,256]{1,0:T(8,128)}, f32[128,256]{1,0:T(8,128)}, f32[128,256]{1,0:T(8,128)}, f32[128,1024]{1,0:T(8,128)}, f32[128,128]{1,0:T(8,128)}, /...) custom-call(bf16[8,128,3200]{2,1,0:T(8,128)(2,1)} %bitcast.307, ...), custom_call_target="tpu_custom_call" | custom-call | tf_op jit(solution)/shard_map/pallas_call | solution.py:490
  (435 shorter events, 217.0 us)
Async XLA Ops:
  7.2 190.8 %copy-start = (bf16[512,2048]{1,0:T(8,128)(2,1)S(1)}, bf16[512,2048]{1,0:T(8,128)(2,1)}, u32[]{:S(2)}) copy-start(bf16[512,2048]{1,0:T(8,128)(2,1)} %param.46) | copy-start | bytes 6291460
  7.2 23.9 %all-gather.6.cloned.1.call-start = ((), (), s32[]{:S(2)}) async-start(), calls=%async_computation.9 | async-start | bytes 1310720 | tf_op jit(solution)/shard_map/all_gather | solution.py:55
  11.6 57.6 %reduce-scatter.6.cloned.1.call-start = ((), (), s32[]{:S(2)}) async-start(), calls=%async_computation.10 | async-start | bytes 1310720 | tf_op jit(solution)/shard_map/reduce_scatter | solution.py:61
  41.4 28.8 %copy-start.69 = (f32[8,4,64]{2,1,0:T(4,128)}, f32[8,4,64]{2,1,0:T(4,128)S(1)}, u32[]{:S(2)}) copy-start(f32[8,4,64]{2,1,0:T(4,128)S(1)} %fusion.98) | copy-start | bytes 24580
  41.4 30.0 %copy-start.66 = (f32[1024]{0:T(1024)S(1)}, f32[1024]{0:T(1024)}, u32[]{:S(2)}) copy-start(f32[1024]{0:T(1024)} %param.35) | copy-start | bytes 12292
  44.1 46.1 %all-gather.8.cloned.1.call-start = ((), (), s32[]{:S(2)}) async-start(), calls=%async_computation.11 | async-start | bytes 1310720 | tf_op jit(solution)/shard_map/all_gather | solution.py:55
  73.3 54.6 %reduce-scatter.8.cloned.1.call-start = ((), (), s32[]{:S(2)}) async-start(), calls=%async_computation.12 | async-start | bytes 1310720 | tf_op jit(solution)/shard_map/reduce_scatter | solution.py:61
  100.5 29.2 %copy-start.108 = (f32[2]{0:T(128)S(1)}, f32[2]{0:T(128)}, u32[]{:S(2)}) copy-start(f32[2]{0:T(128)} %param.29) | copy-start | bytes 28
  100.5 29.2 %copy-start.26 = (bf16[512,768]{1,0:T(8,128)(2,1)S(1)}, bf16[512,768]{1,0:T(8,128)(2,1)}, u32[]{:S(2)}) copy-start(bf16[512,768]{1,0:T(8,128)(2,1)} %param.48) | copy-start | bytes 2359300
  102.8 54.6 %copy-start.98 = (s32[2,256]{1,0:T(2,128)S(1)}, s32[2,256]{1,0:T(2,128)}, u32[]{:S(2)}) copy-start(s32[2,256]{1,0:T(2,128)} %param.28) | copy-start | bytes 6148
  102.8 63.3 %copy-start.107 = (s32[2,256]{1,0:T(2,128)S(1)}, s32[2,256]{1,0:T(2,128)}, u32[]{:S(2)}) copy-start(s32[2,256]{1,0:T(2,128)} %param.27) | copy-start | bytes 6148
  102.8 43.8 %all-gather.10.cloned.1.call-start = ((), (), s32[]{:S(2)}) async-start(), calls=%async_computation.13 | async-start | bytes 1310720 | tf_op jit(solution)/shard_map/all_gather | solution.py:55
  149.0 13.0 %all-to-all-start = ((bf16[8,1,64,128]{3,2,1,0:T(8,128)(2,1)}), bf16[8,1,64,128]{3,2,1,0:T(8,128)(2,1)}, u32[]{:S(2)}, u32[]{:S(2)}) async-start(bf16[8,1,64,128]{3,2,1,0:T(8,128)(2,1)} %fusion.91), calls=%async_computation.2 | async-start | bytes 262144 | tf_op jit(solution)/shard_map/all_to_all | solution.py:549
  162.0 7.9 %all-to-all-start.1 = ((bf16[8,1,64,128]{3,2,1,0:T(8,128)(2,1)}), bf16[8,1,64,128]{3,2,1,0:T(8,128)(2,1)S(1)}, u32[]{:S(2)}, u32[]{:S(2)}) async-start(bf16[8,1,64,128]{3,2,1,0:T(8,128)(2,1)} %all-to-all-done), calls=%async_computation.3 | async-start | bytes 262144 | tf_op jit(solution)/shard_map/all_to_all | solution.py:548
  165.3 140.9 %reduce-scatter.10.cloned.1.call-start = ((), (), s32[]{:S(2)}) async-start(), calls=%async_computation.14 | async-start | bytes 1310720 | tf_op jit(solution)/shard_map/reduce_scatter | solution.py:61
  264.0 42.3 %copy-start.44 = (bf16[8,4,64,64]{3,2,1,0:T(8,128)(2,1)S(1)}, bf16[8,4,64,64]{3,2,1,0:T(8,128)(2,1)}, u32[]{:S(2)}) copy-start(bf16[8,4,64,64]{3,2,1,0:T(8,128)(2,1)} %copy-done.43) | copy-start | bytes 786436
  284.3 40.3 %all-gather.12.cloned.1.call-start = ((), (), s32[]{:S(2)}) async-start(), calls=%async_computation.15 | async-start | bytes 1310720 | tf_op jit(solution)/shard_map/all_gather | solution.py:55
  306.2 51.9 %reduce-scatter.12.cloned.1.call-start = ((), (), s32[]{:S(2)}) async-start(), calls=%async_computation.16 | async-start | bytes 1310720 | tf_op jit(solution)/shard_map/reduce_scatter | solution.py:61
  333.0 69.0 %all-gather.14.cloned.1.call-start = ((), (), s32[]{:S(2)}) async-start(), calls=%async_computation.17 | async-start | bytes 1310720 | tf_op jit(solution)/shard_map/all_gather | solution.py:55
  363.1 115.6 %reduce-scatter.14.cloned.1.call-start = ((), (), s32[]{:S(2)}) async-start(), calls=%async_computation.18 | async-start | bytes 1310720 | tf_op jit(solution)/shard_map/reduce_scatter | solution.py:61
  481.9 131.9 %copy-start.22 = (bf16[2,64,1024]{2,1,0:T(8,128)(2,1)S(1)}, bf16[2,64,1024]{2,1,0:T(8,128)(2,1)}, u32[]{:S(2)}) copy-start(bf16[2,64,1024]{2,1,0:T(8,128)(2,1)} %reduce-scatter.12.cloned.1.call-done) | copy-start | bytes 786436
  481.9 131.9 %copy-start.29 = (bf16[2,64,1024]{2,1,0:T(8,128)(2,1)S(1)}, bf16[2,64,1024]{2,1,0:T(8,128)(2,1)}, u32[]{:S(2)}) copy-start(bf16[2,64,1024]{2,1,0:T(8,128)(2,1)} %reduce-scatter.14.cloned.1.call-done) | copy-start | bytes 786436
  481.9 131.9 %copy-start.91 = (f32[2,64]{1,0:T(2,128)S(1)}, f32[2,64]{1,0:T(2,128)}, u32[]{:S(2)}) copy-start(f32[2,64]{1,0:T(2,128)} %copy-done.90) | copy-start | bytes 1540
  481.9 147.2 %copy-start.1 = (bf16[512,2048]{1,0:T(8,128)(2,1)S(1)}, bf16[512,2048]{1,0:T(8,128)(2,1)}, u32[]{:S(2)}) copy-start(bf16[512,2048]{1,0:T(8,128)(2,1)} %param.46) | copy-start | bytes 6291460
  (107 other events, 859.3 us)
Sparse Core Ops, SparseCore 0:
  11.7 19.4 all-gather.5
  44.2 24.8 reduce-scatter.5
  73.4 16.7 all-gather.7
  102.9 24.8 reduce-scatter.7
  129.8 16.7 all-gather.9
  284.4 21.7 reduce-scatter.9
  307.8 16.7 all-gather.11
  333.1 24.8 reduce-scatter.11
  363.3 16.7 all-gather.13
  420.5 24.9 reduce-scatter.13

commit v2 on v0

--- a/solution.py
+++ b/solution.py
@@ -1,6 +1,10 @@
+import math
+
 import jax
 import jax.numpy as jnp
 from jax import lax
+from jax.experimental import pallas as pl
+from jax.experimental.pallas import tpu as pltpu
 from jax.sharding import PartitionSpec as P
 
 HE = 16
@@ -13,6 +17,1198 @@
 masked_score = -1e30
 low_type = jnp.bfloat16
 full_type = jnp.float32
+
+
+MESH = pl.DeviceIdType.MESH
+LANES = 128
+
+
+def log2_of(count):
+    bits = count.bit_length() - 1
+    assert 1 << bits == count
+    return bits
+
+
+def bit_reverse(index, bits):
+    out = 0
+    for position in range(bits):
+        out = out * 2 + ((index >> position) & 1)
+    return out
+
+
+def partner(axis, bit):
+    dp, mp = lax.axis_index("dp"), lax.axis_index("mp")
+    step = 1 << bit
+    if axis == "dp":
+        return (dp ^ step, mp), (dp >> bit) & 1
+    return (dp, mp ^ step), (mp >> bit) & 1
+
+
+def enter_barrier(partners):
+    barrier = pltpu.get_barrier_semaphore()
+    for peer in partners:
+        pl.semaphore_signal(barrier, inc=1, device_id=peer, device_id_type=MESH)
+    pl.semaphore_wait(barrier, len(partners))
+
+
+class HalvingSum:
+    def __init__(self, stages, buffers, window, send_sems, recv_sems):
+        self.stages, self.buffers, self.window = stages, buffers, window
+        self.send_sems, self.recv_sems = send_sems, recv_sems
+        self.copies = [None] * len(stages)
+
+    def view(self, index, start, size):
+        return self.buffers[index].at[(pl.ds(start, size),) + self.window]
+
+    def start(self, index):
+        peer, mine = partner(*self.stages[index])
+        half = self.buffers[index].shape[0] // 2
+        copy = pltpu.make_async_remote_copy(
+            src_ref=self.view(index, (1 - mine) * half, half),
+            dst_ref=self.view(index + 1, 0, half),
+            send_sem=self.send_sems.at[index],
+            recv_sem=self.recv_sems.at[index],
+            device_id=peer,
+            device_id_type=MESH,
+        )
+        copy.start()
+        self.copies[index] = copy
+
+    def finish(self, index):
+        self.copies[index].wait()
+        peer, mine = partner(*self.stages[index])
+        half = self.buffers[index].shape[0] // 2
+
+        def one(position, carry):
+            there = self.buffers[index + 1].at[(position,) + self.window]
+            here = self.buffers[index].at[(mine * half + position,) + self.window]
+            there[...] = there[...] + here[...]
+            return carry
+
+        lax.fori_loop(0, half, one, 0)
+
+
+def dec_pieces(data_count, model_count, shapes):
+    offset, pieces = 0, []
+    for rows, columns in shapes:
+        height, width = rows // data_count, columns // model_count
+        tiles = -(-width // LANES)
+        pieces.append((offset, height, width, tiles))
+        offset += height * tiles
+    return pieces, offset
+
+
+LOG2E = 1.4426950408889634
+
+
+def dot_as(left, right, left_dim, right_dim):
+    return lax.dot_general(
+        left, right, (((left_dim,), (right_dim,)), ((), ())), preferred_element_type=full_type
+    )
+
+
+def norm_parts(values):
+    center = values - jnp.mean(values, axis=-1, keepdims=True)
+    scale = lax.rsqrt(jnp.mean(center * center, axis=-1, keepdims=True) + eps_norm)
+    return center * scale, scale
+
+
+def norm_back(normed, scale, grad_scaled):
+    first = jnp.mean(grad_scaled, axis=-1, keepdims=True)
+    second = jnp.mean(grad_scaled * normed, axis=-1, keepdims=True)
+    return (grad_scaled - first - normed * second) * scale
+
+
+def gelu_pair(values):
+    below = 0.5 + 0.5 * lax.erf(values * (0.5**0.5))
+    density = jnp.exp2(values * values * (-0.5 * LOG2E)) * ((2.0 * math.pi) ** -0.5)
+    return values * below, below + values * density
+
+
+def decoder_kernel(images, heads, side, pieces, data_count, model_count, *refs):
+    (
+        arrived,
+        order_ref,
+        keep_ref,
+        dist_ref,
+        gain_attn,
+        w_query,
+        w_key,
+        w_value,
+        w_out,
+        gain_mlp,
+        w_up,
+        w_down,
+        w_pred,
+        mask_token,
+        cotangent,
+        decoded,
+        packed,
+        grad_arrived,
+        small,
+        xs,
+        qkv_weights,
+        a_s,
+        qkv_s,
+        e_s,
+        inv_s,
+        o_s,
+        mid_s,
+        c_s,
+        g_s,
+        du_s,
+        low_s,
+        dy_s,
+        dm_s,
+        db_s,
+        do_s,
+    ) = refs
+    length = side * side
+    visible = arrived.shape[1]
+    width = w_query.shape[0]
+    hidden = w_up.shape[1]
+    size = width // heads
+    scaling = float(size) ** -0.5
+    chunk = 512
+    place = lax.broadcasted_iota(jnp.int32, (length, visible), 0)
+    turn = lax.broadcasted_iota(jnp.int32, (length, visible), 1)
+
+    def picks(image):
+        order = order_ref[image, :, :visible]
+        count = jnp.sum(keep_ref[image], axis=1, keepdims=True)
+        return jnp.where((order == place) & (turn < count), 1.0, 0.0)
+
+    def rows_of(image):
+        return pl.ds(pl.multiple_of(image * length, length), length)
+
+    for position, weight in enumerate((w_query, w_key, w_value)):
+        qkv_weights[position * width : (position + 1) * width, :] = weight[...].T
+    small[...] = jnp.zeros_like(small)
+
+    def first_part(image, carry):
+        rows = rows_of(image)
+        pick = picks(image)
+        hidden_rows = 1.0 - jnp.sum(pick, axis=1, keepdims=True)
+        quarter = width // 4
+        lane = lax.broadcasted_iota(jnp.int32, (side, quarter), 1).astype(full_type)
+        line = lax.broadcasted_iota(jnp.int32, (side, quarter), 0).astype(full_type)
+        angle = dist_ref[image] * line * jnp.exp(lane * (-math.log(10000.0) / quarter))
+        table = jnp.concatenate([jnp.sin(angle), jnp.cos(angle)], axis=1)
+        by_row = jnp.broadcast_to(table[:, None, :], (side, side, 2 * quarter))
+        by_col = jnp.broadcast_to(table[None, :, :], (side, side, 2 * quarter))
+        codes = jnp.concatenate(
+            [by_row.reshape(length, 2 * quarter), by_col.reshape(length, 2 * quarter)], axis=1
+        )
+        start = jnp.dot(pick.astype(low_type), arrived[image], preferred_element_type=full_type)
+        start = start + hidden_rows * mask_token[...] + codes
+        xs[...] = start
+        normed, scale = norm_parts(start)
+        a_s[rows, :] = (normed * gain_attn[...]).astype(low_type)
+        for position in range(3):
+            part = dot_as(
+                qkv_weights[position * width : (position + 1) * width, :], a_s[rows, :], 1, 1
+            )
+            if position == 0:
+                part = part * (scaling * LOG2E)
+            qkv_s[position * width : (position + 1) * width, rows] = part.astype(low_type)
+
+        def one_head(head, inner):
+            span = pl.multiple_of(head * size, size)
+            query = qkv_s[pl.ds(span, size), rows]
+            key = qkv_s[pl.ds(width + span, size), rows]
+            value = qkv_s[pl.ds(2 * width + span, size), rows]
+            scores = dot_as(key, query, 0, 0)
+            weights = jnp.exp2(scores - jnp.max(scores, axis=0, keepdims=True))
+            inverse = 1.0 / jnp.sum(weights, axis=0, keepdims=True)
+            weights = weights.astype(low_type)
+            e_s[head] = weights
+            inv_s[head] = inverse
+            mixed = jnp.dot(value, weights, preferred_element_type=full_type)
+            o_s[pl.ds(span, size), rows] = (mixed * inverse).astype(low_type)
+            return inner
+
+        lax.fori_loop(0, heads, one_head, 0, unroll=4)
+
+        middle = start + dot_as(o_s[:, rows], w_out[...], 0, 0)
+        mid_s[...] = middle
+        normed, scale = norm_parts(middle)
+        c_s[rows, :] = (normed * gain_mlp[...]).astype(low_type)
+        for position in range(hidden // chunk):
+            cols = slice(position * chunk, (position + 1) * chunk)
+            pre = jnp.dot(c_s[rows, :], w_up[:, cols], preferred_element_type=full_type)
+            active, slope = gelu_pair(pre)
+            g_s[rows, cols] = active.astype(low_type)
+            du_s[rows, cols] = slope.astype(low_type)
+        outputs = middle + jnp.dot(g_s[rows, :], w_down[...], preferred_element_type=full_type)
+        low_s[rows, :] = outputs.astype(low_type)
+        decoded[image] = jnp.dot(low_s[rows, :], w_pred[...], preferred_element_type=full_type)
+
+        grad_out = dot_as(cotangent[image], w_pred[...], 1, 1)
+        dm_s[rows, :] = grad_out.astype(low_type)
+        for position in range(hidden // chunk):
+            cols = slice(position * chunk, (position + 1) * chunk)
+            grad_active = dot_as(dm_s[rows, :], w_down[cols, :], 1, 1)
+            du_s[rows, cols] = (grad_active * du_s[rows, cols].astype(full_type)).astype(low_type)
+        grad_second = dot_as(du_s[rows, :], w_up[...], 1, 1)
+        normed, scale = norm_parts(mid_s[...])
+        small[1:2, :] += jnp.sum(grad_second * normed, axis=0, keepdims=True)
+        grad_middle = grad_out + norm_back(normed, scale, grad_second * gain_mlp[...])
+        dy_s[...] = grad_middle
+        db_s[rows, :] = grad_middle.astype(low_type)
+        do_s[...] = dot_as(w_out[...], db_s[rows, :], 1, 1)
+
+        def back_head(head, inner):
+            span = pl.multiple_of(head * size, size)
+            query = qkv_s[pl.ds(span, size), rows]
+            key = qkv_s[pl.ds(width + span, size), rows]
+            value = qkv_s[pl.ds(2 * width + span, size), rows]
+            weights = e_s[head]
+            grad_full = do_s[pl.ds(span, size), :] * (inv_s[head] * scaling)
+            mixed = o_s[pl.ds(span, size), rows].astype(full_type)
+            shift = jnp.sum(grad_full * mixed, axis=0, keepdims=True)
+            grad_low = grad_full.astype(low_type)
+            grad_probs = dot_as(value, grad_low, 0, 0)
+            grad_scores = (weights.astype(full_type) * (grad_probs - shift)).astype(low_type)
+            grad_value = dot_as(grad_low, weights, 1, 1) * (1.0 / scaling)
+            grad_query = jnp.dot(key, grad_scores, preferred_element_type=full_type)
+            grad_key = dot_as(query, grad_scores, 1, 1) * (1.0 / (scaling * LOG2E))
+            qkv_s[pl.ds(span, size), rows] = grad_query.astype(low_type)
+            qkv_s[pl.ds(width + span, size), rows] = grad_key.astype(low_type)
+            qkv_s[pl.ds(2 * width + span, size), rows] = grad_value.astype(low_type)
+            return inner
+
+        lax.fori_loop(0, heads, back_head, 0, unroll=4)
+
+        grad_normed = dot_as(qkv_s[:, rows], qkv_weights[...], 0, 0)
+        normed, scale = norm_parts(xs[...])
+        small[0:1, :] += jnp.sum(grad_normed * normed, axis=0, keepdims=True)
+        grad_start = dy_s[...] + norm_back(normed, scale, grad_normed * gain_attn[...])
+        small[2:3, :] += jnp.sum(hidden_rows * grad_start, axis=0, keepdims=True)
+        grad_arrived[image] = dot_as(
+            pick.astype(low_type), grad_start.astype(low_type), 0, 0
+        ).astype(low_type)
+        return carry
+
+    lax.fori_loop(0, images, first_part, 0)
+
+    data_bits, model_bits = log2_of(data_count), log2_of(model_count)
+
+    def store(piece, product):
+        offset, height, span, tiles = piece
+        for column in range(model_count):
+            for tile in range(tiles):
+                lanes = min(LANES, span - tile * LANES)
+                first = column * span + tile * LANES
+                block = product[:, first : first + lanes].astype(low_type)
+                for row in range(data_count):
+                    spot = bit_reverse(column, model_bits) * data_count
+                    spot = spot + bit_reverse(row, data_bits)
+                    packed[
+                        spot, offset + tile * height : offset + (tile + 1) * height, :lanes
+                    ] = block[row * height : (row + 1) * height, :]
+
+    for position in range(3):
+        grads = qkv_s[position * width : (position + 1) * width, :]
+        store(pieces[position], dot_as(a_s[...], grads, 0, 1))
+    store(pieces[3], jnp.dot(o_s[...], db_s[...], preferred_element_type=full_type))
+    store(pieces[4], dot_as(c_s[...], du_s[...], 0, 0))
+    store(pieces[5], dot_as(g_s[...], dm_s[...], 0, 0))
+    store(pieces[6], dot_as(low_s[...], cotangent[...].reshape(-1, cotangent.shape[2]), 0, 0))
+
+
+def decode(
+    arrived, grid_order, grid_keep, ground_dist, weights, mask_token, pred_proj, cotangent
+):
+    gain_attn, w_query, w_key, w_value, w_out, gain_mlp, w_up, w_down = weights
+    data_count, model_count = lax.axis_size("dp"), lax.axis_size("mp")
+    images, length, pixels = cotangent.shape
+    width, hidden = w_up.shape
+    rows = images * length
+    matrices = [w_query, w_key, w_value, w_out, w_up, w_down, pred_proj]
+    pieces, height = dec_pieces(data_count, model_count, [m.shape for m in matrices])
+
+    def kernel(*refs):
+        decoder_kernel(images, HD, SIDE, pieces, data_count, model_count, *refs)
+
+    vmem = pl.BlockSpec(memory_space=pltpu.VMEM)
+    return pl.pallas_call(
+        kernel,
+        out_shape=[
+            jax.ShapeDtypeStruct((images, length, pixels), full_type),
+            jax.ShapeDtypeStruct((data_count * model_count, height, LANES), low_type),
+            jax.ShapeDtypeStruct(arrived.shape, low_type),
+            jax.ShapeDtypeStruct((3, width), full_type),
+        ],
+        in_specs=[vmem] * 3 + [pl.BlockSpec(memory_space=pltpu.SMEM)] + [vmem] * 11,
+        out_specs=[vmem] * 4,
+        scratch_shapes=[
+            pltpu.VMEM((length, width), full_type),
+            pltpu.VMEM((3 * width, width), low_type),
+            pltpu.VMEM((rows, width), low_type),
+            pltpu.VMEM((3 * width, rows), low_type),
+            pltpu.VMEM((HD, length, length), low_type),
+            pltpu.VMEM((HD, 1, length), full_type),
+            pltpu.VMEM((width, rows), low_type),
+            pltpu.VMEM((length, width), full_type),
+            pltpu.VMEM((rows, width), low_type),
+            pltpu.VMEM((rows, hidden), low_type),
+            pltpu.VMEM((rows, hidden), low_type),
+            pltpu.VMEM((rows, width), low_type),
+            pltpu.VMEM((length, width), full_type),
+            pltpu.VMEM((rows, width), low_type),
+            pltpu.VMEM((rows, width), low_type),
+            pltpu.VMEM((width, length), full_type),
+        ],
+        compiler_params=pltpu.CompilerParams(vmem_limit_bytes=60 * 2**20),
+    )(
+        arrived,
+        grid_order[:, None, :],
+        grid_keep[:, None, :],
+        ground_dist,
+        gain_attn.reshape(1, -1),
+        w_query,
+        w_key,
+        w_value,
+        w_out,
+        gain_mlp.reshape(1, -1),
+        w_up,
+        w_down,
+        pred_proj,
+        mask_token.reshape(1, -1),
+        cotangent,
+    )
+
+
+def low_bit(mask):
+    return (mask & -mask).bit_length() - 1
+
+
+def visit_order(count):
+    return sorted(range(count), key=lambda mask: (mask.bit_length(), -mask))
+
+
+def visit_mask(step, count):
+    mask = jnp.int32(0)
+    for position, value in enumerate(visit_order(count)):
+        mask = jnp.where(step == position, value, mask)
+    return mask
+
+
+class Gather:
+    def __init__(self, own, slot_view, send_sems, recv_sems):
+        self.own, self.slot_view = own, slot_view
+        self.send_sems, self.recv_sems = send_sems, recv_sems
+        self.count = lax.axis_size("mp")
+        self.index = lax.axis_index("mp")
+
+    def copy(self, mask):
+        bit = low_bit(mask)
+        carried = mask ^ (1 << bit)
+        place = self.slot_view(self.index ^ carried)
+        return pltpu.make_async_remote_copy(
+            src_ref=self.own if carried == 0 else place,
+            dst_ref=place,
+            send_sem=self.send_sems.at[mask],
+            recv_sem=self.recv_sems.at[mask],
+            device_id=partner("mp", bit)[0],
+            device_id_type=MESH,
+        )
+
+    def start(self):
+        for bit in reversed(range(log2_of(self.count))):
+            self.copy(1 << bit).start()
+
+    def arrive(self, mask):
+        self.copy(mask).wait_recv()
+        for bit in reversed(range(low_bit(mask))):
+            self.copy(mask | (1 << bit)).start()
+
+    def arrive_group(self, length):
+        group = [mask for mask in range(1, self.count) if mask.bit_length() == length]
+        for mask in sorted(group, key=lambda one: -low_bit(one)):
+            self.arrive(mask)
+
+    def arrive_all(self):
+        for length in range(1, log2_of(self.count) + 1):
+            self.arrive_group(length)
+
+    def arrive_at(self, step):
+        for length in range(1, log2_of(self.count) + 1):
+            @pl.when(step == 1 << (length - 1))
+            def _():
+                self.arrive_group(length)
+
+    def drain(self):
+        for mask in range(1, self.count):
+            self.copy(mask).wait_send()
+
+
+class Scatter:
+    def __init__(self, parts, total, landing, send_sems, recv_sems):
+        self.parts, self.total, self.landing = parts, total, landing
+        self.send_sems, self.recv_sems = send_sems, recv_sems
+        self.count = lax.axis_size("mp")
+        self.index = lax.axis_index("mp")
+
+    def copy(self, mask):
+        return pltpu.make_async_remote_copy(
+            src_ref=self.parts.at[self.index ^ mask],
+            dst_ref=self.landing.at[mask],
+            send_sem=self.send_sems.at[mask],
+            recv_sem=self.recv_sems.at[mask],
+            device_id=partner("mp", low_bit(mask))[0],
+            device_id_type=MESH,
+        )
+
+    def put(self, mask, product):
+        @pl.when(mask == 0)
+        def _():
+            self.total[...] = self.total[...] + product
+
+        @pl.when(mask != 0)
+        def _():
+            self.parts[self.index ^ mask] = product.astype(low_type)
+
+        for odd in range(1, self.count, 2):
+            @pl.when(mask == odd)
+            def _():
+                self.copy(odd).start()
+
+    def finish_bit(self, bit):
+        step = 1 << bit
+        masks = [mask for mask in range(1, self.count) if low_bit(mask) == bit]
+        for mask in reversed(masks):
+            self.copy(mask).wait_recv()
+            rest = mask ^ step
+            if rest:
+                place = self.index ^ rest
+                self.parts[place] = self.parts[place] + self.landing[mask]
+                if low_bit(rest) == bit + 1:
+                    self.copy(rest).start()
+            else:
+                self.total[...] = self.total[...] + self.landing[mask].astype(full_type)
+
+    def drain(self):
+        for mask in range(1, self.count):
+            self.copy(mask).wait_send()
+
+
+def exchange_partners(images):
+    data_count, model_count = lax.axis_size("dp"), lax.axis_size("mp")
+    data, model = lax.axis_index("dp"), lax.axis_index("mp")
+    out = []
+    for image in range(images):
+        spot = (model * images + image) * data_count + data
+        device = spot // images
+        out.append((device // model_count, device % model_count, spot % images))
+    return out
+
+
+def is_here(peer):
+    return (peer[0] == lax.axis_index("dp")) & (peer[1] == lax.axis_index("mp"))
+
+
+class Exchange:
+    def __init__(self, images, source, target, send_sems, recv_sems):
+        self.partners = exchange_partners(images)
+        self.source, self.target = source, target
+        self.send_sems, self.recv_sems = send_sems, recv_sems
+
+    def copy(self, image):
+        data, model, slot = self.partners[image]
+        return pltpu.make_async_remote_copy(
+            src_ref=self.source.at[image],
+            dst_ref=self.target.at[slot],
+            send_sem=self.send_sems.at[image],
+            recv_sem=self.recv_sems.at[slot],
+            device_id=(data, model),
+            device_id_type=MESH,
+        )
+
+    def start(self):
+        for image, (data, model, slot) in enumerate(self.partners):
+            here = is_here((data, model))
+
+            @pl.when(here)
+            def _():
+                self.target[slot] = self.source[image]
+
+            @pl.when(jnp.logical_not(here))
+            def _():
+                self.copy(image).start()
+
+    def finish(self):
+        for image, (data, model, slot) in enumerate(self.partners):
+            @pl.when(jnp.logical_not(is_here((data, model))))
+            def _():
+                pltpu.make_async_remote_copy(
+                    src_ref=self.source.at[image],
+                    dst_ref=self.target.at[image],
+                    send_sem=self.send_sems.at[image],
+                    recv_sem=self.recv_sems.at[image],
+                    device_id=(data, model),
+                    device_id_type=MESH,
+                ).wait()
+
+
+def encoder_barrier(images, axes):
+    barrier = pltpu.get_barrier_semaphore()
+    count = images
+    for axis in axes:
+        for bit in range(log2_of(lax.axis_size(axis))):
+            count += 1
+            pl.semaphore_signal(
+                barrier, inc=1, device_id=partner(axis, bit)[0], device_id_type=MESH
+            )
+    for data, model, slot in exchange_partners(images):
+        pl.semaphore_signal(barrier, inc=1, device_id=(data, model), device_id_type=MESH)
+    pl.semaphore_wait(barrier, count)
+
+
+def encoder_kernel(images, visible, heads, *refs):
+    (
+        lengths,
+        tokens,
+        gain_attn,
+        w_query,
+        w_key,
+        w_value,
+        w_out,
+        gain_mlp,
+        w_up,
+        w_down,
+        w_embed,
+        arrived,
+        a_s,
+        qkv_s,
+        e_s,
+        inv_s,
+        o_own,
+        c_s,
+        g_s,
+        slope_s,
+        mid_s,
+        low_s,
+        embed_full,
+        qkv_weights,
+        token_slots,
+        out_full,
+        o_full,
+        embed_slots,
+        parts,
+        landing,
+        total,
+        embedded,
+        sems,
+        swap_sems,
+    ) = refs
+    count = lax.axis_size("mp")
+    index = lax.axis_index("mp")
+    block_rows = images * visible
+    columns = w_query.shape[1]
+    size = columns // heads
+    scaling = float(size) ** -0.5
+    hidden = w_up.shape[1]
+    chunk = 512
+
+    encoder_barrier(images, ["mp"])
+    token_gather = Gather(
+        tokens, lambda slot: token_slots.at[slot], sems.at[0], sems.at[1]
+    )
+    out_gather = Gather(
+        w_out,
+        lambda slot: out_full.at[pl.ds(pl.multiple_of(slot * columns, columns), columns)],
+        sems.at[2],
+        sems.at[3],
+    )
+    o_gather = Gather(
+        o_own,
+        lambda slot: o_full.at[pl.ds(pl.multiple_of(slot * columns, columns), columns)],
+        sems.at[4],
+        sems.at[5],
+    )
+    embed_gather = Gather(w_embed, lambda slot: embed_slots.at[slot], sems.at[6], sems.at[7])
+    scatter = Scatter(parts, total, landing, sems.at[8], sems.at[9])
+    swap = Exchange(images, embedded, arrived, swap_sems.at[0], swap_sems.at[1])
+
+    token_gather.start()
+    token_slots[index] = tokens[...]
+    out_full[pl.ds(pl.multiple_of(index * columns, columns), columns), :] = w_out[...]
+    embed_slots[index] = w_embed[...]
+    for position, weight in enumerate((w_query, w_key, w_value)):
+        qkv_weights[position * columns : (position + 1) * columns, :] = weight[...].T
+
+    def rows_of(slot):
+        return pl.ds(pl.multiple_of(slot * block_rows, block_rows), block_rows)
+
+    def attend(step, carry):
+        token_gather.arrive_at(step)
+
+        @pl.when(step == count // 2)
+        def _():
+            out_gather.start()
+
+        slot = index ^ visit_mask(step, count)
+        rows = rows_of(slot)
+        normed, scale = norm_parts(token_slots[slot].astype(full_type))
+        a_s[rows, :] = (normed * gain_attn[...]).astype(low_type)
+        for position in range(3):
+            span = slice(position * columns, (position + 1) * columns)
+            part = dot_as(qkv_weights[span, :], a_s[rows, :], 1, 1)
+            if position == 0:
+                part = part * (scaling * LOG2E)
+            qkv_s[span, rows] = part.astype(low_type)
+        key_row = lax.broadcasted_iota(jnp.int32, (block_rows, block_rows), 0)
+        query_row = lax.broadcasted_iota(jnp.int32, (block_rows, block_rows), 1)
+        valid = jnp.zeros((block_rows, block_rows), jnp.bool_)
+        for image in range(images):
+            first = image * visible
+            keys = (key_row >= first) & (key_row < first + lengths[slot * images + image])
+            valid = valid | (keys & (query_row >= first) & (query_row < first + visible))
+        for head in range(heads):
+            span = slice(head * size, (head + 1) * size)
+            query = qkv_s[span, rows]
+            key = qkv_s[columns + head * size : columns + (head + 1) * size, rows]
+            value = qkv_s[2 * columns + head * size : 2 * columns + (head + 1) * size, rows]
+            scores = jnp.where(valid, dot_as(key, query, 0, 0), masked_score)
+            weights = jnp.exp2(scores - jnp.max(scores, axis=0, keepdims=True))
+            inverse = 1.0 / jnp.sum(weights, axis=0, keepdims=True)
+            weights = weights.astype(low_type)
+            e_s[slot * heads + head] = weights
+            inv_s[slot * heads + head] = inverse
+            mixed = jnp.dot(value, weights, preferred_element_type=full_type)
+            o_own[span, rows] = (mixed * inverse).astype(low_type)
+        return carry
+
+    lax.fori_loop(0, count, attend, 0)
+    o_gather.start()
+    o_full[pl.ds(pl.multiple_of(index * columns, columns), columns), :] = o_own[...]
+    out_gather.arrive_all()
+    o_gather.arrive_all()
+    embed_gather.start()
+    total[...] = jnp.zeros_like(total)
+
+    def expand(step, carry):
+        mask = count - 1 - step
+        slot = index ^ mask
+        rows = rows_of(slot)
+        middle = token_slots[slot].astype(full_type) + dot_as(o_full[:, rows], out_full[...], 0, 0)
+
+        @pl.when(mask == 0)
+        def _():
+            mid_s[...] = middle
+
+        normed, scale = norm_parts(middle)
+        c_s[rows, :] = (normed * gain_mlp[...]).astype(low_type)
+        for first in range(0, hidden, chunk):
+            cols = slice(first, first + chunk)
+            pre = jnp.dot(c_s[rows, :], w_up[:, cols], preferred_element_type=full_type)
+            active, slope = gelu_pair(pre)
+            g_s[rows, cols] = active.astype(low_type)
+            slope_s[rows, cols] = slope.astype(low_type)
+        scatter.put(
+            mask, jnp.dot(g_s[rows, :], w_down[...], preferred_element_type=full_type)
+        )
+        return carry
+
+    lax.fori_loop(0, count, expand, 0)
+    bits = log2_of(count)
+    for bit in range(bits):
+        if bit == bits - 1:
+            embed_gather.arrive_all()
+            width = w_embed.shape[1]
+            for slot in range(count):
+                embed_full[:, slot * width : (slot + 1) * width] = embed_slots[slot]
+        scatter.finish_bit(bit)
+    low_s[...] = (mid_s[...] + total[...]).astype(low_type)
+    out = jnp.dot(low_s[...], embed_full[...], preferred_element_type=full_type)
+    embedded[...] = out.astype(low_type).reshape(embedded.shape)
+    swap.start()
+    for one in (token_gather, out_gather, o_gather, embed_gather, scatter):
+        one.drain()
+    swap.finish()
+
+
+def encode(tokens, lengths, weights, embed_proj):
+    gain_attn, w_query, w_key, w_value, w_out, gain_mlp, w_up, w_down = weights
+    model_count = lax.axis_size("mp")
+    images, visible, width = tokens.shape
+    rows = images * visible
+    heads = HE // model_count
+    columns, hidden = w_query.shape[1], w_up.shape[1]
+    out_width = embed_proj.shape[1] * model_count
+    every = rows * model_count
+
+    def kernel(*refs):
+        encoder_kernel(images, visible, heads, *refs)
+
+    vmem = pl.BlockSpec(memory_space=pltpu.VMEM)
+    shapes = [
+        ((images, visible, out_width), low_type),
+        ((every, width), low_type),
+        ((3 * columns, every), low_type),
+        ((model_count * heads, rows, rows), low_type),
+        ((model_count * heads, 1, rows), full_type),
+        ((columns, every), low_type),
+        ((every, width), low_type),
+        ((every, hidden), low_type),
+        ((every, hidden), low_type),
+        ((rows, width), full_type),
+        ((rows, width), low_type),
+        ((width, out_width), low_type),
+        ((3 * columns, width), low_type),
+    ]
+    return pl.pallas_call(
+        kernel,
+        out_shape=[jax.ShapeDtypeStruct(shape, kind) for shape, kind in shapes],
+        in_specs=[pl.BlockSpec(memory_space=pltpu.SMEM)] + [vmem] * 10,
+        out_specs=[vmem] * len(shapes),
+        scratch_shapes=[
+            pltpu.VMEM((model_count, rows, width), low_type),
+            pltpu.VMEM((width, width), low_type),
+            pltpu.VMEM((width, every), low_type),
+            pltpu.VMEM((model_count,) + embed_proj.shape, low_type),
+            pltpu.VMEM((model_count, rows, width), low_type),
+            pltpu.VMEM((model_count, rows, width), low_type),
+            pltpu.VMEM((rows, width), full_type),
+            pltpu.VMEM((images, visible, out_width), low_type),
+            pltpu.SemaphoreType.DMA((10, model_count)),
+            pltpu.SemaphoreType.DMA((2, images)),
+        ],
+        compiler_params=pltpu.CompilerParams(
+            collective_id=1, has_side_effects=True, vmem_limit_bytes=60 * 2**20
+        ),
+    )(
+        lengths,
+        tokens.reshape(rows, width),
+        gain_attn.reshape(1, -1),
+        w_query,
+        w_key,
+        w_value,
+        w_out,
+        gain_mlp.reshape(1, -1),
+        w_up,
+        w_down,
+        embed_proj,
+    )
+
+
+class Bulk:
+    def __init__(self, one):
+        self.one, self.stage = one, None
+
+    def start(self):
+        self.one.start(0)
+        self.stage = 0
+
+    def done(self):
+        return self.stage == len(self.one.stages)
+
+    def advance(self):
+        if self.done():
+            return
+        self.one.finish(self.stage)
+        self.stage += 1
+        if not self.done():
+            self.one.start(self.stage)
+
+
+def encoder_back_kernel(plan, *refs):
+    images, visible, heads, dec_pieces_list, embed_piece = plan
+    refs = list(refs)
+
+    def take(number):
+        head = refs[:number]
+        del refs[:number]
+        return head
+
+    (
+        grad_arrived,
+        tokens,
+        gain_attn,
+        w_out,
+        gain_mlp,
+        w_up,
+        w_down,
+        a_s,
+        qkv_s,
+        e_s,
+        inv_s,
+        o_own,
+        c_s,
+        g_s,
+        slope_s,
+        mid_s,
+        low_s,
+        embed_full,
+        qkv_weights,
+        dec_packed,
+        dec_small,
+    ) = take(21)
+    data_count, model_count = lax.axis_size("dp"), lax.axis_size("mp")
+    data_bits, model_bits = log2_of(data_count), log2_of(model_count)
+    (grad_tokens, g_query, g_key, g_value, g_up, g_out, g_down, g_embed, norm_wide, norm_thin) = (
+        take(10)
+    )
+    dec_outs = take(len(dec_pieces_list))
+    (
+        demb_own,
+        demb_slots,
+        dm_s,
+        du_s,
+        db_own,
+        db_s,
+        dqkv_s,
+        total,
+        parts_mlp,
+        landing_mlp,
+        parts_attn,
+        landing_attn,
+        dy_s,
+        do_s,
+        sems,
+        swap_sems,
+        row_packed,
+        col_packed,
+        embed_packed,
+    ) = take(19)
+    row_bufs = [row_packed] + take(data_bits)
+    col_bufs = [col_packed] + take(data_bits)
+    dec_bufs = [dec_packed] + take(data_bits + model_bits)
+    embed_bufs = [embed_packed] + take(data_bits + model_bits)
+    wide_acc, wide_got, thin_acc, thin_got = take(4)
+    row_sems, col_sems, dec_sems, embed_sems, norm_sems = take(5)
+    assert not refs
+
+    index = lax.axis_index("mp")
+    count = model_count
+    block_rows = images * visible
+    columns = w_out.shape[0]
+    size = columns // heads
+    scaling = float(size) ** -0.5
+    hidden, width = w_down.shape
+    chunk = 512
+    enc_stages = [("dp", bit) for bit in range(data_bits)]
+    all_stages = [("mp", bit) for bit in range(model_bits)] + enc_stages
+
+    encoder_barrier(images, ["mp", "dp"])
+    swap = Exchange(images, grad_arrived, demb_own, swap_sems.at[0], swap_sems.at[1])
+    swap.start()
+
+    def bulk(stages, bufs, axis, first, extent, pair, cut):
+        window = [slice(None), slice(None)]
+        window[axis - 1] = pl.ds(first, extent)
+        return Bulk(
+            HalvingSum(stages, bufs, tuple(window), pair.at[0, cut], pair.at[1, cut])
+        )
+
+    cuts = dec_sems.shape[1]
+    height = dec_packed.shape[1] // cuts
+    dec_sums = [
+        bulk(all_stages, dec_bufs, 1, cut * height, height, dec_sems, cut) for cut in range(cuts)
+    ]
+    embed_sum = bulk(all_stages, embed_bufs, 1, 0, embed_packed.shape[1], embed_sems, 0)
+    up_sums = [
+        bulk(enc_stages, row_bufs, 2, cut * (hidden // 2), hidden // 2, row_sems, cut)
+        for cut in range(2)
+    ]
+    qkv_sum = bulk(enc_stages, row_bufs, 2, hidden, 3 * columns, row_sems, 2)
+    down_sums = [
+        bulk(enc_stages, col_bufs, 1, cut * (hidden // 2), hidden // 2, col_sems, cut)
+        for cut in range(2)
+    ]
+    out_sum = bulk(enc_stages, col_bufs, 1, hidden, columns, col_sems, 2)
+
+    for one in dec_sums:
+        one.start()
+    swap.finish()
+    demb_gather = Gather(demb_own, lambda slot: demb_slots.at[slot], sems.at[0], sems.at[1])
+    demb_gather.start()
+    demb_slots[index] = demb_own[...]
+
+    def rows_of(slot):
+        return pl.ds(pl.multiple_of(slot * block_rows, block_rows), block_rows)
+
+    def first_back(step, carry):
+        demb_gather.arrive_at(step)
+        mask = visit_mask(step, count)
+        slot = index ^ mask
+        rows = rows_of(slot)
+        grad_rows = demb_slots[slot].reshape(block_rows, -1)
+        grad_out = dot_as(grad_rows, embed_full[...], 1, 1)
+
+        @pl.when(mask == 0)
+        def _():
+            dy_s[...] = grad_out
+
+        dm_s[rows, :] = grad_out.astype(low_type)
+        for first in range(0, hidden, chunk):
+            cols = slice(first, first + chunk)
+            grad_active = dot_as(dm_s[rows, :], w_down[cols, :], 1, 1)
+            du_s[rows, cols] = (grad_active * slope_s[rows, cols].astype(full_type)).astype(
+                low_type
+            )
+        return carry
+
+    lax.fori_loop(0, count, first_back, 0)
+    scatter = Scatter(parts_mlp, total, landing_mlp, sems.at[2], sems.at[3])
+    total[...] = jnp.zeros_like(total)
+
+    def second_back(step, carry):
+        mask = count - 1 - step
+        rows = rows_of(index ^ mask)
+        scatter.put(mask, dot_as(du_s[rows, :], w_up[...], 1, 1))
+        return carry
+
+    lax.fori_loop(0, count, second_back, 0)
+    for bit in range(model_bits - 1):
+        scatter.finish_bit(bit)
+
+    def store_rows(product, first):
+        high = width // data_count
+        for row in range(data_count):
+            row_packed[bit_reverse(row, data_bits), :, first : first + product.shape[1]] = (
+                product[row * high : (row + 1) * high, :].astype(low_type)
+            )
+
+    def store_cols(product, first):
+        wide = width // data_count
+        for col in range(data_count):
+            col_packed[
+                bit_reverse(col, data_bits), first : first + product.shape[0], :wide
+            ] = product[:, col * wide : (col + 1) * wide].astype(low_type)
+
+    for cut in range(2):
+        cols = slice(cut * (hidden // 2), (cut + 1) * (hidden // 2))
+        store_cols(dot_as(g_s[:, cols], dm_s[...], 0, 0), cut * (hidden // 2))
+        down_sums[cut].start()
+    for one in dec_sums[: cuts // 2]:
+        one.advance()
+    scatter.finish_bit(model_bits - 1)
+
+    normed, scale = norm_parts(mid_s[...])
+    grad_second = total[...]
+    wide_acc[0, 1:2, :] = jnp.sum(grad_second * normed, axis=0, keepdims=True)
+    grad_middle = dy_s[...] + norm_back(normed, scale, grad_second * gain_mlp[...])
+    dy_s[...] = grad_middle
+    db_own[...] = grad_middle.astype(low_type)
+    db_gather = Gather(db_own, lambda slot: db_s.at[rows_of(slot)], sems.at[4], sems.at[5])
+    db_gather.start()
+    db_s[rows_of(index), :] = db_own[...]
+    for cut in range(2):
+        cols = slice(cut * (hidden // 2), (cut + 1) * (hidden // 2))
+        store_rows(dot_as(c_s[...], du_s[:, cols], 0, 0), cut * (hidden // 2))
+        up_sums[cut].start()
+    for one in dec_sums[cuts // 2 :]:
+        one.advance()
+    offset, high, span, tiles = embed_piece
+    product = dot_as(low_s[...], demb_own[...].reshape(block_rows, -1), 0, 0)
+    for column in range(model_count):
+        for row in range(data_count):
+            spot = bit_reverse(column, model_bits) * data_count + bit_reverse(row, data_bits)
+            for tile in range(tiles):
+                lanes = min(LANES, span - tile * LANES)
+                first = column * span + tile * LANES
+                embed_packed[spot, tile * high : (tile + 1) * high, :lanes] = product[
+                    row * high : (row + 1) * high, first : first + lanes
+                ].astype(low_type)
+    embed_sum.start()
+
+    second_scatter = Scatter(parts_attn, total, landing_attn, sems.at[6], sems.at[7])
+    total[...] = jnp.zeros_like(total)
+
+    def third_back(step, carry):
+        db_gather.arrive_at(step)
+        mask = visit_mask(step, count)
+        slot = index ^ mask
+        rows = rows_of(slot)
+        do_s[...] = dot_as(w_out[...], db_s[rows, :], 1, 1)
+        for head in range(heads):
+            span = slice(head * size, (head + 1) * size)
+            key_span = slice(columns + head * size, columns + (head + 1) * size)
+            value_span = slice(2 * columns + head * size, 2 * columns + (head + 1) * size)
+            query, key, value = qkv_s[span, rows], qkv_s[key_span, rows], qkv_s[value_span, rows]
+            weights = e_s[slot * heads + head]
+            grad_full = do_s[span, :] * (inv_s[slot * heads + head] * scaling)
+            shift = jnp.sum(
+                grad_full * o_own[span, rows].astype(full_type), axis=0, keepdims=True
+            )
+            grad_low = grad_full.astype(low_type)
+            grad_probs = dot_as(value, grad_low, 0, 0)
+            grad_scores = (weights.astype(full_type) * (grad_probs - shift)).astype(low_type)
+            grad_value = dot_as(grad_low, weights, 1, 1) * (1.0 / scaling)
+            grad_query = jnp.dot(key, grad_scores, preferred_element_type=full_type)
+            grad_key = dot_as(query, grad_scores, 1, 1) * (1.0 / (scaling * LOG2E))
+            dqkv_s[span, rows] = grad_query.astype(low_type)
+            dqkv_s[key_span, rows] = grad_key.astype(low_type)
+            dqkv_s[value_span, rows] = grad_value.astype(low_type)
+        second_scatter.put(mask, dot_as(dqkv_s[:, rows], qkv_weights[...], 0, 0))
+        return carry
+
+    lax.fori_loop(0, count, third_back, 0)
+    for bit in range(model_bits - 1):
+        second_scatter.finish_bit(bit)
+    store_cols(jnp.dot(o_own[...], db_s[...], preferred_element_type=full_type), hidden)
+    out_sum.start()
+    store_rows(dot_as(a_s[...], dqkv_s[...], 0, 1), hidden)
+    qkv_sum.start()
+    second_scatter.finish_bit(model_bits - 1)
+    normed, scale = norm_parts(tokens[...].astype(full_type))
+    grad_normed = total[...]
+    wide_acc[0, 0:1, :] = jnp.sum(grad_normed * normed, axis=0, keepdims=True)
+    grad_tokens[...] = dy_s[...] + norm_back(normed, scale, grad_normed * gain_attn[...])
+    thin_acc[0] = dec_small[...]
+
+    def norm_copies(stage):
+        peer = partner(*all_stages[stage])[0]
+        return [
+            pltpu.make_async_remote_copy(
+                src_ref=acc.at[stage],
+                dst_ref=got.at[stage],
+                send_sem=norm_sems.at[0, kind, stage],
+                recv_sem=norm_sems.at[1, kind, stage],
+                device_id=peer,
+                device_id_type=MESH,
+            )
+            for kind, (acc, got) in enumerate(((wide_acc, wide_got), (thin_acc, thin_got)))
+        ]
+
+    everything = down_sums + up_sums + [out_sum, qkv_sum] + dec_sums + [embed_sum]
+    for stage in range(len(all_stages)):
+        copies = norm_copies(stage)
+        for copy in copies:
+            copy.start()
+        for one in everything:
+            one.advance()
+        for copy in copies:
+            copy.wait()
+        wide_acc[stage + 1] = wide_acc[stage] + wide_got[stage]
+        thin_acc[stage + 1] = thin_acc[stage] + thin_got[stage]
+    for one in everything:
+        while not one.done():
+            one.advance()
+    norm_wide[...] = wide_acc[len(all_stages)]
+    norm_thin[...] = thin_acc[len(all_stages)]
+    for one in (demb_gather, scatter, db_gather, second_scatter):
+        one.drain()
+
+    rows_out, cols_out = row_bufs[-1], col_bufs[-1]
+    g_up[...] = rows_out[0, :, :hidden].astype(full_type)
+    for position, out in enumerate((g_query, g_key, g_value)):
+        first = hidden + position * columns
+        out[...] = rows_out[0, :, first : first + columns].astype(full_type)
+    wide = width // data_count
+    g_down[...] = cols_out[0, :hidden, :wide].astype(full_type)
+    g_out[...] = cols_out[0, hidden : hidden + columns, :wide].astype(full_type)
+    unpack([g_embed], [embed_piece], embed_bufs[-1])
+    unpack(dec_outs, dec_pieces_list, dec_bufs[-1])
+
+
+def unpack(outs, pieces, source):
+    for out, (offset, rows, width, tiles) in zip(outs, pieces):
+        for tile in range(tiles):
+            lanes = min(LANES, width - tile * LANES)
+            block = source[0, offset + tile * rows : offset + (tile + 1) * rows, :lanes]
+            out[:, tile * LANES : tile * LANES + lanes] = block.astype(full_type)
+
+
+def encode_back(grad_arrived, tokens, weights, saved, embed_proj, dec_packed, dec_small, dec_shapes):
+    gain_attn, w_query, w_key, w_value, w_out, gain_mlp, w_up, w_down = weights
+    data_count, model_count = lax.axis_size("dp"), lax.axis_size("mp")
+    data_bits, model_bits = log2_of(data_count), log2_of(model_count)
+    images, visible, width = tokens.shape
+    rows = images * visible
+    every = rows * model_count
+    heads = HE // model_count
+    columns, hidden = w_query.shape[1], w_up.shape[1]
+    out_width = embed_proj.shape[1] * model_count
+    pieces, height = dec_pieces(data_count, model_count, dec_shapes)
+    embed_pieces, embed_height = dec_pieces(data_count, model_count, [(width, out_width)])
+    high, wide = width // data_count, width // data_count
+    wide_pad = -(-wide // LANES) * LANES
+    devices = data_count * model_count
+    stages = data_bits + model_bits
+    dec_cuts = 4
+    plan = (images, visible, heads, pieces, embed_pieces[0])
+
+    def kernel(*refs):
+        encoder_back_kernel(plan, *refs)
+
+    vmem = pl.BlockSpec(memory_space=pltpu.VMEM)
+    outs = [
+        (rows, width),
+        (high, columns),
+        (high, columns),
+        (high, columns),
+        (high, hidden),
+        (columns, wide),
+        (hidden, wide),
+        (embed_pieces[0][1], embed_pieces[0][2]),
+        (2, width),
+        dec_small.shape,
+    ] + [(piece[1], piece[2]) for piece in pieces]
+    row_shape = (high, hidden + 3 * columns)
+    col_shape = (hidden + columns, wide_pad)
+    scratch = [
+        pltpu.VMEM((images, visible, out_width), low_type),
+        pltpu.VMEM((model_count, images, visible, out_width), low_type),
+        pltpu.VMEM((every, width), low_type),
+        pltpu.VMEM((every, hidden), low_type),
+        pltpu.VMEM((rows, width), low_type),
+        pltpu.VMEM((every, width), low_type),
+        pltpu.VMEM((3 * columns, every), low_type),
+        pltpu.VMEM((rows, width), full_type),
+        pltpu.VMEM((model_count, rows, width), low_type),
+        pltpu.VMEM((model_count, rows, width), low_type),
+        pltpu.VMEM((model_count, rows, width), low_type),
+        pltpu.VMEM((model_count, rows, width), low_type),
+        pltpu.VMEM((rows, width), full_type),
+        pltpu.VMEM((columns, rows), full_type),
+        pltpu.SemaphoreType.DMA((8, model_count)),
+        pltpu.SemaphoreType.DMA((2, images)),
+        pltpu.VMEM((data_count,) + row_shape, low_type),
+        pltpu.VMEM((data_count,) + col_shape, low_type),
+        pltpu.VMEM((devices, embed_height, LANES), low_type),
+    ]
+    scratch += [pltpu.VMEM((data_count >> (bit + 1),) + row_shape, low_type) for bit in range(data_bits)]
+    scratch += [pltpu.VMEM((data_count >> (bit + 1),) + col_shape, low_type) for bit in range(data_bits)]
+    scratch += [pltpu.VMEM((devices >> (bit + 1), height, LANES), low_type) for bit in range(stages)]
+    scratch += [
+        pltpu.VMEM((devices >> (bit + 1), embed_height, LANES), low_type) for bit in range(stages)
+    ]
+    for shape in ((2, width), dec_small.shape):
+        scratch += [
+            pltpu.VMEM((stages + 1,) + shape, full_type),
+            pltpu.VMEM((stages,) + shape, full_type),
+        ]
+    scratch += [
+        pltpu.SemaphoreType.DMA((2, 3, data_bits)),
+        pltpu.SemaphoreType.DMA((2, 3, data_bits)),
+        pltpu.SemaphoreType.DMA((2, dec_cuts, stages)),
+        pltpu.SemaphoreType.DMA((2, 1, stages)),
+        pltpu.SemaphoreType.DMA((2, 2, stages)),
+    ]
+    return pl.pallas_call(
+        kernel,
+        out_shape=[jax.ShapeDtypeStruct(shape, full_type) for shape in outs],
+        in_specs=[vmem] * 21,
+        out_specs=[vmem] * len(outs),
+        scratch_shapes=scratch,
+        compiler_params=pltpu.CompilerParams(
+            collective_id=2, has_side_effects=True, vmem_limit_bytes=62 * 2**20
+        ),
+    )(
+        grad_arrived,
+        tokens.reshape(rows, width),
+        gain_attn.reshape(1, -1),
+        w_out,
+        gain_mlp.reshape(1, -1),
+        w_up,
+        w_down,
+        *saved,
+        dec_packed,
+        dec_small,
+    )
 
 
 def layer_norm(values, scale_gain):
@@ -277,7 +1473,7 @@
     )
 
 
-def per_device(
+def per_device_plain(
     tokens,
     lengths,
     grid_order,
@@ -461,6 +1657,133 @@
         dec_final[4],
         dec_final[5],
         dec_final[6],
+    )
+
+
+VMEM_BUDGET = 56 * 2**20
+
+
+def kernel_bytes(tokens, enc_up, enc_query, dec_up, pred_proj):
+    data_count, model_count = lax.axis_size("dp"), lax.axis_size("mp")
+    images, visible, width = tokens.shape
+    every = images * visible * model_count
+    hidden, columns = enc_up.shape[1], enc_query.shape[1]
+    out_width, wide = dec_up.shape[0], max(width // data_count, LANES)
+    shapes = [(out_width, out_width)] * 4
+    shapes += [dec_up.shape, dec_up.shape[::-1], pred_proj.shape, (width, out_width)]
+    height = dec_pieces(data_count, model_count, shapes)[1]
+    rows = 8 * every * width + 3 * every * hidden
+    sums = width * (hidden + 3 * columns) + data_count * (hidden + columns) * wide
+    sums = 2 * (sums + data_count * model_count * height * LANES)
+    return 2 * (rows + sums + 2 * width * hidden + 4 * width * columns)
+
+
+def per_device(
+    tokens,
+    lengths,
+    grid_order,
+    grid_keep,
+    ground_dist,
+    enc_norm,
+    enc_query,
+    enc_key,
+    enc_value,
+    enc_proj,
+    enc_norm2,
+    enc_up,
+    enc_down,
+    embed_proj,
+    mask_token,
+    dec_norm,
+    dec_query,
+    dec_key,
+    dec_value,
+    dec_proj,
+    dec_norm2,
+    dec_up,
+    dec_down,
+    pred_proj,
+    cotangent,
+):
+    if kernel_bytes(tokens, enc_up, enc_query, dec_up, pred_proj) > VMEM_BUDGET:
+        return per_device_plain(
+            tokens,
+            lengths,
+            grid_order,
+            grid_keep,
+            ground_dist,
+            enc_norm,
+            enc_query,
+            enc_key,
+            enc_value,
+            enc_proj,
+            enc_norm2,
+            enc_up,
+            enc_down,
+            embed_proj,
+            mask_token,
+            dec_norm,
+            dec_query,
+            dec_key,
+            dec_value,
+            dec_proj,
+            dec_norm2,
+            dec_up,
+            dec_down,
+            pred_proj,
+            cotangent,
+        )
+    enc_weights = (enc_norm, enc_query, enc_key, enc_value, enc_proj, enc_norm2, enc_up, enc_down)
+    dec_weights = (dec_norm, dec_query, dec_key, dec_value, dec_proj, dec_norm2, dec_up, dec_down)
+    arrived, *saved = encode(tokens, lengths, enc_weights, embed_proj)
+    decoded, dec_packed, grad_arrived, dec_small = decode(
+        arrived, grid_order, grid_keep, ground_dist, dec_weights, mask_token, pred_proj, cotangent
+    )
+    matrices = [dec_query, dec_key, dec_value, dec_proj, dec_up, dec_down, pred_proj]
+    (
+        grad_tokens,
+        g_query,
+        g_key,
+        g_value,
+        g_up,
+        g_out,
+        g_down,
+        g_embed,
+        norm_wide,
+        norm_thin,
+        *dec_grads,
+    ) = encode_back(
+        grad_arrived,
+        tokens,
+        enc_weights,
+        saved,
+        embed_proj,
+        dec_packed,
+        dec_small,
+        [matrix.shape for matrix in matrices],
+    )
+    return (
+        decoded,
+        grad_tokens.reshape(tokens.shape),
+        norm_wide[0],
+        g_query,
+        g_key,
+        g_value,
+        g_out,
+        norm_wide[1],
+        g_up,
+        g_down,
+        g_embed,
+        norm_thin[2],
+        norm_thin[0],
+        dec_grads[0],
+        dec_grads[1],
+        dec_grads[2],
+        dec_grads[3],
+        norm_thin[1],
+        dec_grads[4],
+        dec_grads[5],
+        dec_grads[6],
     )
 
 

time: 1840 us -> 290 us (0.16)
  waiting for transfers between devices: 1490 us -> 0 us
  Pallas kernels: 0 us -> 270 us
  matrix products: 148 us -> 0 us
  blocking collectives: 56.6 us -> 0 us
  other arithmetic: 55.8 us -> 0 us
  local copies, waits for them, and re-layouts: 44.7 us -> 18.9 us
    reduce_scatter x17 -> x0, waiting for transfers between devices: 1290 us -> none  [the longest x1 140 us: per_device(): lax.psum_scatter(owner_blocks(dec_list[5], data_count, model_count), ('dp...]
    pallas_call x0 -> x3, Pallas kernels: none -> 270 us  [the longest x1 165 us: encode_back(): pl.pallas_call(kernel, out_shape=[jax.ShapeDtypeStruct(shape, full_type)...]
    dot_general x56 -> x0, matrix products: 148 us -> none  [the longest x14 31.7 us: matmul(): product = jnp.dot(flat_rows, right_side, preferred_element_type=full_type)]
    unnamed x26 -> x0, waiting for transfers between devices: 127 us -> none
    all_gather x5 -> x0, waiting for transfers between devices: 72.5 us -> none  [spread_rows(): return lax.all_gather(values, 'mp', axis=0, tiled=True)]
    psum x1 -> x0, blocking collectives: 39.7 us -> none  [per_device(): lax.psum((enc_grads[0], enc_grads[5], dec_grads[0], dec_grads[5], grad_ma...]
    convert_element_type x18 -> x0, other arithmetic: 35.7 us -> none  [the longest x2 16.4 us: block_forward(): active = exact_gelu(pre_act).astype(low_type)]
  transfers between devices with their start and end apart: 26 -> 0, of which waited for: 25 -> 0; matrix products, arithmetic and copies ran while one was open for 6% -> 0% of each run, Pallas kernels for 0% -> 0%
where the time goes in v2:
time: 290 us; the launch traced here: 289 us
  Pallas kernels  270 us (93%)
  local copies, waits for them, and re-layouts  18.9 us (7%)
    pallas_call x1, Pallas kernels, encode_back(): pl.pallas_call(kernel, out_shape=[jax.ShapeDtypeStruct(shape, full_type)...  165 us
    pallas_call x1, Pallas kernels, encode(): pl.pallas_call(kernel, out_shape=[jax.ShapeDtypeStruct(shape, kind) for s...  59.4 us
    pallas_call x1, Pallas kernels, decode(): pl.pallas_call(kernel, out_shape=[jax.ShapeDtypeStruct((images, length, p...  45.2 us
    unnamed x39, local copies, waits for them, and re-layouts  14.9 us

profile of v2, /device:TPU:0, one launch (start us, length us, event | category | flops | bytes accessed | tf_op | source)
XLA Modules:
  0.0 289.2 jit_solution(6710762716715566604)
XLA Ops:
  0.7 59.4 %shard_map.400 = (bf16[2,64,512]{2,1,0:T(8,128)(2,1)}, bf16[512,1024]{1,0:T(8,128)(2,1)}, bf16[768,512]{1,0:T(8,128)(2,1)}, bf16[16,128,128]{2,1,0:T(8,128)(2,1)...) custom-call(s32[8]{0:T(128)} %refs_0_.1, ...), custom_call_target="tpu_custom_call" | custom-call | tf_op jit(solution)/shard_map/pallas_call | solution.py:761
  60.1 0.6 broadcast_in_dim.6.refs_1_
  60.7 0.6 broadcast_in_dim.7.refs_2_
  61.3 45.2 %shard_map.401 = (f32[2,256,768]{2,1,0:T(8,128)}, bf16[32,896,128]{2,1,0:T(8,128)(2,1)}, bf16[2,64,512]{2,1,0:T(8,128)(2,1)}, f32[3,512]{1,0:T(4,128)}) custom-call(bf16[2,64,512]{2,1,0:T(8,128)(2,1)} %get-tuple-element.55.refs_0_, s32[2,1,256]{2,1,0:T(1,128)} %broadcast_in_dim.6.refs_1_, s32[2,1,256]{2,1,0:T(1,128)} %broadcast_in_dim.7.refs_2_, f32[2]{0:T(128)} %refs_3_.4, ...), custom_call_target="tpu_custom_call" | custom-call | tf_op jit(solution)/shard_map/pallas_call | solution.py:334
  106.5 164.9 %shard_map.402 = (f32[128,1024]{1,0:T(8,128)}, f32[128,256]{1,0:T(8,128)}, f32[128,256]{1,0:T(8,128)}, f32[128,256]{1,0:T(8,128)}, f32[128,1024]{1,0:T(8,128)}, ...) custom-call(bf16[2,64,512]{2,1,0:T(8,128)(2,1)} %get-tuple-element.5, ...), custom_call_target="tpu_custom_call" | custom-call | tf_op jit(solution)/shard_map/pallas_call | solution.py:1191
  271.5 1.4 fusion.1
  272.9 1.4 fusion
  274.3 1.9 copy.61
  276.3 1.6 copy.62
  277.9 1.6 copy.63
  279.4 1.6 copy.64
  281.0 1.6 copy.65
  282.6 0.8 copy.66
  283.4 0.8 copy.67
  284.2 0.0 copy-done.5
  284.2 0.6 copy.68
  284.8 0.6 copy.69
  285.4 0.6 copy.70
  286.0 0.0 copy-done.7
  286.0 0.6 copy.71
  286.6 0.6 copy.72
  287.3 0.7 copy.73
  287.9 0.7 copy.74
  288.6 0.6 copy.75
  (22 shorter events, 0.0 us)
Async XLA Ops:
  0.7 59.5 %copy-start.10 = (s32[2,256]{1,0:T(2,128)S(1)}, s32[2,256]{1,0:T(2,128)}, u32[]{:S(2)}) copy-start(s32[2,256]{1,0:T(2,128)} %param.27) | copy-start | bytes 6148
  0.7 60.0 %copy-start.11 = (s32[2,256]{1,0:T(2,128)S(1)}, s32[2,256]{1,0:T(2,128)}, u32[]{:S(2)}) copy-start(s32[2,256]{1,0:T(2,128)} %param.28) | copy-start | bytes 6148
  271.5 11.1 %copy-start.1 = (f32[128,1024]{1,0:T(8,128)S(1)}, f32[128,1024]{1,0:T(8,128)}, u32[]{:S(2)}) copy-start(f32[128,1024]{1,0:T(8,128)} %get-tuple-element.123) | copy-start | bytes 1572868
  271.5 11.9 %copy-start = (f32[1024,128]{1,0:T(8,128)S(1)}, f32[1024,128]{1,0:T(8,128)}, u32[]{:S(2)}) copy-start(f32[1024,128]{1,0:T(8,128)} %get-tuple-element.124) | copy-start | bytes 1572868
  274.3 9.9 %copy-start.5 = (f32[128,128]{1,0:T(8,128)S(1)}, f32[128,128]{1,0:T(8,128)}, u32[]{:S(2)}) copy-start(f32[128,128]{1,0:T(8,128)} %get-tuple-element.125) | copy-start | bytes 196612
  274.3 10.5 %copy-start.9 = (f32[64,128]{1,0:T(8,128)S(1)}, f32[64,128]{1,0:T(8,128)}, u32[]{:S(2)}) copy-start(f32[64,128]{1,0:T(8,128)} %get-tuple-element.128) | copy-start | bytes 98308
  274.3 11.1 %copy-start.8 = (f32[64,128]{1,0:T(8,128)S(1)}, f32[64,128]{1,0:T(8,128)}, u32[]{:S(2)}) copy-start(f32[64,128]{1,0:T(8,128)} %get-tuple-element.129) | copy-start | bytes 98308
  274.3 11.7 %copy-start.7 = (f32[64,128]{1,0:T(8,128)S(1)}, f32[64,128]{1,0:T(8,128)}, u32[]{:S(2)}) copy-start(f32[64,128]{1,0:T(8,128)} %get-tuple-element.130) | copy-start | bytes 98308
  274.3 12.4 %copy-start.6 = (f32[64,128]{1,0:T(8,128)S(1)}, f32[64,128]{1,0:T(8,128)}, u32[]{:S(2)}) copy-start(f32[64,128]{1,0:T(8,128)} %get-tuple-element.131) | copy-start | bytes 98308
  274.3 13.0 %copy-start.3 = (f32[64,512]{1,0:T(8,128)S(1)}, f32[64,512]{1,0:T(8,128)}, u32[]{:S(2)}) copy-start(f32[64,512]{1,0:T(8,128)} %get-tuple-element.133) | copy-start | bytes 393220
  276.3 11.7 %copy-start.2 = (f32[256,128]{1,0:T(8,128)S(1)}, f32[256,128]{1,0:T(8,128)}, u32[]{:S(2)}) copy-start(f32[256,128]{1,0:T(8,128)} %get-tuple-element.134) | copy-start | bytes 393220
  276.3 12.3 %copy-start.4 = (f32[64,192]{1,0:T(8,128)S(1)}, f32[64,192]{1,0:T(8,128)}, u32[]{:S(2)}) copy-start(f32[64,192]{1,0:T(8,128)} %get-tuple-element.135) | copy-start | bytes 147460

commit v3 on v2

--- a/solution.py
+++ b/solution.py
@@ -29,10 +29,10 @@
     return bits
 
 
-def bit_reverse(index, bits):
+def spot_of(data, model, stages):
     out = 0
-    for position in range(bits):
-        out = out * 2 + ((index >> position) & 1)
+    for axis, bit in stages:
+        out = out * 2 + (((data if axis == "dp" else model) >> bit) & 1)
     return out
 
 
@@ -55,15 +55,14 @@
     def __init__(self, stages, buffers, window, send_sems, recv_sems):
         self.stages, self.buffers, self.window = stages, buffers, window
         self.send_sems, self.recv_sems = send_sems, recv_sems
-        self.copies = [None] * len(stages)
 
     def view(self, index, start, size):
         return self.buffers[index].at[(pl.ds(start, size),) + self.window]
 
-    def start(self, index):
+    def copy(self, index):
         peer, mine = partner(*self.stages[index])
         half = self.buffers[index].shape[0] // 2
-        copy = pltpu.make_async_remote_copy(
+        return pltpu.make_async_remote_copy(
             src_ref=self.view(index, (1 - mine) * half, half),
             dst_ref=self.view(index + 1, 0, half),
             send_sem=self.send_sems.at[index],
@@ -71,11 +70,12 @@
             device_id=peer,
             device_id_type=MESH,
         )
-        copy.start()
-        self.copies[index] = copy
+
+    def start(self, index):
+        self.copy(index).start()
 
     def finish(self, index):
-        self.copies[index].wait()
+        self.copy(index).wait()
         peer, mine = partner(*self.stages[index])
         half = self.buffers[index].shape[0] // 2
 
@@ -125,260 +125,6 @@
     return values * below, below + values * density
 
 
-def decoder_kernel(images, heads, side, pieces, data_count, model_count, *refs):
-    (
-        arrived,
-        order_ref,
-        keep_ref,
-        dist_ref,
-        gain_attn,
-        w_query,
-        w_key,
-        w_value,
-        w_out,
-        gain_mlp,
-        w_up,
-        w_down,
-        w_pred,
-        mask_token,
-        cotangent,
-        decoded,
-        packed,
-        grad_arrived,
-        small,
-        xs,
-        qkv_weights,
-        a_s,
-        qkv_s,
-        e_s,
-        inv_s,
-        o_s,
-        mid_s,
-        c_s,
-        g_s,
-        du_s,
-        low_s,
-        dy_s,
-        dm_s,
-        db_s,
-        do_s,
-    ) = refs
-    length = side * side
-    visible = arrived.shape[1]
-    width = w_query.shape[0]
-    hidden = w_up.shape[1]
-    size = width // heads
-    scaling = float(size) ** -0.5
-    chunk = 512
-    place = lax.broadcasted_iota(jnp.int32, (length, visible), 0)
-    turn = lax.broadcasted_iota(jnp.int32, (length, visible), 1)
-
-    def picks(image):
-        order = order_ref[image, :, :visible]
-        count = jnp.sum(keep_ref[image], axis=1, keepdims=True)
-        return jnp.where((order == place) & (turn < count), 1.0, 0.0)
-
-    def rows_of(image):
-        return pl.ds(pl.multiple_of(image * length, length), length)
-
-    for position, weight in enumerate((w_query, w_key, w_value)):
-        qkv_weights[position * width : (position + 1) * width, :] = weight[...].T
-    small[...] = jnp.zeros_like(small)
-
-    def first_part(image, carry):
-        rows = rows_of(image)
-        pick = picks(image)
-        hidden_rows = 1.0 - jnp.sum(pick, axis=1, keepdims=True)
-        quarter = width // 4
-        lane = lax.broadcasted_iota(jnp.int32, (side, quarter), 1).astype(full_type)
-        line = lax.broadcasted_iota(jnp.int32, (side, quarter), 0).astype(full_type)
-        angle = dist_ref[image] * line * jnp.exp(lane * (-math.log(10000.0) / quarter))
-        table = jnp.concatenate([jnp.sin(angle), jnp.cos(angle)], axis=1)
-        by_row = jnp.broadcast_to(table[:, None, :], (side, side, 2 * quarter))
-        by_col = jnp.broadcast_to(table[None, :, :], (side, side, 2 * quarter))
-        codes = jnp.concatenate(
-            [by_row.reshape(length, 2 * quarter), by_col.reshape(length, 2 * quarter)], axis=1
-        )
-        start = jnp.dot(pick.astype(low_type), arrived[image], preferred_element_type=full_type)
-        start = start + hidden_rows * mask_token[...] + codes
-        xs[...] = start
-        normed, scale = norm_parts(start)
-        a_s[rows, :] = (normed * gain_attn[...]).astype(low_type)
-        for position in range(3):
-            part = dot_as(
-                qkv_weights[position * width : (position + 1) * width, :], a_s[rows, :], 1, 1
-            )
-            if position == 0:
-                part = part * (scaling * LOG2E)
-            qkv_s[position * width : (position + 1) * width, rows] = part.astype(low_type)
-
-        def one_head(head, inner):
-            span = pl.multiple_of(head * size, size)
-            query = qkv_s[pl.ds(span, size), rows]
-            key = qkv_s[pl.ds(width + span, size), rows]
-            value = qkv_s[pl.ds(2 * width + span, size), rows]
-            scores = dot_as(key, query, 0, 0)
-            weights = jnp.exp2(scores - jnp.max(scores, axis=0, keepdims=True))
-            inverse = 1.0 / jnp.sum(weights, axis=0, keepdims=True)
-            weights = weights.astype(low_type)
-            e_s[head] = weights
-            inv_s[head] = inverse
-            mixed = jnp.dot(value, weights, preferred_element_type=full_type)
-            o_s[pl.ds(span, size), rows] = (mixed * inverse).astype(low_type)
-            return inner
-
-        lax.fori_loop(0, heads, one_head, 0, unroll=4)
-
-        middle = start + dot_as(o_s[:, rows], w_out[...], 0, 0)
-        mid_s[...] = middle
-        normed, scale = norm_parts(middle)
-        c_s[rows, :] = (normed * gain_mlp[...]).astype(low_type)
-        for position in range(hidden // chunk):
-            cols = slice(position * chunk, (position + 1) * chunk)
-            pre = jnp.dot(c_s[rows, :], w_up[:, cols], preferred_element_type=full_type)
-            active, slope = gelu_pair(pre)
-            g_s[rows, cols] = active.astype(low_type)
-            du_s[rows, cols] = slope.astype(low_type)
-        outputs = middle + jnp.dot(g_s[rows, :], w_down[...], preferred_element_type=full_type)
-        low_s[rows, :] = outputs.astype(low_type)
-        decoded[image] = jnp.dot(low_s[rows, :], w_pred[...], preferred_element_type=full_type)
-
-        grad_out = dot_as(cotangent[image], w_pred[...], 1, 1)
-        dm_s[rows, :] = grad_out.astype(low_type)
-        for position in range(hidden // chunk):
-            cols = slice(position * chunk, (position + 1) * chunk)
-            grad_active = dot_as(dm_s[rows, :], w_down[cols, :], 1, 1)
-            du_s[rows, cols] = (grad_active * du_s[rows, cols].astype(full_type)).astype(low_type)
-        grad_second = dot_as(du_s[rows, :], w_up[...], 1, 1)
-        normed, scale = norm_parts(mid_s[...])
-        small[1:2, :] += jnp.sum(grad_second * normed, axis=0, keepdims=True)
-        grad_middle = grad_out + norm_back(normed, scale, grad_second * gain_mlp[...])
-        dy_s[...] = grad_middle
-        db_s[rows, :] = grad_middle.astype(low_type)
-        do_s[...] = dot_as(w_out[...], db_s[rows, :], 1, 1)
-
-        def back_head(head, inner):
-            span = pl.multiple_of(head * size, size)
-            query = qkv_s[pl.ds(span, size), rows]
-            key = qkv_s[pl.ds(width + span, size), rows]
-            value = qkv_s[pl.ds(2 * width + span, size), rows]
-            weights = e_s[head]
-            grad_full = do_s[pl.ds(span, size), :] * (inv_s[head] * scaling)
-            mixed = o_s[pl.ds(span, size), rows].astype(full_type)
-            shift = jnp.sum(grad_full * mixed, axis=0, keepdims=True)
-            grad_low = grad_full.astype(low_type)
-            grad_probs = dot_as(value, grad_low, 0, 0)
-            grad_scores = (weights.astype(full_type) * (grad_probs - shift)).astype(low_type)
-            grad_value = dot_as(grad_low, weights, 1, 1) * (1.0 / scaling)
-            grad_query = jnp.dot(key, grad_scores, preferred_element_type=full_type)
-            grad_key = dot_as(query, grad_scores, 1, 1) * (1.0 / (scaling * LOG2E))
-            qkv_s[pl.ds(span, size), rows] = grad_query.astype(low_type)
-            qkv_s[pl.ds(width + span, size), rows] = grad_key.astype(low_type)
-            qkv_s[pl.ds(2 * width + span, size), rows] = grad_value.astype(low_type)
-            return inner
-
-        lax.fori_loop(0, heads, back_head, 0, unroll=4)
-
-        grad_normed = dot_as(qkv_s[:, rows], qkv_weights[...], 0, 0)
-        normed, scale = norm_parts(xs[...])
-        small[0:1, :] += jnp.sum(grad_normed * normed, axis=0, keepdims=True)
-        grad_start = dy_s[...] + norm_back(normed, scale, grad_normed * gain_attn[...])
-        small[2:3, :] += jnp.sum(hidden_rows * grad_start, axis=0, keepdims=True)
-        grad_arrived[image] = dot_as(
-            pick.astype(low_type), grad_start.astype(low_type), 0, 0
-        ).astype(low_type)
-        return carry
-
-    lax.fori_loop(0, images, first_part, 0)
-
-    data_bits, model_bits = log2_of(data_count), log2_of(model_count)
-
-    def store(piece, product):
-        offset, height, span, tiles = piece
-        for column in range(model_count):
-            for tile in range(tiles):
-                lanes = min(LANES, span - tile * LANES)
-                first = column * span + tile * LANES
-                block = product[:, first : first + lanes].astype(low_type)
-                for row in range(data_count):
-                    spot = bit_reverse(column, model_bits) * data_count
-                    spot = spot + bit_reverse(row, data_bits)
-                    packed[
-                        spot, offset + tile * height : offset + (tile + 1) * height, :lanes
-                    ] = block[row * height : (row + 1) * height, :]
-
-    for position in range(3):
-        grads = qkv_s[position * width : (position + 1) * width, :]
-        store(pieces[position], dot_as(a_s[...], grads, 0, 1))
-    store(pieces[3], jnp.dot(o_s[...], db_s[...], preferred_element_type=full_type))
-    store(pieces[4], dot_as(c_s[...], du_s[...], 0, 0))
-    store(pieces[5], dot_as(g_s[...], dm_s[...], 0, 0))
-    store(pieces[6], dot_as(low_s[...], cotangent[...].reshape(-1, cotangent.shape[2]), 0, 0))
-
-
-def decode(
-    arrived, grid_order, grid_keep, ground_dist, weights, mask_token, pred_proj, cotangent
-):
-    gain_attn, w_query, w_key, w_value, w_out, gain_mlp, w_up, w_down = weights
-    data_count, model_count = lax.axis_size("dp"), lax.axis_size("mp")
-    images, length, pixels = cotangent.shape
-    width, hidden = w_up.shape
-    rows = images * length
-    matrices = [w_query, w_key, w_value, w_out, w_up, w_down, pred_proj]
-    pieces, height = dec_pieces(data_count, model_count, [m.shape for m in matrices])
-
-    def kernel(*refs):
-        decoder_kernel(images, HD, SIDE, pieces, data_count, model_count, *refs)
-
-    vmem = pl.BlockSpec(memory_space=pltpu.VMEM)
-    return pl.pallas_call(
-        kernel,
-        out_shape=[
-            jax.ShapeDtypeStruct((images, length, pixels), full_type),
-            jax.ShapeDtypeStruct((data_count * model_count, height, LANES), low_type),
-            jax.ShapeDtypeStruct(arrived.shape, low_type),
-            jax.ShapeDtypeStruct((3, width), full_type),
-        ],
-        in_specs=[vmem] * 3 + [pl.BlockSpec(memory_space=pltpu.SMEM)] + [vmem] * 11,
-        out_specs=[vmem] * 4,
-        scratch_shapes=[
-            pltpu.VMEM((length, width), full_type),
-            pltpu.VMEM((3 * width, width), low_type),
-            pltpu.VMEM((rows, width), low_type),
-            pltpu.VMEM((3 * width, rows), low_type),
-            pltpu.VMEM((HD, length, length), low_type),
-            pltpu.VMEM((HD, 1, length), full_type),
-            pltpu.VMEM((width, rows), low_type),
-            pltpu.VMEM((length, width), full_type),
-            pltpu.VMEM((rows, width), low_type),
-            pltpu.VMEM((rows, hidden), low_type),
-            pltpu.VMEM((rows, hidden), low_type),
-            pltpu.VMEM((rows, width), low_type),
-            pltpu.VMEM((length, width), full_type),
-            pltpu.VMEM((rows, width), low_type),
-            pltpu.VMEM((rows, width), low_type),
-            pltpu.VMEM((width, length), full_type),
-        ],
-        compiler_params=pltpu.CompilerParams(vmem_limit_bytes=60 * 2**20),
-    )(
-        arrived,
-        grid_order[:, None, :],
-        grid_keep[:, None, :],
-        ground_dist,
-        gain_attn.reshape(1, -1),
-        w_query,
-        w_key,
-        w_value,
-        w_out,
-        gain_mlp.reshape(1, -1),
-        w_up,
-        w_down,
-        pred_proj,
-        mask_token.reshape(1, -1),
-        cotangent,
-    )
-
-
 def low_bit(mask):
     return (mask & -mask).bit_length() - 1
 
@@ -406,7 +152,7 @@
         carried = mask ^ (1 << bit)
         place = self.slot_view(self.index ^ carried)
         return pltpu.make_async_remote_copy(
-            src_ref=self.own if carried == 0 else place,
+            src_ref=self.own if carried == 0 and self.own is not None else place,
             dst_ref=place,
             send_sem=self.send_sems.at[mask],
             recv_sem=self.recv_sems.at[mask],
@@ -452,8 +198,8 @@
 
     def copy(self, mask):
         return pltpu.make_async_remote_copy(
-            src_ref=self.parts.at[self.index ^ mask],
-            dst_ref=self.landing.at[mask],
+            src_ref=self.parts.at[mask - 1],
+            dst_ref=self.landing.at[mask - 1],
             send_sem=self.send_sems.at[mask],
             recv_sem=self.recv_sems.at[mask],
             device_id=partner("mp", low_bit(mask))[0],
@@ -467,7 +213,7 @@
 
         @pl.when(mask != 0)
         def _():
-            self.parts[self.index ^ mask] = product.astype(low_type)
+            self.parts[mask - 1] = product.astype(low_type)
 
         for odd in range(1, self.count, 2):
             @pl.when(mask == odd)
@@ -481,12 +227,11 @@
             self.copy(mask).wait_recv()
             rest = mask ^ step
             if rest:
-                place = self.index ^ rest
-                self.parts[place] = self.parts[place] + self.landing[mask]
+                self.parts[rest - 1] = self.parts[rest - 1] + self.landing[mask - 1]
                 if low_bit(rest) == bit + 1:
                     self.copy(rest).start()
             else:
-                self.total[...] = self.total[...] + self.landing[mask].astype(full_type)
+                self.total[...] = self.total[...] + self.landing[mask - 1].astype(full_type)
 
     def drain(self):
         for mask in range(1, self.count):
@@ -551,6 +296,17 @@
                 ).wait()
 
 
+class Move:
+    def __init__(self, source, target, sem):
+        self.copy = pltpu.make_async_copy(source, target, sem)
+        self.copy.start()
+
+    def wait(self):
+        if self.copy is not None:
+            self.copy.wait()
+            self.copy = None
+
+
 def encoder_barrier(images, axes):
     barrier = pltpu.get_barrier_semaphore()
     count = images
@@ -570,15 +326,23 @@
         lengths,
         tokens,
         gain_attn,
+        w_query_hbm,
+        w_key_hbm,
+        w_value_hbm,
+        w_out,
+        gain_mlp,
+        w_up_hbm,
+        w_down_hbm,
+        w_embed,
+        arrived,
+        *saved_hbm,
+    ) = refs[:24]
+    (
         w_query,
         w_key,
         w_value,
-        w_out,
-        gain_mlp,
         w_up,
         w_down,
-        w_embed,
-        arrived,
         a_s,
         qkv_s,
         e_s,
@@ -591,6 +355,7 @@
         low_s,
         embed_full,
         qkv_weights,
+        move_sems,
         token_slots,
         out_full,
         o_full,
@@ -601,7 +366,7 @@
         embedded,
         sems,
         swap_sems,
-    ) = refs
+    ) = refs[24:]
     count = lax.axis_size("mp")
     index = lax.axis_index("mp")
     block_rows = images * visible
@@ -611,6 +376,26 @@
     hidden = w_up.shape[1]
     chunk = 512
 
+    loads = [
+        Move(source, target, move_sems.at[position])
+        for position, (source, target) in enumerate(
+            (
+                (w_query_hbm, w_query),
+                (w_key_hbm, w_key),
+                (w_value_hbm, w_value),
+                (w_up_hbm, w_up),
+                (w_down_hbm, w_down),
+            )
+        )
+    ]
+    saved = [a_s, qkv_s, e_s, inv_s, o_own, c_s, g_s, slope_s, mid_s, low_s, embed_full, qkv_weights]
+    stores = []
+
+    def save(*arrays):
+        for array in arrays:
+            position = [array is one for one in saved].index(True)
+            stores.append(Move(array, saved_hbm[position], move_sems.at[len(loads) + position]))
+
     encoder_barrier(images, ["mp"])
     token_gather = Gather(
         tokens, lambda slot: token_slots.at[slot], sems.at[0], sems.at[1]
@@ -636,7 +421,9 @@
     out_full[pl.ds(pl.multiple_of(index * columns, columns), columns), :] = w_out[...]
     embed_slots[index] = w_embed[...]
     for position, weight in enumerate((w_query, w_key, w_value)):
+        loads[position].wait()
         qkv_weights[position * columns : (position + 1) * columns, :] = weight[...].T
+    save(qkv_weights)
 
     def rows_of(slot):
         return pl.ds(pl.multiple_of(slot * block_rows, block_rows), block_rows)
@@ -682,6 +469,9 @@
 
     lax.fori_loop(0, count, attend, 0)
     o_gather.start()
+    save(a_s, qkv_s, e_s, inv_s, o_own)
+    for move in loads:
+        move.wait()
     o_full[pl.ds(pl.multiple_of(index * columns, columns), columns), :] = o_own[...]
     out_gather.arrive_all()
     o_gather.arrive_all()
@@ -712,6 +502,7 @@
         return carry
 
     lax.fori_loop(0, count, expand, 0)
+    save(c_s, g_s, slope_s, mid_s)
     bits = log2_of(count)
     for bit in range(bits):
         if bit == bits - 1:
@@ -724,8 +515,11 @@
     out = jnp.dot(low_s[...], embed_full[...], preferred_element_type=full_type)
     embedded[...] = out.astype(low_type).reshape(embedded.shape)
     swap.start()
+    save(embed_full, low_s)
     for one in (token_gather, out_gather, o_gather, embed_gather, scatter):
         one.drain()
+    for move in stores:
+        move.wait()
     swap.finish()
 
 
@@ -743,6 +537,7 @@
         encoder_kernel(images, visible, heads, *refs)
 
     vmem = pl.BlockSpec(memory_space=pltpu.VMEM)
+    hbm = pl.BlockSpec(memory_space=pl.ANY)
     shapes = [
         ((images, visible, out_width), low_type),
         ((every, width), low_type),
@@ -761,15 +556,29 @@
     return pl.pallas_call(
         kernel,
         out_shape=[jax.ShapeDtypeStruct(shape, kind) for shape, kind in shapes],
-        in_specs=[pl.BlockSpec(memory_space=pltpu.SMEM)] + [vmem] * 10,
-        out_specs=[vmem] * len(shapes),
+        in_specs=[pl.BlockSpec(memory_space=pltpu.SMEM)]
+        + [vmem] * 2
+        + [hbm] * 3
+        + [vmem] * 2
+        + [hbm] * 2
+        + [vmem],
+        out_specs=[vmem] + [hbm] * (len(shapes) - 1),
         scratch_shapes=[
+            pltpu.VMEM((width, columns), low_type),
+            pltpu.VMEM((width, columns), low_type),
+            pltpu.VMEM((width, columns), low_type),
+            pltpu.VMEM((width, hidden), low_type),
+            pltpu.VMEM((hidden, width), low_type),
+        ]
+        + [pltpu.VMEM(shape, kind) for shape, kind in shapes[1:]]
+        + [
+            pltpu.SemaphoreType.DMA((5 + len(shapes),)),
             pltpu.VMEM((model_count, rows, width), low_type),
             pltpu.VMEM((width, width), low_type),
             pltpu.VMEM((width, every), low_type),
             pltpu.VMEM((model_count,) + embed_proj.shape, low_type),
-            pltpu.VMEM((model_count, rows, width), low_type),
-            pltpu.VMEM((model_count, rows, width), low_type),
+            pltpu.VMEM((model_count - 1, rows, width), low_type),
+            pltpu.VMEM((model_count - 1, rows, width), low_type),
             pltpu.VMEM((rows, width), full_type),
             pltpu.VMEM((images, visible, out_width), low_type),
             pltpu.SemaphoreType.DMA((10, model_count)),
@@ -793,6 +602,17 @@
     )
 
 
+CUTS = 4
+LATE_UP = 0
+
+
+def at_step(step, when, sums):
+    @pl.when(step == when)
+    def _():
+        for one in sums:
+            one.advance()
+
+
 class Bulk:
     def __init__(self, one):
         self.one, self.stage = one, None
@@ -813,8 +633,8 @@
             self.one.start(self.stage)
 
 
-def encoder_back_kernel(plan, *refs):
-    images, visible, heads, dec_pieces_list, embed_piece = plan
+def back_kernel(plan, *refs):
+    images, visible, enc_heads, heads, side, pieces, embed_piece, scopes = plan
     refs = list(refs)
 
     def take(number):
@@ -823,55 +643,28 @@
         return head
 
     (
-        grad_arrived,
+        dist_ref,
+        arrived,
+        order_ref,
+        keep_ref,
+        dec_gain_attn,
+        dec_gain_mlp,
+        mask_token,
         tokens,
         gain_attn,
-        w_out,
         gain_mlp,
-        w_up,
-        w_down,
-        a_s,
-        qkv_s,
-        e_s,
-        inv_s,
-        o_own,
-        c_s,
-        g_s,
-        slope_s,
-        mid_s,
-        low_s,
-        embed_full,
-        qkv_weights,
-        dec_packed,
-        dec_small,
-    ) = take(21)
+    ) = take(10)
+    dec_hbm = take(8)
+    enc_hbm = take(15)
+    decoded, grad_tokens, norm_wide, norm_thin, rows_out, cols_out, dec_out, embed_out = take(8)
+    move_sems, decoded_sems = take(2)
+    grad_arrived, dec_packed, small = take(3)
+    demb_own, demb_slots, db_s, total = take(4)
+    parts_mlp, landing_mlp, parts_attn, landing_attn = take(4)
+    sems, swap_sems = take(2)
     data_count, model_count = lax.axis_size("dp"), lax.axis_size("mp")
     data_bits, model_bits = log2_of(data_count), log2_of(model_count)
-    (grad_tokens, g_query, g_key, g_value, g_up, g_out, g_down, g_embed, norm_wide, norm_thin) = (
-        take(10)
-    )
-    dec_outs = take(len(dec_pieces_list))
-    (
-        demb_own,
-        demb_slots,
-        dm_s,
-        du_s,
-        db_own,
-        db_s,
-        dqkv_s,
-        total,
-        parts_mlp,
-        landing_mlp,
-        parts_attn,
-        landing_attn,
-        dy_s,
-        do_s,
-        sems,
-        swap_sems,
-        row_packed,
-        col_packed,
-        embed_packed,
-    ) = take(19)
+    row_packed, col_packed, embed_packed = take(3)
     row_bufs = [row_packed] + take(data_bits)
     col_bufs = [col_packed] + take(data_bits)
     dec_bufs = [dec_packed] + take(data_bits + model_bits)
@@ -882,260 +675,707 @@
 
     index = lax.axis_index("mp")
     count = model_count
-    block_rows = images * visible
-    columns = w_out.shape[0]
-    size = columns // heads
-    scaling = float(size) ** -0.5
-    hidden, width = w_down.shape
+    enc_stages = [("dp", bit) for bit in range(data_bits)]
+    late_stages = enc_stages[1:] + enc_stages[:1]
+    model_stages = [("mp", bit) for bit in range(model_bits)]
+    all_stages = model_stages + enc_stages
+    crossed_stages = model_stages + late_stages
+    spread_stages = model_stages[:1] + enc_stages + model_stages[1:]
     chunk = 512
-    enc_stages = [("dp", bit) for bit in range(data_bits)]
-    all_stages = [("mp", bit) for bit in range(model_bits)] + enc_stages
-
-    encoder_barrier(images, ["mp", "dp"])
-    swap = Exchange(images, grad_arrived, demb_own, swap_sems.at[0], swap_sems.at[1])
-    swap.start()
 
     def bulk(stages, bufs, axis, first, extent, pair, cut):
         window = [slice(None), slice(None)]
         window[axis - 1] = pl.ds(first, extent)
-        return Bulk(
-            HalvingSum(stages, bufs, tuple(window), pair.at[0, cut], pair.at[1, cut])
-        )
-
-    cuts = dec_sems.shape[1]
-    height = dec_packed.shape[1] // cuts
+        return Bulk(HalvingSum(stages, bufs, tuple(window), pair.at[0, cut], pair.at[1, cut]))
+
+    dec_orders = [spread_stages] * 5 + [crossed_stages] * 2
+    dec_spans = [(pieces[0][0], pieces[4][0])]
+    for piece in pieces[4:]:
+        dec_spans.append((piece[0], piece[0] + piece[1] * piece[3]))
     dec_sums = [
-        bulk(all_stages, dec_bufs, 1, cut * height, height, dec_sems, cut) for cut in range(cuts)
+        bulk(dec_orders[3 + cut], dec_bufs, 1, first, last - first, dec_sems, cut)
+        for cut, (first, last) in enumerate(dec_spans)
     ]
-    embed_sum = bulk(all_stages, embed_bufs, 1, 0, embed_packed.shape[1], embed_sems, 0)
-    up_sums = [
-        bulk(enc_stages, row_bufs, 2, cut * (hidden // 2), hidden // 2, row_sems, cut)
-        for cut in range(2)
-    ]
-    qkv_sum = bulk(enc_stages, row_bufs, 2, hidden, 3 * columns, row_sems, 2)
-    down_sums = [
-        bulk(enc_stages, col_bufs, 1, cut * (hidden // 2), hidden // 2, col_sems, cut)
-        for cut in range(2)
-    ]
-    out_sum = bulk(enc_stages, col_bufs, 1, hidden, columns, col_sems, 2)
-
-    for one in dec_sums:
-        one.start()
-    swap.finish()
-    demb_gather = Gather(demb_own, lambda slot: demb_slots.at[slot], sems.at[0], sems.at[1])
-    demb_gather.start()
-    demb_slots[index] = demb_own[...]
-
-    def rows_of(slot):
-        return pl.ds(pl.multiple_of(slot * block_rows, block_rows), block_rows)
-
-    def first_back(step, carry):
-        demb_gather.arrive_at(step)
-        mask = visit_mask(step, count)
-        slot = index ^ mask
-        rows = rows_of(slot)
-        grad_rows = demb_slots[slot].reshape(block_rows, -1)
-        grad_out = dot_as(grad_rows, embed_full[...], 1, 1)
-
-        @pl.when(mask == 0)
-        def _():
-            dy_s[...] = grad_out
-
-        dm_s[rows, :] = grad_out.astype(low_type)
-        for first in range(0, hidden, chunk):
-            cols = slice(first, first + chunk)
-            grad_active = dot_as(dm_s[rows, :], w_down[cols, :], 1, 1)
-            du_s[rows, cols] = (grad_active * slope_s[rows, cols].astype(full_type)).astype(
-                low_type
-            )
-        return carry
-
-    lax.fori_loop(0, count, first_back, 0)
-    scatter = Scatter(parts_mlp, total, landing_mlp, sems.at[2], sems.at[3])
-    total[...] = jnp.zeros_like(total)
-
-    def second_back(step, carry):
-        mask = count - 1 - step
-        rows = rows_of(index ^ mask)
-        scatter.put(mask, dot_as(du_s[rows, :], w_up[...], 1, 1))
-        return carry
-
-    lax.fori_loop(0, count, second_back, 0)
-    for bit in range(model_bits - 1):
-        scatter.finish_bit(bit)
-
-    def store_rows(product, first):
-        high = width // data_count
-        for row in range(data_count):
-            row_packed[bit_reverse(row, data_bits), :, first : first + product.shape[1]] = (
-                product[row * high : (row + 1) * high, :].astype(low_type)
-            )
-
-    def store_cols(product, first):
-        wide = width // data_count
-        for col in range(data_count):
-            col_packed[
-                bit_reverse(col, data_bits), first : first + product.shape[0], :wide
-            ] = product[:, col * wide : (col + 1) * wide].astype(low_type)
-
-    for cut in range(2):
-        cols = slice(cut * (hidden // 2), (cut + 1) * (hidden // 2))
-        store_cols(dot_as(g_s[:, cols], dm_s[...], 0, 0), cut * (hidden // 2))
-        down_sums[cut].start()
-    for one in dec_sums[: cuts // 2]:
-        one.advance()
-    scatter.finish_bit(model_bits - 1)
-
-    normed, scale = norm_parts(mid_s[...])
-    grad_second = total[...]
-    wide_acc[0, 1:2, :] = jnp.sum(grad_second * normed, axis=0, keepdims=True)
-    grad_middle = dy_s[...] + norm_back(normed, scale, grad_second * gain_mlp[...])
-    dy_s[...] = grad_middle
-    db_own[...] = grad_middle.astype(low_type)
-    db_gather = Gather(db_own, lambda slot: db_s.at[rows_of(slot)], sems.at[4], sems.at[5])
-    db_gather.start()
-    db_s[rows_of(index), :] = db_own[...]
-    for cut in range(2):
-        cols = slice(cut * (hidden // 2), (cut + 1) * (hidden // 2))
-        store_rows(dot_as(c_s[...], du_s[:, cols], 0, 0), cut * (hidden // 2))
-        up_sums[cut].start()
-    for one in dec_sums[cuts // 2 :]:
-        one.advance()
-    offset, high, span, tiles = embed_piece
-    product = dot_as(low_s[...], demb_own[...].reshape(block_rows, -1), 0, 0)
-    for column in range(model_count):
-        for row in range(data_count):
-            spot = bit_reverse(column, model_bits) * data_count + bit_reverse(row, data_bits)
+    attn_sum, up_sum, down_sum, pred_sum = dec_sums
+
+    def store_dec(which, product):
+        offset, height, span, tiles = pieces[which]
+        for column in range(model_count):
             for tile in range(tiles):
                 lanes = min(LANES, span - tile * LANES)
                 first = column * span + tile * LANES
-                embed_packed[spot, tile * high : (tile + 1) * high, :lanes] = product[
-                    row * high : (row + 1) * high, first : first + lanes
-                ].astype(low_type)
-    embed_sum.start()
-
-    second_scatter = Scatter(parts_attn, total, landing_attn, sems.at[6], sems.at[7])
-    total[...] = jnp.zeros_like(total)
-
-    def third_back(step, carry):
-        db_gather.arrive_at(step)
-        mask = visit_mask(step, count)
-        slot = index ^ mask
-        rows = rows_of(slot)
-        do_s[...] = dot_as(w_out[...], db_s[rows, :], 1, 1)
-        for head in range(heads):
-            span = slice(head * size, (head + 1) * size)
-            key_span = slice(columns + head * size, columns + (head + 1) * size)
-            value_span = slice(2 * columns + head * size, 2 * columns + (head + 1) * size)
-            query, key, value = qkv_s[span, rows], qkv_s[key_span, rows], qkv_s[value_span, rows]
-            weights = e_s[slot * heads + head]
-            grad_full = do_s[span, :] * (inv_s[slot * heads + head] * scaling)
-            shift = jnp.sum(
-                grad_full * o_own[span, rows].astype(full_type), axis=0, keepdims=True
+                block = product[:, first : first + lanes].astype(low_type)
+                for row in range(data_count):
+                    dec_packed[
+                        spot_of(row, column, dec_orders[which]),
+                        offset + tile * height : offset + (tile + 1) * height,
+                        :lanes,
+                    ] = block[row * height : (row + 1) * height, :]
+
+    swap = Exchange(images, grad_arrived, demb_own, swap_sems.at[0], swap_sems.at[1])
+
+    def decoder(
+        w_out,
+        xs,
+        qkv_weights,
+        a_s,
+        qkv_s,
+        e_s,
+        inv_s,
+        o_s,
+        dy_s,
+        db_dec,
+        do_s,
+    ):
+        length = side * side
+        width = w_out.shape[0]
+        size = width // heads
+        scaling = float(size) ** -0.5
+        place = lax.broadcasted_iota(jnp.int32, (length, visible), 0)
+        turn = lax.broadcasted_iota(jnp.int32, (length, visible), 1)
+        out_move = Move(dec_hbm[3], w_out, move_sems.at[3])
+
+        def turned(*inputs):
+            turned_moves = [
+                Move(dec_hbm[position], one, move_sems.at[position])
+                for position, one in enumerate(inputs)
+            ]
+            encoder_barrier(images, ["mp", "dp"])
+            for position, one in enumerate(inputs):
+                turned_moves[position].wait()
+                qkv_weights[position * width : (position + 1) * width, :] = one[...].T
+
+        pl.run_scoped(turned, *scopes[3])
+
+        def picks(image):
+            order = order_ref[image, :, :visible]
+            kept = jnp.sum(keep_ref[image], axis=1, keepdims=True)
+            return jnp.where((order == place) & (turn < kept), 1.0, 0.0)
+
+        def rows_of(image):
+            if isinstance(image, int):
+                return slice(image * length, (image + 1) * length)
+            return pl.ds(pl.multiple_of(image * length, length), length)
+
+        def dense(w_up, w_down, w_pred, cotangent, mid_s, c_s, g_s, du_s, low_s, dm_s, staged):
+            hidden = w_up.shape[1]
+            second_moves = [
+                Move(source, target, move_sems.at[4 + position])
+                for position, (source, target) in enumerate(
+                    zip(dec_hbm[4:], (w_up, w_down, w_pred, cotangent))
+                )
+            ]
+            out_move.wait()
+            for move in second_moves:
+                move.wait()
+            small[...] = jnp.zeros_like(small)
+
+            def stage_copy(image):
+                return pltpu.make_async_copy(staged, decoded.at[image], decoded_sems.at[image])
+
+            def one_image(image, carry):
+                rows = rows_of(image)
+                pick = picks(image)
+                hidden_rows = 1.0 - jnp.sum(pick, axis=1, keepdims=True)
+                quarter = width // 4
+                lane = lax.broadcasted_iota(jnp.int32, (side, quarter), 1).astype(full_type)
+                line = lax.broadcasted_iota(jnp.int32, (side, quarter), 0).astype(full_type)
+                angle = dist_ref[image] * line * jnp.exp(lane * (-math.log(10000.0) / quarter))
+                table = jnp.concatenate([jnp.sin(angle), jnp.cos(angle)], axis=1)
+                by_row = jnp.broadcast_to(table[:, None, :], (side, side, 2 * quarter))
+                by_col = jnp.broadcast_to(table[None, :, :], (side, side, 2 * quarter))
+                codes = jnp.concatenate(
+                    [by_row.reshape(length, 2 * quarter), by_col.reshape(length, 2 * quarter)],
+                    axis=1,
+                )
+                start = jnp.dot(
+                    pick.astype(low_type), arrived[image], preferred_element_type=full_type
+                )
+                start = start + hidden_rows * mask_token[...] + codes
+                xs[rows, :] = start
+                normed, scale = norm_parts(start)
+                a_s[rows, :] = (normed * dec_gain_attn[...]).astype(low_type)
+                for position in range(3):
+                    span = slice(position * width, (position + 1) * width)
+                    part = dot_as(qkv_weights[span, :], a_s[rows, :], 1, 1)
+                    if position == 0:
+                        part = part * (scaling * LOG2E)
+                    qkv_s[span, rows] = part.astype(low_type)
+
+                def one_head(head, inner):
+                    span = pl.multiple_of(head * size, size)
+                    query = qkv_s[pl.ds(span, size), rows]
+                    key = qkv_s[pl.ds(width + span, size), rows]
+                    value = qkv_s[pl.ds(2 * width + span, size), rows]
+                    scores = dot_as(key, query, 0, 0)
+                    weights = jnp.exp2(scores - jnp.max(scores, axis=0, keepdims=True))
+                    inverse = 1.0 / jnp.sum(weights, axis=0, keepdims=True)
+                    weights = weights.astype(low_type)
+                    e_s[image * heads + head] = weights
+                    inv_s[image * heads + head] = inverse
+                    mixed = jnp.dot(value, weights, preferred_element_type=full_type)
+                    o_s[pl.ds(span, size), rows] = (mixed * inverse).astype(low_type)
+                    return inner
+
+                lax.fori_loop(0, heads, one_head, 0, unroll=4)
+
+                middle = start + dot_as(o_s[:, rows], w_out[...], 0, 0)
+                mid_s[...] = middle
+                normed, scale = norm_parts(middle)
+                c_s[rows, :] = (normed * dec_gain_mlp[...]).astype(low_type)
+                for first in range(0, hidden, chunk):
+                    cols = slice(first, first + chunk)
+                    pre = jnp.dot(c_s[rows, :], w_up[:, cols], preferred_element_type=full_type)
+                    active, slope = gelu_pair(pre)
+                    g_s[rows, cols] = active.astype(low_type)
+                    du_s[rows, cols] = slope.astype(low_type)
+                outputs = middle + jnp.dot(
+                    g_s[rows, :], w_down[...], preferred_element_type=full_type
+                )
+                low_s[rows, :] = outputs.astype(low_type)
+
+                @pl.when(image > 0)
+                def _():
+                    stage_copy(image - 1).wait()
+
+                staged[...] = jnp.dot(
+                    low_s[rows, :], w_pred[...], preferred_element_type=full_type
+                )
+                stage_copy(image).start()
+
+                grad_out = dot_as(cotangent[image], w_pred[...], 1, 1)
+                dm_s[rows, :] = grad_out.astype(low_type)
+                for first in range(0, hidden, chunk):
+                    cols = slice(first, first + chunk)
+                    grad_active = dot_as(dm_s[rows, :], w_down[cols, :], 1, 1)
+                    du_s[rows, cols] = (grad_active * du_s[rows, cols].astype(full_type)).astype(
+                        low_type
+                    )
+                grad_second = dot_as(du_s[rows, :], w_up[...], 1, 1)
+                normed, scale = norm_parts(mid_s[...])
+                small[1:2, :] += jnp.sum(grad_second * normed, axis=0, keepdims=True)
+                grad_middle = grad_out + norm_back(
+                    normed, scale, grad_second * dec_gain_mlp[...]
+                )
+                dy_s[rows, :] = grad_middle
+                db_dec[rows, :] = grad_middle.astype(low_type)
+                return carry
+
+            lax.fori_loop(0, images, one_image, 0)
+            all_pixels = cotangent[...].reshape(-1, cotangent.shape[2])
+            store_dec(6, dot_as(low_s[...], all_pixels, 0, 0))
+            pred_sum.start()
+            store_dec(5, dot_as(g_s[...], dm_s[...], 0, 0))
+            down_sum.start()
+            pred_sum.advance()
+            store_dec(4, dot_as(c_s[...], du_s[...], 0, 0))
+            up_sum.start()
+            down_sum.advance()
+            stage_copy(images - 1).wait()
+
+        pl.run_scoped(dense, *scopes[1])
+
+        for image in range(images):
+            rows = rows_of(image)
+            do_s[...] = dot_as(w_out[...], db_dec[rows, :], 1, 1)
+
+            def back_head(head, inner):
+                span = pl.multiple_of(head * size, size)
+                query = qkv_s[pl.ds(span, size), rows]
+                key = qkv_s[pl.ds(width + span, size), rows]
+                value = qkv_s[pl.ds(2 * width + span, size), rows]
+                weights = e_s[image * heads + head]
+                grad_full = do_s[pl.ds(span, size), :] * (inv_s[image * heads + head] * scaling)
+                mixed = o_s[pl.ds(span, size), rows].astype(full_type)
+                shift = jnp.sum(grad_full * mixed, axis=0, keepdims=True)
+                grad_low = grad_full.astype(low_type)
+                grad_probs = dot_as(value, grad_low, 0, 0)
+                grad_scores = (weights.astype(full_type) * (grad_probs - shift)).astype(low_type)
+                grad_value = dot_as(grad_low, weights, 1, 1) * (1.0 / scaling)
+                grad_query = jnp.dot(key, grad_scores, preferred_element_type=full_type)
+                grad_key = dot_as(query, grad_scores, 1, 1) * (1.0 / (scaling * LOG2E))
+                qkv_s[pl.ds(span, size), rows] = grad_query.astype(low_type)
+                qkv_s[pl.ds(width + span, size), rows] = grad_key.astype(low_type)
+                qkv_s[pl.ds(2 * width + span, size), rows] = grad_value.astype(low_type)
+                return inner
+
+            lax.fori_loop(0, heads, back_head, 0, unroll=4)
+
+            grad_normed = dot_as(qkv_s[:, rows], qkv_weights[...], 0, 0)
+            normed, scale = norm_parts(xs[rows, :])
+            small[0:1, :] += jnp.sum(grad_normed * normed, axis=0, keepdims=True)
+            grad_start = dy_s[rows, :] + norm_back(
+                normed, scale, grad_normed * dec_gain_attn[...]
             )
-            grad_low = grad_full.astype(low_type)
-            grad_probs = dot_as(value, grad_low, 0, 0)
-            grad_scores = (weights.astype(full_type) * (grad_probs - shift)).astype(low_type)
-            grad_value = dot_as(grad_low, weights, 1, 1) * (1.0 / scaling)
-            grad_query = jnp.dot(key, grad_scores, preferred_element_type=full_type)
-            grad_key = dot_as(query, grad_scores, 1, 1) * (1.0 / (scaling * LOG2E))
-            dqkv_s[span, rows] = grad_query.astype(low_type)
-            dqkv_s[key_span, rows] = grad_key.astype(low_type)
-            dqkv_s[value_span, rows] = grad_value.astype(low_type)
-        second_scatter.put(mask, dot_as(dqkv_s[:, rows], qkv_weights[...], 0, 0))
-        return carry
-
-    lax.fori_loop(0, count, third_back, 0)
-    for bit in range(model_bits - 1):
-        second_scatter.finish_bit(bit)
-    store_cols(jnp.dot(o_own[...], db_s[...], preferred_element_type=full_type), hidden)
-    out_sum.start()
-    store_rows(dot_as(a_s[...], dqkv_s[...], 0, 1), hidden)
-    qkv_sum.start()
-    second_scatter.finish_bit(model_bits - 1)
-    normed, scale = norm_parts(tokens[...].astype(full_type))
-    grad_normed = total[...]
-    wide_acc[0, 0:1, :] = jnp.sum(grad_normed * normed, axis=0, keepdims=True)
-    grad_tokens[...] = dy_s[...] + norm_back(normed, scale, grad_normed * gain_attn[...])
-    thin_acc[0] = dec_small[...]
-
-    def norm_copies(stage):
-        peer = partner(*all_stages[stage])[0]
-        return [
-            pltpu.make_async_remote_copy(
-                src_ref=acc.at[stage],
-                dst_ref=got.at[stage],
-                send_sem=norm_sems.at[0, kind, stage],
-                recv_sem=norm_sems.at[1, kind, stage],
-                device_id=peer,
-                device_id_type=MESH,
-            )
-            for kind, (acc, got) in enumerate(((wide_acc, wide_got), (thin_acc, thin_got)))
+            pick = picks(image)
+            hidden_rows = 1.0 - jnp.sum(pick, axis=1, keepdims=True)
+            small[2:3, :] += jnp.sum(hidden_rows * grad_start, axis=0, keepdims=True)
+            grad_arrived[image] = dot_as(
+                pick.astype(low_type), grad_start.astype(low_type), 0, 0
+            ).astype(low_type)
+            if image == 0:
+                up_sum.advance()
+                pred_sum.advance()
+        swap.start()
+        for position in range(3):
+            grads = qkv_s[position * width : (position + 1) * width, :]
+            store_dec(position, dot_as(a_s[...], grads, 0, 1))
+        store_dec(3, jnp.dot(o_s[...], db_dec[...], preferred_element_type=full_type))
+        attn_sum.start()
+        pred_sum.advance()
+        down_sum.advance()
+
+    pl.run_scoped(decoder, *scopes[0])
+    thin_acc[0] = small[...]
+
+    def encoder(*local):
+        local = list(local)
+        loaded = local[:15]
+        (
+            w_out,
+            w_up,
+            w_down,
+            a_s,
+            qkv_s,
+            e_s,
+            inv_s,
+            o_own,
+            c_s,
+            g_s,
+            slope_s,
+            mid_s,
+            low_s,
+            embed_full,
+            qkv_weights,
+        ) = loaded
+        dm_s, du_s, dqkv_s, dy_s, do_s = local[15:]
+        block_rows = images * visible
+        columns = w_out.shape[0]
+        size = columns // enc_heads
+        scaling = float(size) ** -0.5
+        hidden, width = w_down.shape
+        moves = {}
+        for position in (13, 2, 10, 1, 9, 11, 8, 12, 0, 4, 5, 6, 7, 14, 3):
+            moves[position] = Move(enc_hbm[position], loaded[position], move_sems.at[8 + position])
+
+        def ready(*arrays):
+            for array in arrays:
+                moves[[array is one for one in loaded].index(True)].wait()
+
+        embed_sum = bulk(spread_stages, embed_bufs, 1, 0, embed_packed.shape[1], embed_sems, 0)
+        part = hidden // CUTS
+        up_orders = [enc_stages] * (CUTS - LATE_UP) + [late_stages] * LATE_UP
+        up_sums = [
+            bulk(up_orders[cut], row_bufs, 2, cut * part, part, row_sems, cut)
+            for cut in range(CUTS)
         ]
-
-    everything = down_sums + up_sums + [out_sum, qkv_sum] + dec_sums + [embed_sum]
-    for stage in range(len(all_stages)):
-        copies = norm_copies(stage)
-        for copy in copies:
-            copy.start()
+        qkv_orders = [enc_stages, enc_stages, enc_stages]
+        qkv_sums = [
+            bulk(order, row_bufs, 2, hidden + cut * columns, columns, row_sems, CUTS + cut)
+            for cut, order in enumerate(qkv_orders)
+        ]
+        down_sums = [
+            bulk(enc_stages, col_bufs, 1, cut * part, part, col_sems, cut) for cut in range(CUTS)
+        ]
+        out_sum = bulk(late_stages, col_bufs, 1, hidden, columns, col_sems, CUTS)
+
+        swap.finish()
+        demb_gather = Gather(demb_own, lambda slot: demb_slots.at[slot], sems.at[0], sems.at[1])
+        demb_gather.start()
+        demb_slots[index] = demb_own[...]
+        ready(low_s)
+        offset, high, span, tiles = embed_piece
+        product = dot_as(low_s[...], demb_own[...].reshape(block_rows, -1), 0, 0)
+        for column in range(model_count):
+            for row in range(data_count):
+                spot = spot_of(row, column, spread_stages)
+                for tile in range(tiles):
+                    lanes = min(LANES, span - tile * LANES)
+                    first = column * span + tile * LANES
+                    embed_packed[spot, tile * high : (tile + 1) * high, :lanes] = product[
+                        row * high : (row + 1) * high, first : first + lanes
+                    ].astype(low_type)
+        embed_sum.start()
+        attn_sum.advance()
+        up_sum.advance()
+        pred_sum.advance()
+        ready(embed_full, w_down, slope_s)
+
+        def rows_of(slot):
+            return pl.ds(pl.multiple_of(slot * block_rows, block_rows), block_rows)
+
+        def first_back(step, carry):
+            demb_gather.arrive_at(step)
+            at_step(step, 2, [embed_sum, down_sum])
+            mask = visit_mask(step, count)
+            slot = index ^ mask
+            rows = rows_of(slot)
+            grad_rows = demb_slots[slot].reshape(block_rows, -1)
+            grad_out = dot_as(grad_rows, embed_full[...], 1, 1)
+
+            @pl.when(mask == 0)
+            def _():
+                dy_s[...] = grad_out
+
+            dm_s[rows, :] = grad_out.astype(low_type)
+            for first in range(0, hidden, chunk):
+                cols = slice(first, first + chunk)
+                grad_active = dot_as(dm_s[rows, :], w_down[cols, :], 1, 1)
+                du_s[rows, cols] = (grad_active * slope_s[rows, cols].astype(full_type)).astype(
+                    low_type
+                )
+            return carry
+
+        lax.fori_loop(0, count, first_back, 0)
+        ready(w_up)
+        scatter = Scatter(parts_mlp, total, landing_mlp, sems.at[2], sems.at[3])
+        total[...] = jnp.zeros_like(total)
+
+        def second_back(step, carry):
+            at_step(step, 1, [up_sum, attn_sum, down_sum])
+            mask = count - 1 - step
+            rows = rows_of(index ^ mask)
+            scatter.put(mask, dot_as(du_s[rows, :], w_up[...], 1, 1))
+            return carry
+
+        lax.fori_loop(0, count, second_back, 0)
+        for bit in range(model_bits - 1):
+            scatter.finish_bit(bit)
+
+        def store_rows(product, first, stages):
+            high = width // data_count
+            for row in range(data_count):
+                row_packed[spot_of(row, 0, stages), :, first : first + product.shape[1]] = (
+                    product[row * high : (row + 1) * high, :].astype(low_type)
+                )
+
+        def store_cols(product, first, stages):
+            wide = width // data_count
+            for col in range(data_count):
+                col_packed[
+                    spot_of(col, 0, stages), first : first + product.shape[0], :wide
+                ] = product[:, col * wide : (col + 1) * wide].astype(low_type)
+
+        ready(g_s)
+        for cut in range(CUTS):
+            cols = slice(cut * part, (cut + 1) * part)
+            store_cols(dot_as(g_s[:, cols], dm_s[...], 0, 0), cut * part, enc_stages)
+            down_sums[cut].start()
+        ready(mid_s)
+        for one in (embed_sum, up_sum, attn_sum, pred_sum):
+            one.advance()
+        scatter.finish_bit(model_bits - 1)
+
+        normed, scale = norm_parts(mid_s[...])
+        grad_second = total[...]
+        wide_acc[0, 1:2, :] = jnp.sum(grad_second * normed, axis=0, keepdims=True)
+        grad_middle = dy_s[...] + norm_back(normed, scale, grad_second * gain_mlp[...])
+        dy_s[...] = grad_middle
+        db_s[rows_of(index), :] = grad_middle.astype(low_type)
+        db_gather = Gather(None, lambda slot: db_s.at[rows_of(slot)], sems.at[4], sems.at[5])
+        db_gather.start()
+        ready(c_s)
+        for cut in range(CUTS):
+            cols = slice(cut * part, (cut + 1) * part)
+            store_rows(dot_as(c_s[...], du_s[:, cols], 0, 0), cut * part, up_orders[cut])
+            up_sums[cut].start()
+        for one in (embed_sum, attn_sum, down_sum, up_sum):
+            one.advance()
+
+        ready(w_out, qkv_s, e_s, inv_s, o_own, qkv_weights)
+        second_scatter = Scatter(parts_attn, total, landing_attn, sems.at[6], sems.at[7])
+        total[...] = jnp.zeros_like(total)
+
+        def third_back(step, carry):
+            db_gather.arrive_at(step)
+            at_step(step, 1, [embed_sum, attn_sum] + down_sums[:2])
+            at_step(step, count - 1, [embed_sum] + down_sums[2:])
+            mask = visit_mask(step, count)
+            slot = index ^ mask
+            rows = rows_of(slot)
+            do_s[...] = dot_as(w_out[...], db_s[rows, :], 1, 1)
+            for head in range(enc_heads):
+                span = slice(head * size, (head + 1) * size)
+                key_span = slice(columns + head * size, columns + (head + 1) * size)
+                value_span = slice(2 * columns + head * size, 2 * columns + (head + 1) * size)
+                query, key, value = qkv_s[span, rows], qkv_s[key_span, rows], qkv_s[value_span, rows]
+                weights = e_s[slot * enc_heads + head]
+                grad_full = do_s[span, :] * (inv_s[slot * enc_heads + head] * scaling)
+                shift = jnp.sum(
+                    grad_full * o_own[span, rows].astype(full_type), axis=0, keepdims=True
+                )
+                grad_low = grad_full.astype(low_type)
+                grad_probs = dot_as(value, grad_low, 0, 0)
+                grad_scores = (weights.astype(full_type) * (grad_probs - shift)).astype(low_type)
+                grad_value = dot_as(grad_low, weights, 1, 1) * (1.0 / scaling)
+                grad_query = jnp.dot(key, grad_scores, preferred_element_type=full_type)
+                grad_key = dot_as(query, grad_scores, 1, 1) * (1.0 / (scaling * LOG2E))
+                dqkv_s[span, rows] = grad_query.astype(low_type)
+                dqkv_s[key_span, rows] = grad_key.astype(low_type)
+                dqkv_s[value_span, rows] = grad_value.astype(low_type)
+            second_scatter.put(mask, dot_as(dqkv_s[:, rows], qkv_weights[...], 0, 0))
+            return carry
+
+        lax.fori_loop(0, count, third_back, 0)
+        for bit in range(model_bits - 1):
+            second_scatter.finish_bit(bit)
+        store_cols(
+            jnp.dot(o_own[...], db_s[...], preferred_element_type=full_type), hidden, late_stages
+        )
+        out_sum.start()
+        ready(a_s)
+        for cut, order in enumerate(qkv_orders):
+            span = slice(cut * columns, (cut + 1) * columns)
+            product = dot_as(a_s[...], dqkv_s[span, :], 0, 1)
+            store_rows(product, hidden + cut * columns, order)
+            qkv_sums[cut].start()
+        for one in up_sums[:2] + down_sums:
+            one.advance()
+        second_scatter.finish_bit(model_bits - 1)
+        normed, scale = norm_parts(tokens[...].astype(full_type))
+        grad_normed = total[...]
+        wide_acc[0, 0:1, :] = jnp.sum(grad_normed * normed, axis=0, keepdims=True)
+        grad_tokens[...] = dy_s[...] + norm_back(normed, scale, grad_normed * gain_attn[...])
+
+        def norm_copies(stage):
+            peer = partner(*all_stages[stage])[0]
+            return [
+                pltpu.make_async_remote_copy(
+                    src_ref=acc.at[stage],
+                    dst_ref=got.at[stage],
+                    send_sem=norm_sems.at[0, kind, stage],
+                    recv_sem=norm_sems.at[1, kind, stage],
+                    device_id=peer,
+                    device_id_type=MESH,
+                )
+                for kind, (acc, got) in enumerate(((wide_acc, wide_got), (thin_acc, thin_got)))
+            ]
+
+        sums = dec_sums + [embed_sum] + down_sums + up_sums
+        last = [out_sum] + qkv_sums
+        rounds = [sums, sums]
+        for turn in range(len(last) + data_bits - 1):
+            rounds.append([last[turn - back] for back in range(data_bits) if 0 <= turn - back < len(last)])
+        pending = []
+        for turn, group in enumerate(rounds):
+            if turn < len(all_stages):
+                pending = norm_copies(turn)
+                for copy in pending:
+                    copy.start()
+            for one in group:
+                one.advance()
+            if turn < len(all_stages):
+                for copy in pending:
+                    copy.wait()
+                wide_acc[turn + 1] = wide_acc[turn] + wide_got[turn]
+                thin_acc[turn + 1] = thin_acc[turn] + thin_got[turn]
+        everything = sums + last
         for one in everything:
-            one.advance()
-        for copy in copies:
-            copy.wait()
-        wide_acc[stage + 1] = wide_acc[stage] + wide_got[stage]
-        thin_acc[stage + 1] = thin_acc[stage] + thin_got[stage]
-    for one in everything:
-        while not one.done():
-            one.advance()
-    norm_wide[...] = wide_acc[len(all_stages)]
-    norm_thin[...] = thin_acc[len(all_stages)]
-    for one in (demb_gather, scatter, db_gather, second_scatter):
-        one.drain()
-
-    rows_out, cols_out = row_bufs[-1], col_bufs[-1]
-    g_up[...] = rows_out[0, :, :hidden].astype(full_type)
+            while not one.done():
+                one.advance()
+        norm_wide[...] = wide_acc[len(all_stages)]
+        norm_thin[...] = thin_acc[len(all_stages)]
+        for one in (demb_gather, scatter, db_gather, second_scatter):
+            one.drain()
+
+
+    pl.run_scoped(encoder, *scopes[2])
+    rows_out[...] = row_bufs[-1][0]
+    cols_out[...] = col_bufs[-1][0]
+    dec_out[...] = dec_bufs[-1][0]
+    embed_out[...] = embed_bufs[-1][0]
+
+
+def unpack_kernel(widths, dec_list, embed_list, *refs):
+    hidden, columns, wide = widths
+    grad_tokens, norm_wide, norm_thin, rows_in, cols_in, dec_in, embed_in = refs[:7]
+    out_tokens, g_query, g_key, g_value, g_up, g_out, g_down, g_embed = refs[7:15]
+    small = refs[15:20]
+    dec_outs = refs[20:]
+    out_tokens[...] = grad_tokens[...]
+    g_up[...] = rows_in[:, :hidden].astype(full_type)
     for position, out in enumerate((g_query, g_key, g_value)):
         first = hidden + position * columns
-        out[...] = rows_out[0, :, first : first + columns].astype(full_type)
-    wide = width // data_count
-    g_down[...] = cols_out[0, :hidden, :wide].astype(full_type)
-    g_out[...] = cols_out[0, hidden : hidden + columns, :wide].astype(full_type)
-    unpack([g_embed], [embed_piece], embed_bufs[-1])
-    unpack(dec_outs, dec_pieces_list, dec_bufs[-1])
-
-
-def unpack(outs, pieces, source):
-    for out, (offset, rows, width, tiles) in zip(outs, pieces):
-        for tile in range(tiles):
-            lanes = min(LANES, width - tile * LANES)
-            block = source[0, offset + tile * rows : offset + (tile + 1) * rows, :lanes]
-            out[:, tile * LANES : tile * LANES + lanes] = block.astype(full_type)
-
-
-def encode_back(grad_arrived, tokens, weights, saved, embed_proj, dec_packed, dec_small, dec_shapes):
+        out[...] = rows_in[:, first : first + columns].astype(full_type)
+    g_down[...] = cols_in[:hidden, :wide].astype(full_type)
+    g_out[...] = cols_in[hidden : hidden + columns, :wide].astype(full_type)
+    for position in range(2):
+        small[position][...] = norm_wide[position : position + 1, :]
+    for position in range(3):
+        small[2 + position][...] = norm_thin[position : position + 1, :]
+    for outs, pieces, source in (([g_embed], embed_list, embed_in), (dec_outs, dec_list, dec_in)):
+        for out, (offset, rows, width, tiles) in zip(outs, pieces):
+            for tile in range(tiles):
+                lanes = min(LANES, width - tile * LANES)
+                block = source[offset + tile * rows : offset + (tile + 1) * rows, :lanes]
+                out[:, tile * LANES : tile * LANES + lanes] = block.astype(full_type)
+
+
+def decode_and_back(
+    arrived,
+    grid_order,
+    grid_keep,
+    ground_dist,
+    dec_weights,
+    mask_token,
+    pred_proj,
+    cotangent,
+    tokens,
+    weights,
+    saved,
+    embed_proj,
+):
     gain_attn, w_query, w_key, w_value, w_out, gain_mlp, w_up, w_down = weights
+    (dec_gain_attn, dec_query, dec_key, dec_value, dec_proj, dec_gain_mlp, dec_up, dec_down) = (
+        dec_weights
+    )
     data_count, model_count = lax.axis_size("dp"), lax.axis_size("mp")
     data_bits, model_bits = log2_of(data_count), log2_of(model_count)
     images, visible, width = tokens.shape
     rows = images * visible
     every = rows * model_count
-    heads = HE // model_count
+    enc_heads = HE // model_count
     columns, hidden = w_query.shape[1], w_up.shape[1]
     out_width = embed_proj.shape[1] * model_count
-    pieces, height = dec_pieces(data_count, model_count, dec_shapes)
+    length, pixels = cotangent.shape[1:]
+    grid_rows = images * length
+    dec_hidden = dec_up.shape[1]
+    matrices = [dec_query, dec_key, dec_value, dec_proj, dec_up, dec_down, pred_proj]
+    pieces, height = dec_pieces(data_count, model_count, [one.shape for one in matrices])
     embed_pieces, embed_height = dec_pieces(data_count, model_count, [(width, out_width)])
     high, wide = width // data_count, width // data_count
     wide_pad = -(-wide // LANES) * LANES
     devices = data_count * model_count
     stages = data_bits + model_bits
-    dec_cuts = 4
-    plan = (images, visible, heads, pieces, embed_pieces[0])
+    row_shape = (high, hidden + 3 * columns)
+    col_shape = (hidden + columns, wide_pad)
+    vmem = pl.BlockSpec(memory_space=pltpu.VMEM)
+    hbm = pl.BlockSpec(memory_space=pl.ANY)
+    low = lambda *shape: pltpu.VMEM(shape, low_type)
+    full = lambda *shape: pltpu.VMEM(shape, full_type)
+    loaded = [w_out, w_up, w_down, *saved]
+    turned_scope = [low(out_width, out_width)] * 3
+    attn_scope = [
+        low(out_width, out_width),
+        full(grid_rows, out_width),
+        low(3 * out_width, out_width),
+        low(grid_rows, out_width),
+        low(3 * out_width, grid_rows),
+        low(images * HD, length, length),
+        full(images * HD, 1, length),
+        low(out_width, grid_rows),
+        full(grid_rows, out_width),
+        low(grid_rows, out_width),
+        full(out_width, length),
+    ]
+    dense_scope = [
+        low(out_width, dec_hidden),
+        low(dec_hidden, out_width),
+        low(out_width, pixels),
+        low(images, length, pixels),
+        full(length, out_width),
+        low(grid_rows, out_width),
+        low(grid_rows, dec_hidden),
+        low(grid_rows, dec_hidden),
+        low(grid_rows, out_width),
+        low(grid_rows, out_width),
+        full(length, pixels),
+    ]
+    enc_scope = [pltpu.VMEM(one.shape, one.dtype) for one in loaded] + [
+        low(every, width),
+        low(every, hidden),
+        low(3 * columns, every),
+        full(rows, width),
+        full(columns, rows),
+    ]
+    plan = (
+        images,
+        visible,
+        enc_heads,
+        HD,
+        SIDE,
+        pieces,
+        embed_pieces[0],
+        (attn_scope, dense_scope, enc_scope, turned_scope),
+    )
 
     def kernel(*refs):
-        encoder_back_kernel(plan, *refs)
-
-    vmem = pl.BlockSpec(memory_space=pltpu.VMEM)
+        back_kernel(plan, *refs)
+
     outs = [
+        (cotangent.shape, full_type),
+        ((rows, width), full_type),
+        ((2, width), full_type),
+        ((3, out_width), full_type),
+        (row_shape, low_type),
+        (col_shape, low_type),
+        ((height, LANES), low_type),
+        ((embed_height, LANES), low_type),
+    ]
+    scratch = [
+        pltpu.SemaphoreType.DMA((8 + len(loaded),)),
+        pltpu.SemaphoreType.DMA((images,)),
+        low(images, visible, out_width),
+        low(devices, height, LANES),
+        full(3, out_width),
+        low(images, visible, out_width),
+        low(model_count, images, visible, out_width),
+        low(every, width),
+        full(rows, width),
+        low(model_count - 1, rows, width),
+        low(model_count - 1, rows, width),
+        low(model_count - 1, rows, width),
+        low(model_count - 1, rows, width),
+        pltpu.SemaphoreType.DMA((8, model_count)),
+        pltpu.SemaphoreType.DMA((2, images)),
+        low(data_count, *row_shape),
+        low(data_count, *col_shape),
+        low(devices, embed_height, LANES),
+    ]
+    scratch += [low(data_count >> (bit + 1), *row_shape) for bit in range(data_bits)]
+    scratch += [low(data_count >> (bit + 1), *col_shape) for bit in range(data_bits)]
+    scratch += [low(devices >> (bit + 1), height, LANES) for bit in range(stages)]
+    scratch += [low(devices >> (bit + 1), embed_height, LANES) for bit in range(stages)]
+    for shape in ((2, width), (3, out_width)):
+        scratch += [full(stages + 1, *shape), full(stages, *shape)]
+    scratch += [
+        pltpu.SemaphoreType.DMA((2, CUTS + 3, data_bits)),
+        pltpu.SemaphoreType.DMA((2, CUTS + 1, data_bits)),
+        pltpu.SemaphoreType.DMA((2, 4, stages)),
+        pltpu.SemaphoreType.DMA((2, 1, stages)),
+        pltpu.SemaphoreType.DMA((2, 2, stages)),
+    ]
+    results = pl.pallas_call(
+        kernel,
+        out_shape=[jax.ShapeDtypeStruct(shape, kind) for shape, kind in outs],
+        in_specs=[pl.BlockSpec(memory_space=pltpu.SMEM)] + [vmem] * 9 + [hbm] * (8 + len(loaded)),
+        out_specs=[hbm] + [vmem] * (len(outs) - 1),
+        scratch_shapes=scratch,
+        compiler_params=pltpu.CompilerParams(
+            collective_id=2, has_side_effects=True, vmem_limit_bytes=255 * 2**18
+        ),
+    )(
+        ground_dist,
+        arrived,
+        grid_order[:, None, :],
+        grid_keep[:, None, :],
+        dec_gain_attn.reshape(1, -1),
+        dec_gain_mlp.reshape(1, -1),
+        mask_token.reshape(1, -1),
+        tokens.reshape(rows, width),
+        gain_attn.reshape(1, -1),
+        gain_mlp.reshape(1, -1),
+        dec_query,
+        dec_key,
+        dec_value,
+        dec_proj,
+        dec_up,
+        dec_down,
+        pred_proj,
+        cotangent,
+        *loaded,
+    )
+    final = [
         (rows, width),
         (high, columns),
         (high, columns),
@@ -1144,71 +1384,19 @@
         (columns, wide),
         (hidden, wide),
         (embed_pieces[0][1], embed_pieces[0][2]),
-        (2, width),
-        dec_small.shape,
-    ] + [(piece[1], piece[2]) for piece in pieces]
-    row_shape = (high, hidden + 3 * columns)
-    col_shape = (hidden + columns, wide_pad)
-    scratch = [
-        pltpu.VMEM((images, visible, out_width), low_type),
-        pltpu.VMEM((model_count, images, visible, out_width), low_type),
-        pltpu.VMEM((every, width), low_type),
-        pltpu.VMEM((every, hidden), low_type),
-        pltpu.VMEM((rows, width), low_type),
-        pltpu.VMEM((every, width), low_type),
-        pltpu.VMEM((3 * columns, every), low_type),
-        pltpu.VMEM((rows, width), full_type),
-        pltpu.VMEM((model_count, rows, width), low_type),
-        pltpu.VMEM((model_count, rows, width), low_type),
-        pltpu.VMEM((model_count, rows, width), low_type),
-        pltpu.VMEM((model_count, rows, width), low_type),
-        pltpu.VMEM((rows, width), full_type),
-        pltpu.VMEM((columns, rows), full_type),
-        pltpu.SemaphoreType.DMA((8, model_count)),
-        pltpu.SemaphoreType.DMA((2, images)),
-        pltpu.VMEM((data_count,) + row_shape, low_type),
-        pltpu.VMEM((data_count,) + col_shape, low_type),
-        pltpu.VMEM((devices, embed_height, LANES), low_type),
     ]
-    scratch += [pltpu.VMEM((data_count >> (bit + 1),) + row_shape, low_type) for bit in range(data_bits)]
-    scratch += [pltpu.VMEM((data_count >> (bit + 1),) + col_shape, low_type) for bit in range(data_bits)]
-    scratch += [pltpu.VMEM((devices >> (bit + 1), height, LANES), low_type) for bit in range(stages)]
-    scratch += [
-        pltpu.VMEM((devices >> (bit + 1), embed_height, LANES), low_type) for bit in range(stages)
-    ]
-    for shape in ((2, width), dec_small.shape):
-        scratch += [
-            pltpu.VMEM((stages + 1,) + shape, full_type),
-            pltpu.VMEM((stages,) + shape, full_type),
-        ]
-    scratch += [
-        pltpu.SemaphoreType.DMA((2, 3, data_bits)),
-        pltpu.SemaphoreType.DMA((2, 3, data_bits)),
-        pltpu.SemaphoreType.DMA((2, dec_cuts, stages)),
-        pltpu.SemaphoreType.DMA((2, 1, stages)),
-        pltpu.SemaphoreType.DMA((2, 2, stages)),
-    ]
-    return pl.pallas_call(
-        kernel,
-        out_shape=[jax.ShapeDtypeStruct(shape, full_type) for shape in outs],
-        in_specs=[vmem] * 21,
-        out_specs=[vmem] * len(outs),
-        scratch_shapes=scratch,
-        compiler_params=pltpu.CompilerParams(
-            collective_id=2, has_side_effects=True, vmem_limit_bytes=62 * 2**20
-        ),
-    )(
-        grad_arrived,
-        tokens.reshape(rows, width),
-        gain_attn.reshape(1, -1),
-        w_out,
-        gain_mlp.reshape(1, -1),
-        w_up,
-        w_down,
-        *saved,
-        dec_packed,
-        dec_small,
-    )
+    final += [(1, width)] * 2 + [(1, out_width)] * 3
+    final += [(piece[1], piece[2]) for piece in pieces]
+
+    def last_kernel(*refs):
+        unpack_kernel((hidden, columns, wide), pieces, embed_pieces, *refs)
+
+    return results[0], pl.pallas_call(
+        last_kernel,
+        out_shape=[jax.ShapeDtypeStruct(shape, full_type) for shape in final],
+        in_specs=[vmem] * (len(outs) - 1),
+        out_specs=[vmem] * len(final),
+    )(*results[1:])
 
 
 def layer_norm(values, scale_gain):
@@ -1736,10 +1924,20 @@
     enc_weights = (enc_norm, enc_query, enc_key, enc_value, enc_proj, enc_norm2, enc_up, enc_down)
     dec_weights = (dec_norm, dec_query, dec_key, dec_value, dec_proj, dec_norm2, dec_up, dec_down)
     arrived, *saved = encode(tokens, lengths, enc_weights, embed_proj)
-    decoded, dec_packed, grad_arrived, dec_small = decode(
-        arrived, grid_order, grid_keep, ground_dist, dec_weights, mask_token, pred_proj, cotangent
-    )
-    matrices = [dec_query, dec_key, dec_value, dec_proj, dec_up, dec_down, pred_proj]
+    decoded, grads = decode_and_back(
+        arrived,
+        grid_order,
+        grid_keep,
+        ground_dist,
+        dec_weights,
+        mask_token,
+        pred_proj,
+        cotangent,
+        tokens,
+        enc_weights,
+        saved,
+        embed_proj,
+    )
     (
         grad_tokens,
         g_query,
@@ -1749,38 +1947,32 @@
         g_out,
         g_down,
         g_embed,
-        norm_wide,
-        norm_thin,
+        n_enc_attn,
+        n_enc_mlp,
+        n_dec_attn,
+        n_dec_mlp,
+        n_mask,
         *dec_grads,
-    ) = encode_back(
-        grad_arrived,
-        tokens,
-        enc_weights,
-        saved,
-        embed_proj,
-        dec_packed,
-        dec_small,
-        [matrix.shape for matrix in matrices],
-    )
+    ) = grads
     return (
         decoded,
         grad_tokens.reshape(tokens.shape),
-        norm_wide[0],
+        n_enc_attn[0],
         g_query,
         g_key,
         g_value,
         g_out,
-        norm_wide[1],
+        n_enc_mlp[0],
         g_up,
         g_down,
         g_embed,
-        norm_thin[2],
-        norm_thin[0],
+        n_mask[0],
+        n_dec_attn[0],
         dec_grads[0],
         dec_grads[1],
         dec_grads[2],
         dec_grads[3],
-        norm_thin[1],
+        n_dec_mlp[0],
         dec_grads[4],
         dec_grads[5],
         dec_grads[6],

time: 290 us -> 231 us (0.80)
  Pallas kernels: 270 us -> 226 us
  local copies, waits for them, and re-layouts: 18.9 us -> 3.67 us
    pallas_call x2, Pallas kernels: 210 us -> 171 us  [the longest x1 168 us: decode_and_back(): pl.pallas_call(kernel, out_shape=[jax.ShapeDtypeStruct(shape, kind) for s...]
    unnamed x39 -> x3, local copies, waits for them, and re-layouts: 14.9 us -> 1.15 us
    pallas_call x1, Pallas kernels: 59.4 us -> 54.9 us  [encode(): pl.pallas_call(kernel, out_shape=[jax.ShapeDtypeStruct(shape, kind) for s...]
where the time goes in v3:
time: 231 us
  Pallas kernels  226 us (98%)
  local copies, waits for them, and re-layouts  3.67 us (2%)
    pallas_call x1, Pallas kernels, decode_and_back(): pl.pallas_call(kernel, out_shape=[jax.ShapeDtypeStruct(shape, kind) for s...  168 us
    pallas_call x1, Pallas kernels, encode(): pl.pallas_call(kernel, out_shape=[jax.ShapeDtypeStruct(shape, kind) for s...  54.9 us

profile of v3, /device:TPU:0, one launch (start us, length us, event | category | flops | bytes accessed | tf_op | source)
XLA Modules:
  0.0 230.8 jit_solution(1121710353204671928)
XLA Ops:
  0.7 1.3 broadcast_in_dim.6.refs_2_
  1.9 1.3 broadcast_in_dim.7.refs_3_
  3.2 54.9 %shard_map.400 = (bf16[2,64,512]{2,1,0:T(8,128)(2,1)}, bf16[512,1024]{1,0:T(8,128)(2,1)}, bf16[768,512]{1,0:T(8,128)(2,1)}, bf16[16,128,128]{2,1,0:T(8,128)(2,1)...) custom-call(s32[8]{0:T(128)} %refs_0_.2, ...), custom_call_target="tpu_custom_call" | custom-call | tf_op jit(solution)/shard_map/pallas_call | solution.py:556
  58.1 168.4 %shard_map.401 = (f32[2,256,768]{2,1,0:T(8,128)}, f32[128,1024]{1,0:T(8,128)}, f32[2,1024]{1,0:T(2,128)}, f32[3,512]{1,0:T(4,128)}, bf16[128,1792]{1,0:T(8,128)(...) custom-call(f32[2]{0:T(128)} %refs_0_.3, ...), custom_call_target="tpu_custom_call" | custom-call | tf_op jit(solution)/shard_map/pallas_call | solution.py:1348
  226.6 0.0 copy-start
  226.6 3.0 %shard_map.402 = (f32[128,1024]{1,0:T(8,128)}, f32[128,256]{1,0:T(8,128)}, f32[128,256]{1,0:T(8,128)}, f32[128,256]{1,0:T(8,128)}, f32[128,1024]{1,0:T(8,128)}, ...) custom-call(f32[128,1024]{1,0:T(8,128)} %get-tuple-element.76.refs_0, ...), custom_call_target="tpu_custom_call" | custom-call | tf_op jit(solution)/shard_map/pallas_call | solution.py:1394
  229.6 0.0 copy-done
  229.6 1.1 copy.47
Async XLA Ops:
  226.6 3.1 %copy-start = (f32[2,256,768]{2,1,0:T(8,128)S(1)}, f32[2,256,768]{2,1,0:T(8,128)}, u32[]{:S(2)}) copy-start(f32[2,256,768]{2,1,0:T(8,128)} %get-tuple-element.124) | copy-start | bytes 4718596

commit v4 on v3

--- a/solution.py
+++ b/solution.py
@@ -417,6 +417,7 @@
     swap = Exchange(images, embedded, arrived, swap_sems.at[0], swap_sems.at[1])
 
     token_gather.start()
+    out_gather.start()
     token_slots[index] = tokens[...]
     out_full[pl.ds(pl.multiple_of(index * columns, columns), columns), :] = w_out[...]
     embed_slots[index] = w_embed[...]
@@ -430,10 +431,6 @@
 
     def attend(step, carry):
         token_gather.arrive_at(step)
-
-        @pl.when(step == count // 2)
-        def _():
-            out_gather.start()
 
         slot = index ^ visit_mask(step, count)
         rows = rows_of(slot)
@@ -469,13 +466,13 @@
 
     lax.fori_loop(0, count, attend, 0)
     o_gather.start()
+    embed_gather.start()
     save(a_s, qkv_s, e_s, inv_s, o_own)
     for move in loads:
         move.wait()
     o_full[pl.ds(pl.multiple_of(index * columns, columns), columns), :] = o_own[...]
     out_gather.arrive_all()
     o_gather.arrive_all()
-    embed_gather.start()
     total[...] = jnp.zeros_like(total)
 
     def expand(step, carry):
@@ -602,15 +599,152 @@
     )
 
 
-CUTS = 4
-LATE_UP = 0
-
-
-def at_step(step, when, sums):
-    @pl.when(step == when)
-    def _():
-        for one in sums:
-            one.advance()
+EARLY_DOWN, EARLY_UP, UP_FIRST = True, False, True
+SUM_ORDERS = {
+    "attn": ["crossed"],
+    "dup": ["spread", "spreadz", "all", "spreadz"],
+    "ddn": ["spread", "spread", "spread", "spread"],
+    "pred": ["all"],
+    "emb": ["spread", "spread"],
+    "dn": ["Z", "Y", "Y", "Y"],
+    "up": ["Y", "Y", "Y", "Y"],
+    "oq": ["Y", "Y", "Y", "Y"],
+}
+PLAN = {
+    "a3": [
+        "pred0",
+        "ddn0",
+        "ddn1",
+        "ddn2",
+        "ddn3",
+        "dup0",
+        "dup1",
+        "dup2",
+        "dup3",
+    ],
+    "a4": [
+        "ddn0",
+        "dup1",
+        "pred0",
+        "ddn1",
+    ],
+    "a5": [
+        "dup3",
+        "dup2",
+        "ddn2",
+        "attn0",
+        "ddn0",
+        "ddn3",
+    ],
+    "f1": [
+        "ddn1",
+        "dup1",
+        "emb0",
+        "emb1",
+        "dup0",
+    ],
+    "f2": [
+        "pred0",
+        "ddn2",
+        "dup3",
+    ],
+    "f3": [
+        "dup2",
+        "ddn3",
+    ],
+    "b0": [
+        "ddn0",
+        "dup1",
+        "ddn1",
+        "dup0",
+        "emb0",
+        "pred0",
+        "dup2",
+        "ddn2",
+        "emb1",
+        "dup3",
+        "ddn3",
+    ],
+    "s2": [
+        "attn0",
+        "ddn0",
+        "dup1",
+    ],
+    "s3": [
+        "ddn1",
+        "ddn2",
+        "dup3",
+    ],
+    "b2": [
+        "ddn3",
+        "dn0",
+        "dn1",
+    ],
+    "b4": [
+        "dup0",
+        "emb0",
+        "pred0",
+    ],
+    "b5": [
+        "dup2",
+        "emb1",
+        "dn2",
+        "dup0",
+    ],
+    "t2": [
+        "attn0",
+        "dn3",
+        "dn1",
+        "dn0",
+        "up0",
+    ],
+    "b6": [
+        "emb0",
+        "emb1",
+        "dn2",
+    ],
+    "b7": [
+        "up1",
+    ],
+    "tail": [
+        "dn3",
+        "attn0",
+        "up2",
+        "dn1",
+        "emb0",
+        "up0",
+        "emb1",
+        "norm",
+        "up3",
+        "dn2",
+        "up1",
+        "norm",
+        "dn0",
+        "dn3",
+        "up2",
+        "o",
+        "up0",
+        "up3",
+        "q",
+        "up1",
+        "up2",
+        "o",
+        "k",
+        "up3",
+        "q",
+        "v",
+        "o",
+        "k",
+        "attn0",
+        "norm",
+        "q",
+        "v",
+        "norm",
+        "k",
+        "v",
+        "norm",
+    ],
+}
 
 
 class Bulk:
@@ -625,7 +759,7 @@
         return self.stage == len(self.one.stages)
 
     def advance(self):
-        if self.done():
+        if self.stage is None or self.done():
             return
         self.one.finish(self.stage)
         self.stage += 1
@@ -679,8 +813,29 @@
     late_stages = enc_stages[1:] + enc_stages[:1]
     model_stages = [("mp", bit) for bit in range(model_bits)]
     all_stages = model_stages + enc_stages
-    crossed_stages = model_stages + late_stages
-    spread_stages = model_stages[:1] + enc_stages + model_stages[1:]
+    near, far = model_stages[:1], model_stages[1:]
+    orders = {
+        "Y": enc_stages,
+        "Z": late_stages,
+        "all": all_stages,
+        "crossed": model_stages + late_stages,
+        "spread": near + enc_stages + far,
+        "spreadz": near + late_stages + far,
+    }
+    sums = {}
+
+    def pump(point):
+        for name in PLAN.get(point, ()):
+            if name in sums:
+                sums[name].advance()
+
+    def pump_at(step, point):
+        for turn in range(count):
+            if PLAN.get(point + str(turn)):
+                @pl.when(step == turn)
+                def _():
+                    pump(point + str(turn))
+
     chunk = 512
 
     def bulk(stages, bufs, axis, first, extent, pair, cut):
@@ -688,15 +843,21 @@
         window[axis - 1] = pl.ds(first, extent)
         return Bulk(HalvingSum(stages, bufs, tuple(window), pair.at[0, cut], pair.at[1, cut]))
 
-    dec_orders = [spread_stages] * 5 + [crossed_stages] * 2
-    dec_spans = [(pieces[0][0], pieces[4][0])]
-    for piece in pieces[4:]:
-        dec_spans.append((piece[0], piece[0] + piece[1] * piece[3]))
-    dec_sums = [
-        bulk(dec_orders[3 + cut], dec_bufs, 1, first, last - first, dec_sems, cut)
-        for cut, (first, last) in enumerate(dec_spans)
-    ]
-    attn_sum, up_sum, down_sum, pred_sum = dec_sums
+    limits = [pieces[0][0]] + [piece[0] for piece in pieces[4:]] + [dec_packed.shape[1]]
+    dec_rows = []
+    for kind, first, last in zip(("attn", "dup", "ddn", "pred"), limits, limits[1:]):
+        names = SUM_ORDERS[kind]
+        extent = (last - first) // len(names)
+        for cut, order in enumerate(names):
+            begin = first + cut * extent
+            sums[kind + str(cut)] = bulk(
+                orders[order], dec_bufs, 1, begin, extent, dec_sems, len(dec_rows)
+            )
+            dec_rows.append((begin, begin + extent, orders[order]))
+
+    def start(kind):
+        for cut in range(len(SUM_ORDERS[kind])):
+            sums[kind + str(cut)].start()
 
     def store_dec(which, product):
         offset, height, span, tiles = pieces[which]
@@ -705,12 +866,16 @@
                 lanes = min(LANES, span - tile * LANES)
                 first = column * span + tile * LANES
                 block = product[:, first : first + lanes].astype(low_type)
-                for row in range(data_count):
-                    dec_packed[
-                        spot_of(row, column, dec_orders[which]),
-                        offset + tile * height : offset + (tile + 1) * height,
-                        :lanes,
-                    ] = block[row * height : (row + 1) * height, :]
+                base = offset + tile * height
+                for begin, end, order in dec_rows:
+                    low_row, high_row = max(begin, base), min(end, base + height)
+                    if low_row >= high_row:
+                        continue
+                    for row in range(data_count):
+                        shift = row * height - base
+                        dec_packed[spot_of(row, column, order), low_row:high_row, :lanes] = block[
+                            low_row + shift : high_row + shift, :
+                        ]
 
     swap = Exchange(images, grad_arrived, demb_own, swap_sems.at[0], swap_sems.at[1])
 
@@ -748,8 +913,12 @@
         pl.run_scoped(turned, *scopes[3])
 
         def picks(image):
-            order = order_ref[image, :, :visible]
-            kept = jnp.sum(keep_ref[image], axis=1, keepdims=True)
+            order = jnp.zeros((1, visible), jnp.int32)
+            flags = jnp.zeros((1, length), jnp.int32)
+            for one in range(images):
+                order = jnp.where(image == one, order_ref[one : one + 1, :visible], order)
+                flags = jnp.where(image == one, keep_ref[one : one + 1, :], flags)
+            kept = jnp.sum(flags, axis=1, keepdims=True)
             return jnp.where((order == place) & (turn < kept), 1.0, 0.0)
 
         def rows_of(image):
@@ -817,7 +986,7 @@
                     o_s[pl.ds(span, size), rows] = (mixed * inverse).astype(low_type)
                     return inner
 
-                lax.fori_loop(0, heads, one_head, 0, unroll=4)
+                lax.fori_loop(0, heads, one_head, 0, unroll=heads)
 
                 middle = start + dot_as(o_s[:, rows], w_out[...], 0, 0)
                 mid_s[...] = middle
@@ -864,13 +1033,13 @@
             lax.fori_loop(0, images, one_image, 0)
             all_pixels = cotangent[...].reshape(-1, cotangent.shape[2])
             store_dec(6, dot_as(low_s[...], all_pixels, 0, 0))
-            pred_sum.start()
+            start("pred")
             store_dec(5, dot_as(g_s[...], dm_s[...], 0, 0))
-            down_sum.start()
-            pred_sum.advance()
+            start("ddn")
+            pump("a1")
             store_dec(4, dot_as(c_s[...], du_s[...], 0, 0))
-            up_sum.start()
-            down_sum.advance()
+            start("dup")
+            pump("a2")
             stage_copy(images - 1).wait()
 
         pl.run_scoped(dense, *scopes[1])
@@ -899,7 +1068,7 @@
                 qkv_s[pl.ds(2 * width + span, size), rows] = grad_value.astype(low_type)
                 return inner
 
-            lax.fori_loop(0, heads, back_head, 0, unroll=4)
+            lax.fori_loop(0, heads, back_head, 0, unroll=heads)
 
             grad_normed = dot_as(qkv_s[:, rows], qkv_weights[...], 0, 0)
             normed, scale = norm_parts(xs[rows, :])
@@ -914,16 +1083,14 @@
                 pick.astype(low_type), grad_start.astype(low_type), 0, 0
             ).astype(low_type)
             if image == 0:
-                up_sum.advance()
-                pred_sum.advance()
+                pump("a3")
         swap.start()
         for position in range(3):
             grads = qkv_s[position * width : (position + 1) * width, :]
             store_dec(position, dot_as(a_s[...], grads, 0, 1))
         store_dec(3, jnp.dot(o_s[...], db_dec[...], preferred_element_type=full_type))
-        attn_sum.start()
-        pred_sum.advance()
-        down_sum.advance()
+        start("attn")
+        pump("a4")
 
     pl.run_scoped(decoder, *scopes[0])
     thin_acc[0] = small[...]
@@ -962,22 +1129,33 @@
             for array in arrays:
                 moves[[array is one for one in loaded].index(True)].wait()
 
-        embed_sum = bulk(spread_stages, embed_bufs, 1, 0, embed_packed.shape[1], embed_sems, 0)
-        part = hidden // CUTS
-        up_orders = [enc_stages] * (CUTS - LATE_UP) + [late_stages] * LATE_UP
-        up_sums = [
-            bulk(up_orders[cut], row_bufs, 2, cut * part, part, row_sems, cut)
-            for cut in range(CUTS)
-        ]
-        qkv_orders = [enc_stages, enc_stages, enc_stages]
-        qkv_sums = [
-            bulk(order, row_bufs, 2, hidden + cut * columns, columns, row_sems, CUTS + cut)
-            for cut, order in enumerate(qkv_orders)
-        ]
-        down_sums = [
-            bulk(enc_stages, col_bufs, 1, cut * part, part, col_sems, cut) for cut in range(CUTS)
-        ]
-        out_sum = bulk(late_stages, col_bufs, 1, hidden, columns, col_sems, CUTS)
+        def cut_sums(kind, bufs, axis, extent, pair, base=0):
+            for cut, order in enumerate(SUM_ORDERS[kind]):
+                sums[kind + str(cut)] = bulk(
+                    orders[order], bufs, axis, cut * extent, extent, pair, base + cut
+                )
+
+        embed_cuts = len(SUM_ORDERS["emb"])
+        embed_part = embed_packed.shape[1] // embed_cuts
+        cut_sums("emb", embed_bufs, 1, embed_part, embed_sems)
+        up_part = hidden // len(SUM_ORDERS["up"])
+        down_part = hidden // len(SUM_ORDERS["dn"])
+        cut_sums("up", row_bufs, 2, up_part, row_sems)
+        cut_sums("dn", col_bufs, 1, down_part, col_sems)
+        out_order, *qkv_orders = (orders[one] for one in SUM_ORDERS["oq"])
+        for cut, name in enumerate("qkv"):
+            sums[name] = bulk(
+                qkv_orders[cut],
+                row_bufs,
+                2,
+                hidden + cut * columns,
+                columns,
+                row_sems,
+                len(SUM_ORDERS["up"]) + cut,
+            )
+        sums["o"] = bulk(
+            out_order, col_bufs, 1, hidden, columns, col_sems, len(SUM_ORDERS["dn"])
+        )
 
         swap.finish()
         demb_gather = Gather(demb_own, lambda slot: demb_slots.at[slot], sems.at[0], sems.at[1])
@@ -988,17 +1166,21 @@
         product = dot_as(low_s[...], demb_own[...].reshape(block_rows, -1), 0, 0)
         for column in range(model_count):
             for row in range(data_count):
-                spot = spot_of(row, column, spread_stages)
-                for tile in range(tiles):
-                    lanes = min(LANES, span - tile * LANES)
-                    first = column * span + tile * LANES
-                    embed_packed[spot, tile * high : (tile + 1) * high, :lanes] = product[
-                        row * high : (row + 1) * high, first : first + lanes
-                    ].astype(low_type)
-        embed_sum.start()
-        attn_sum.advance()
-        up_sum.advance()
-        pred_sum.advance()
+                for cut, order in enumerate(SUM_ORDERS["emb"]):
+                    spot = spot_of(row, column, orders[order])
+                    for tile in range(tiles):
+                        lanes = min(LANES, span - tile * LANES)
+                        first = column * span + tile * LANES
+                        base = tile * high
+                        begin = max(base, cut * embed_part)
+                        end = min(base + high, (cut + 1) * embed_part)
+                        if begin < end:
+                            shift = row * high - base
+                            embed_packed[spot, begin:end, :lanes] = product[
+                                begin + shift : end + shift, first : first + lanes
+                            ].astype(low_type)
+        start("emb")
+        pump("a5")
         ready(embed_full, w_down, slope_s)
 
         def rows_of(slot):
@@ -1006,7 +1188,7 @@
 
         def first_back(step, carry):
             demb_gather.arrive_at(step)
-            at_step(step, 2, [embed_sum, down_sum])
+            pump_at(step, "f")
             mask = visit_mask(step, count)
             slot = index ^ mask
             rows = rows_of(slot)
@@ -1027,20 +1209,6 @@
             return carry
 
         lax.fori_loop(0, count, first_back, 0)
-        ready(w_up)
-        scatter = Scatter(parts_mlp, total, landing_mlp, sems.at[2], sems.at[3])
-        total[...] = jnp.zeros_like(total)
-
-        def second_back(step, carry):
-            at_step(step, 1, [up_sum, attn_sum, down_sum])
-            mask = count - 1 - step
-            rows = rows_of(index ^ mask)
-            scatter.put(mask, dot_as(du_s[rows, :], w_up[...], 1, 1))
-            return carry
-
-        lax.fori_loop(0, count, second_back, 0)
-        for bit in range(model_bits - 1):
-            scatter.finish_bit(bit)
 
         def store_rows(product, first, stages):
             high = width // data_count
@@ -1056,14 +1224,49 @@
                     spot_of(col, 0, stages), first : first + product.shape[0], :wide
                 ] = product[:, col * wide : (col + 1) * wide].astype(low_type)
 
-        ready(g_s)
-        for cut in range(CUTS):
-            cols = slice(cut * part, (cut + 1) * part)
-            store_cols(dot_as(g_s[:, cols], dm_s[...], 0, 0), cut * part, enc_stages)
-            down_sums[cut].start()
+        def down_grads():
+            ready(g_s)
+            for cut, order in enumerate(SUM_ORDERS["dn"]):
+                cols = slice(cut * down_part, (cut + 1) * down_part)
+                product = dot_as(g_s[:, cols], dm_s[...], 0, 0)
+                store_cols(product, cut * down_part, orders[order])
+                sums["dn" + str(cut)].start()
+            pump("b0" if EARLY_DOWN else "b3")
+
+        def up_grads():
+            ready(c_s)
+            for cut, order in enumerate(SUM_ORDERS["up"]):
+                cols = slice(cut * up_part, (cut + 1) * up_part)
+                product = dot_as(c_s[...], du_s[:, cols], 0, 0)
+                store_rows(product, cut * up_part, orders[order])
+                sums["up" + str(cut)].start()
+            pump("b1" if EARLY_UP else "b4")
+
+        if EARLY_DOWN:
+            down_grads()
+        if EARLY_UP:
+            up_grads()
+        ready(w_up)
+        scatter = Scatter(parts_mlp, total, landing_mlp, sems.at[2], sems.at[3])
+        total[...] = jnp.zeros_like(total)
+
+        def second_back(step, carry):
+            pump_at(step, "s")
+            mask = count - 1 - step
+            rows = rows_of(index ^ mask)
+            scatter.put(mask, dot_as(du_s[rows, :], w_up[...], 1, 1))
+            return carry
+
+        lax.fori_loop(0, count, second_back, 0)
+        for bit in range(model_bits - 1):
+            scatter.finish_bit(bit)
+
+        pump("b2")
+        if not EARLY_DOWN:
+            down_grads()
+        if not EARLY_UP and UP_FIRST:
+            up_grads()
         ready(mid_s)
-        for one in (embed_sum, up_sum, attn_sum, pred_sum):
-            one.advance()
         scatter.finish_bit(model_bits - 1)
 
         normed, scale = norm_parts(mid_s[...])
@@ -1074,22 +1277,16 @@
         db_s[rows_of(index), :] = grad_middle.astype(low_type)
         db_gather = Gather(None, lambda slot: db_s.at[rows_of(slot)], sems.at[4], sems.at[5])
         db_gather.start()
-        ready(c_s)
-        for cut in range(CUTS):
-            cols = slice(cut * part, (cut + 1) * part)
-            store_rows(dot_as(c_s[...], du_s[:, cols], 0, 0), cut * part, up_orders[cut])
-            up_sums[cut].start()
-        for one in (embed_sum, attn_sum, down_sum, up_sum):
-            one.advance()
-
+        pump("b5")
+        if not EARLY_UP and not UP_FIRST:
+            up_grads()
         ready(w_out, qkv_s, e_s, inv_s, o_own, qkv_weights)
         second_scatter = Scatter(parts_attn, total, landing_attn, sems.at[6], sems.at[7])
         total[...] = jnp.zeros_like(total)
 
         def third_back(step, carry):
             db_gather.arrive_at(step)
-            at_step(step, 1, [embed_sum, attn_sum] + down_sums[:2])
-            at_step(step, count - 1, [embed_sum] + down_sums[2:])
+            pump_at(step, "t")
             mask = visit_mask(step, count)
             slot = index ^ mask
             rows = rows_of(slot)
@@ -1119,18 +1316,18 @@
         lax.fori_loop(0, count, third_back, 0)
         for bit in range(model_bits - 1):
             second_scatter.finish_bit(bit)
+        pump("b6")
         store_cols(
-            jnp.dot(o_own[...], db_s[...], preferred_element_type=full_type), hidden, late_stages
+            jnp.dot(o_own[...], db_s[...], preferred_element_type=full_type), hidden, out_order
         )
-        out_sum.start()
+        sums["o"].start()
         ready(a_s)
         for cut, order in enumerate(qkv_orders):
             span = slice(cut * columns, (cut + 1) * columns)
             product = dot_as(a_s[...], dqkv_s[span, :], 0, 1)
             store_rows(product, hidden + cut * columns, order)
-            qkv_sums[cut].start()
-        for one in up_sums[:2] + down_sums:
-            one.advance()
+            sums["qkv"[cut]].start()
+        pump("b7")
         second_scatter.finish_bit(model_bits - 1)
         normed, scale = norm_parts(tokens[...].astype(full_type))
         grad_normed = total[...]
@@ -1151,26 +1348,28 @@
                 for kind, (acc, got) in enumerate(((wide_acc, wide_got), (thin_acc, thin_got)))
             ]
 
-        sums = dec_sums + [embed_sum] + down_sums + up_sums
-        last = [out_sum] + qkv_sums
-        rounds = [sums, sums]
-        for turn in range(len(last) + data_bits - 1):
-            rounds.append([last[turn - back] for back in range(data_bits) if 0 <= turn - back < len(last)])
-        pending = []
-        for turn, group in enumerate(rounds):
-            if turn < len(all_stages):
-                pending = norm_copies(turn)
-                for copy in pending:
+        def norm_step(turn):
+            for copy in norm_copies(turn):
+                copy.wait()
+            wide_acc[turn + 1] = wide_acc[turn] + wide_got[turn]
+            thin_acc[turn + 1] = thin_acc[turn] + thin_got[turn]
+            if turn + 1 < len(all_stages):
+                for copy in norm_copies(turn + 1):
                     copy.start()
-            for one in group:
-                one.advance()
-            if turn < len(all_stages):
-                for copy in pending:
-                    copy.wait()
-                wide_acc[turn + 1] = wide_acc[turn] + wide_got[turn]
-                thin_acc[turn + 1] = thin_acc[turn] + thin_got[turn]
-        everything = sums + last
-        for one in everything:
+
+        for copy in norm_copies(0):
+            copy.start()
+        turn = 0
+        for name in PLAN["tail"]:
+            if name == "norm":
+                if turn < len(all_stages):
+                    norm_step(turn)
+                    turn += 1
+            elif name in sums:
+                sums[name].advance()
+        for later in range(turn, len(all_stages)):
+            norm_step(later)
+        for one in sums.values():
             while not one.done():
                 one.advance()
         norm_wide[...] = wide_acc[len(all_stages)]
@@ -1247,6 +1446,7 @@
     wide_pad = -(-wide // LANES) * LANES
     devices = data_count * model_count
     stages = data_bits + model_bits
+    dec_cuts = sum(len(SUM_ORDERS[kind]) for kind in ("attn", "dup", "ddn", "pred"))
     row_shape = (high, hidden + 3 * columns)
     col_shape = (hidden + columns, wide_pad)
     vmem = pl.BlockSpec(memory_space=pltpu.VMEM)
@@ -1339,10 +1539,10 @@
     for shape in ((2, width), (3, out_width)):
         scratch += [full(stages + 1, *shape), full(stages, *shape)]
     scratch += [
-        pltpu.SemaphoreType.DMA((2, CUTS + 3, data_bits)),
-        pltpu.SemaphoreType.DMA((2, CUTS + 1, data_bits)),
-        pltpu.SemaphoreType.DMA((2, 4, stages)),
-        pltpu.SemaphoreType.DMA((2, 1, stages)),
+        pltpu.SemaphoreType.DMA((2, len(SUM_ORDERS["up"]) + 3, data_bits)),
+        pltpu.SemaphoreType.DMA((2, len(SUM_ORDERS["dn"]) + 1, data_bits)),
+        pltpu.SemaphoreType.DMA((2, dec_cuts, stages)),
+        pltpu.SemaphoreType.DMA((2, len(SUM_ORDERS["emb"]), stages)),
         pltpu.SemaphoreType.DMA((2, 2, stages)),
     ]
     results = pl.pallas_call(
@@ -1357,8 +1557,8 @@
     )(
         ground_dist,
         arrived,
-        grid_order[:, None, :],
-        grid_keep[:, None, :],
+        grid_order,
+        grid_keep,
         dec_gain_attn.reshape(1, -1),
         dec_gain_mlp.reshape(1, -1),
         mask_token.reshape(1, -1),

time: 231 us -> 198 us (0.86)
  Pallas kernels: 226 us -> 196 us
  local copies, waits for them, and re-layouts: 3.67 us -> 1.15 us
    pallas_call x1, Pallas kernels: 168 us -> 143 us  [decode_and_back(): pl.pallas_call(kernel, out_shape=[jax.ShapeDtypeStruct(shape, kind) for s...]
    pallas_call x1, Pallas kernels: 54.9 us -> 49.9 us  [encode(): pl.pallas_call(kernel, out_shape=[jax.ShapeDtypeStruct(shape, kind) for s...]
    broadcast_in_dim x2 -> x0, local copies, waits for them, and re-layouts: 2.52 us -> none  [the longest x1 1.26 us: decode_and_back(): grid_order[:, None, :]]
where the time goes in v4:
time: 198 us
  Pallas kernels  196 us (99%)
    pallas_call x1, Pallas kernels, decode_and_back(): pl.pallas_call(kernel, out_shape=[jax.ShapeDtypeStruct(shape, kind) for s...  143 us
    pallas_call x1, Pallas kernels, encode(): pl.pallas_call(kernel, out_shape=[jax.ShapeDtypeStruct(shape, kind) for s...  49.9 us

profile of v4, /device:TPU:0, one launch (start us, length us, event | category | flops | bytes accessed | tf_op | source)
XLA Modules:
  0.0 197.8 jit_solution(4790925092260004515)
XLA Ops:
  0.7 49.9 %shard_map.400 = (bf16[2,64,512]{2,1,0:T(8,128)(2,1)}, bf16[512,1024]{1,0:T(8,128)(2,1)}, bf16[768,512]{1,0:T(8,128)(2,1)}, bf16[16,128,128]{2,1,0:T(8,128)(2,1)...) custom-call(s32[8]{0:T(128)} %refs_0_.2, ...), custom_call_target="tpu_custom_call" | custom-call | tf_op jit(solution)/shard_map/pallas_call | solution.py:553
  50.6 143.0 %shard_map.401 = (f32[2,256,768]{2,1,0:T(8,128)}, f32[128,1024]{1,0:T(8,128)}, f32[2,1024]{1,0:T(2,128)}, f32[3,512]{1,0:T(4,128)}, bf16[128,1792]{1,0:T(8,128)(...) custom-call(f32[2]{0:T(128)} %refs_0_.3, ...), custom_call_target="tpu_custom_call" | custom-call | tf_op jit(solution)/shard_map/pallas_call | solution.py:1548
  193.6 0.0 copy-start
  193.6 3.0 %shard_map.402 = (f32[128,1024]{1,0:T(8,128)}, f32[128,256]{1,0:T(8,128)}, f32[128,256]{1,0:T(8,128)}, f32[128,256]{1,0:T(8,128)}, f32[128,1024]{1,0:T(8,128)}, ...) custom-call(f32[128,1024]{1,0:T(8,128)} %get-tuple-element.76.refs_0, ...), custom_call_target="tpu_custom_call" | custom-call | tf_op jit(solution)/shard_map/pallas_call | solution.py:1594
  196.7 0.0 copy-done
  196.7 1.1 copy.47
Async XLA Ops:
  193.6 3.1 %copy-start = (f32[2,256,768]{2,1,0:T(8,128)S(1)}, f32[2,256,768]{2,1,0:T(8,128)}, u32[]{:S(2)}) copy-start(f32[2,256,768]{2,1,0:T(8,128)} %get-tuple-element.124) | copy-start | bytes 4718596

commit v5 on v4

--- a/solution.py
+++ b/solution.py
@@ -220,18 +220,21 @@
             def _():
                 self.copy(odd).start()
 
+    def finish(self, mask):
+        bit = low_bit(mask)
+        self.copy(mask).wait_recv()
+        rest = mask ^ (1 << bit)
+        if rest:
+            self.parts[rest - 1] = self.parts[rest - 1] + self.landing[mask - 1]
+            if low_bit(rest) == bit + 1:
+                self.copy(rest).start()
+        else:
+            self.total[...] = self.total[...] + self.landing[mask - 1].astype(full_type)
+
     def finish_bit(self, bit):
-        step = 1 << bit
         masks = [mask for mask in range(1, self.count) if low_bit(mask) == bit]
         for mask in reversed(masks):
-            self.copy(mask).wait_recv()
-            rest = mask ^ step
-            if rest:
-                self.parts[rest - 1] = self.parts[rest - 1] + self.landing[mask - 1]
-                if low_bit(rest) == bit + 1:
-                    self.copy(rest).start()
-            else:
-                self.total[...] = self.total[...] + self.landing[mask - 1].astype(full_type)
+            self.finish(mask)
 
     def drain(self):
         for mask in range(1, self.count):
@@ -357,8 +360,11 @@
         qkv_weights,
         move_sems,
         token_slots,
-        out_full,
-        o_full,
+        out_pair,
+        o_pair,
+        part_own,
+        part_sent,
+        part_got,
         embed_slots,
         parts,
         landing,
@@ -366,6 +372,7 @@
         embedded,
         sems,
         swap_sems,
+        pair_sems,
     ) = refs[24:]
     count = lax.axis_size("mp")
     index = lax.axis_index("mp")
@@ -400,34 +407,48 @@
     token_gather = Gather(
         tokens, lambda slot: token_slots.at[slot], sems.at[0], sems.at[1]
     )
-    out_gather = Gather(
-        w_out,
-        lambda slot: out_full.at[pl.ds(pl.multiple_of(slot * columns, columns), columns)],
-        sems.at[2],
-        sems.at[3],
-    )
-    o_gather = Gather(
-        o_own,
-        lambda slot: o_full.at[pl.ds(pl.multiple_of(slot * columns, columns), columns)],
-        sems.at[4],
-        sems.at[5],
-    )
+    near, far = 0, 1
+
+    def rows_of(slot):
+        return pl.ds(pl.multiple_of(slot * block_rows, block_rows), block_rows)
+
+    def pair_copy(which, source, target, bit):
+        return pltpu.make_async_remote_copy(
+            src_ref=source,
+            dst_ref=target,
+            send_sem=pair_sems.at[0, which],
+            recv_sem=pair_sems.at[1, which],
+            device_id=partner("mp", bit)[0],
+            device_id_type=MESH,
+        )
+
+    out_copy = pair_copy(0, w_out, out_pair.at[columns : 2 * columns], near)
+
+    def o_copy(mine):
+        block = index ^ (1 + 2 * mine)
+        target = o_pair.at[mine, columns : 2 * columns]
+        return pair_copy(1 + mine, o_own.at[:, rows_of(block)], target, near)
+
+    def part_copy(mine):
+        return pair_copy(3 + mine, part_sent.at[mine], part_got.at[1 - mine], far)
+
+    def c_copy(mine):
+        place = c_s.at[rows_of(index ^ (2 * mine))]
+        return pair_copy(5 + mine, place, place, near)
+
     embed_gather = Gather(w_embed, lambda slot: embed_slots.at[slot], sems.at[6], sems.at[7])
     scatter = Scatter(parts, total, landing, sems.at[8], sems.at[9])
     swap = Exchange(images, embedded, arrived, swap_sems.at[0], swap_sems.at[1])
 
     token_gather.start()
-    out_gather.start()
+    out_copy.start()
     token_slots[index] = tokens[...]
-    out_full[pl.ds(pl.multiple_of(index * columns, columns), columns), :] = w_out[...]
+    out_pair[:columns, :] = w_out[...]
     embed_slots[index] = w_embed[...]
     for position, weight in enumerate((w_query, w_key, w_value)):
         loads[position].wait()
         qkv_weights[position * columns : (position + 1) * columns, :] = weight[...].T
     save(qkv_weights)
-
-    def rows_of(slot):
-        return pl.ds(pl.multiple_of(slot * block_rows, block_rows), block_rows)
 
     def attend(step, carry):
         token_gather.arrive_at(step)
@@ -462,31 +483,54 @@
             inv_s[slot * heads + head] = inverse
             mixed = jnp.dot(value, weights, preferred_element_type=full_type)
             o_own[span, rows] = (mixed * inverse).astype(low_type)
+        for turn, mine in ((1, 0), (2, 1)):
+            @pl.when(step == turn)
+            def _():
+                o_copy(mine).start()
+
+        for turn, mine in ((0, 0), (3, 1)):
+            @pl.when(step == turn)
+            def _():
+                o_pair[mine, :columns, :] = o_own[:, rows]
+
         return carry
 
-    lax.fori_loop(0, count, attend, 0)
-    o_gather.start()
+    def sum_heads(mine):
+        o_copy(mine).wait_recv()
+        part = dot_as(o_pair[mine], out_pair[...], 0, 0)
+        part_own[mine] = part
+        part_sent[mine] = part.astype(low_type)
+        part_copy(mine).start()
+
+    def middle_of(mine):
+        part_copy(1 - mine).wait_recv()
+        slot = index ^ (2 * mine)
+        middle = token_slots[slot].astype(full_type) + part_own[mine]
+        middle = middle + part_got[mine].astype(full_type)
+        if mine == 0:
+            mid_s[...] = middle
+        normed, scale = norm_parts(middle)
+        c_s[rows_of(slot), :] = (normed * gain_mlp[...]).astype(low_type)
+        c_copy(mine).start()
+
+    lax.fori_loop(0, 2, attend, 0)
+    out_copy.wait_recv()
+    sum_heads(0)
+    lax.fori_loop(2, 4, attend, 0)
+    sum_heads(1)
     embed_gather.start()
     save(a_s, qkv_s, e_s, inv_s, o_own)
     for move in loads:
         move.wait()
-    o_full[pl.ds(pl.multiple_of(index * columns, columns), columns), :] = o_own[...]
-    out_gather.arrive_all()
-    o_gather.arrive_all()
     total[...] = jnp.zeros_like(total)
 
-    def expand(step, carry):
-        mask = count - 1 - step
-        slot = index ^ mask
-        rows = rows_of(slot)
-        middle = token_slots[slot].astype(full_type) + dot_as(o_full[:, rows], out_full[...], 0, 0)
-
-        @pl.when(mask == 0)
-        def _():
-            mid_s[...] = middle
-
-        normed, scale = norm_parts(middle)
-        c_s[rows, :] = (normed * gain_mlp[...]).astype(low_type)
+    def expand(mask, carry):
+        for odd in (1, 3):
+            @pl.when(mask == odd)
+            def _():
+                c_copy(odd // 2).wait_recv()
+
+        rows = rows_of(index ^ mask)
         for first in range(0, hidden, chunk):
             cols = slice(first, first + chunk)
             pre = jnp.dot(c_s[rows, :], w_up[:, cols], preferred_element_type=full_type)
@@ -498,23 +542,29 @@
         )
         return carry
 
-    lax.fori_loop(0, count, expand, 0)
+    middle_of(1)
+    lax.fori_loop(2, 4, expand, 0)
+    scatter.finish(3)
+    middle_of(0)
+    lax.fori_loop(0, 2, expand, 0)
+    scatter.finish(1)
     save(c_s, g_s, slope_s, mid_s)
-    bits = log2_of(count)
-    for bit in range(bits):
-        if bit == bits - 1:
-            embed_gather.arrive_all()
-            width = w_embed.shape[1]
-            for slot in range(count):
-                embed_full[:, slot * width : (slot + 1) * width] = embed_slots[slot]
-        scatter.finish_bit(bit)
+    embed_gather.arrive_all()
+    width = w_embed.shape[1]
+    for slot in range(count):
+        embed_full[:, slot * width : (slot + 1) * width] = embed_slots[slot]
+    scatter.finish(2)
     low_s[...] = (mid_s[...] + total[...]).astype(low_type)
     out = jnp.dot(low_s[...], embed_full[...], preferred_element_type=full_type)
     embedded[...] = out.astype(low_type).reshape(embedded.shape)
     swap.start()
     save(embed_full, low_s)
-    for one in (token_gather, out_gather, o_gather, embed_gather, scatter):
+    for one in (token_gather, embed_gather, scatter):
         one.drain()
+    out_copy.wait_send()
+    for mine in range(2):
+        for copy in (o_copy(mine), part_copy(mine), c_copy(mine)):
+            copy.wait_send()
     for move in stores:
         move.wait()
     swap.finish()
@@ -571,8 +621,11 @@
         + [
             pltpu.SemaphoreType.DMA((5 + len(shapes),)),
             pltpu.VMEM((model_count, rows, width), low_type),
-            pltpu.VMEM((width, width), low_type),
-            pltpu.VMEM((width, every), low_type),
+            pltpu.VMEM((2 * columns, width), low_type),
+            pltpu.VMEM((2, 2 * columns, rows), low_type),
+            pltpu.VMEM((2, rows, width), full_type),
+            pltpu.VMEM((2, rows, width), low_type),
+            pltpu.VMEM((2, rows, width), low_type),
             pltpu.VMEM((model_count,) + embed_proj.shape, low_type),
             pltpu.VMEM((model_count - 1, rows, width), low_type),
             pltpu.VMEM((model_count - 1, rows, width), low_type),
@@ -580,6 +633,7 @@
             pltpu.VMEM((images, visible, out_width), low_type),
             pltpu.SemaphoreType.DMA((10, model_count)),
             pltpu.SemaphoreType.DMA((2, images)),
+            pltpu.SemaphoreType.DMA((2, 7)),
         ],
         compiler_params=pltpu.CompilerParams(
             collective_id=1, has_side_effects=True, vmem_limit_bytes=60 * 2**20
@@ -2093,7 +2147,8 @@
     pred_proj,
     cotangent,
 ):
-    if kernel_bytes(tokens, enc_up, enc_query, dec_up, pred_proj) > VMEM_BUDGET:
+    fits = kernel_bytes(tokens, enc_up, enc_query, dec_up, pred_proj) <= VMEM_BUDGET
+    if not fits or lax.axis_size("mp") != 4:
         return per_device_plain(
             tokens,
             lengths,

time: 198 us -> 190 us (0.960)
  Pallas kernels: 196 us -> 188 us
    pallas_call x1, Pallas kernels: 49.9 us -> 41.8 us  [encode(): pl.pallas_call(kernel, out_shape=[jax.ShapeDtypeStruct(shape, kind) for s...]
where the time goes in v5:
time: 190 us
  Pallas kernels  188 us (99%)
    pallas_call x1, Pallas kernels, decode_and_back(): pl.pallas_call(kernel, out_shape=[jax.ShapeDtypeStruct(shape, kind) for s...  143 us
    pallas_call x1, Pallas kernels, encode(): pl.pallas_call(kernel, out_shape=[jax.ShapeDtypeStruct(shape, kind) for s...  41.8 us

profile of v5, /device:TPU:0, one launch (start us, length us, event | category | flops | bytes accessed | tf_op | source)
XLA Modules:
  0.0 189.7 jit_solution(17628844840044344968)
XLA Ops:
  0.7 41.8 %shard_map.400 = (bf16[2,64,512]{2,1,0:T(8,128)(2,1)}, bf16[512,1024]{1,0:T(8,128)(2,1)}, bf16[768,512]{1,0:T(8,128)(2,1)}, bf16[16,128,128]{2,1,0:T(8,128)(2,1)...) custom-call(s32[8]{0:T(128)} %refs_0_.2, ...), custom_call_target="tpu_custom_call" | custom-call | tf_op jit(solution)/shard_map/pallas_call | solution.py:603
  42.5 143.0 %shard_map.401 = (f32[2,256,768]{2,1,0:T(8,128)}, f32[128,1024]{1,0:T(8,128)}, f32[2,1024]{1,0:T(2,128)}, f32[3,512]{1,0:T(4,128)}, bf16[128,1792]{1,0:T(8,128)(...) custom-call(f32[2]{0:T(128)} %refs_0_.3, ...), custom_call_target="tpu_custom_call" | custom-call | tf_op jit(solution)/shard_map/pallas_call | solution.py:1602
  185.5 0.0 copy-start
  185.5 3.0 %shard_map.402 = (f32[128,1024]{1,0:T(8,128)}, f32[128,256]{1,0:T(8,128)}, f32[128,256]{1,0:T(8,128)}, f32[128,256]{1,0:T(8,128)}, f32[128,1024]{1,0:T(8,128)}, ...) custom-call(f32[128,1024]{1,0:T(8,128)} %get-tuple-element.76.refs_0, ...), custom_call_target="tpu_custom_call" | custom-call | tf_op jit(solution)/shard_map/pallas_call | solution.py:1648
  188.6 0.0 copy-done
  188.6 1.1 copy.47
Async XLA Ops:
  185.5 3.1 %copy-start = (f32[2,256,768]{2,1,0:T(8,128)S(1)}, f32[2,256,768]{2,1,0:T(8,128)}, u32[]{:S(2)}) copy-start(f32[2,256,768]{2,1,0:T(8,128)} %get-tuple-element.124) | copy-start | bytes 4718596

commit v6 on v5

--- a/solution.py
+++ b/solution.py
@@ -273,17 +273,21 @@
             device_id_type=MESH,
         )
 
+    def start_one(self, image):
+        data, model, slot = self.partners[image]
+        here = is_here((data, model))
+
+        @pl.when(here)
+        def _():
+            self.target[slot] = self.source[image]
+
+        @pl.when(jnp.logical_not(here))
+        def _():
+            self.copy(image).start()
+
     def start(self):
-        for image, (data, model, slot) in enumerate(self.partners):
-            here = is_here((data, model))
-
-            @pl.when(here)
-            def _():
-                self.target[slot] = self.source[image]
-
-            @pl.when(jnp.logical_not(here))
-            def _():
-                self.copy(image).start()
+        for image in range(len(self.partners)):
+            self.start_one(image)
 
     def finish(self):
         for image, (data, model, slot) in enumerate(self.partners):
@@ -310,7 +314,7 @@
             self.copy = None
 
 
-def encoder_barrier(images, axes):
+def signal_partners(images, axes):
     barrier = pltpu.get_barrier_semaphore()
     count = images
     for axis in axes:
@@ -321,7 +325,12 @@
             )
     for data, model, slot in exchange_partners(images):
         pl.semaphore_signal(barrier, inc=1, device_id=(data, model), device_id_type=MESH)
-    pl.semaphore_wait(barrier, count)
+    return count
+
+
+def encoder_barrier(images, axes):
+    count = signal_partners(images, axes)
+    pl.semaphore_wait(pltpu.get_barrier_semaphore(), count)
 
 
 def encoder_kernel(images, visible, heads, *refs):
@@ -337,9 +346,10 @@
         w_up_hbm,
         w_down_hbm,
         w_embed,
+        *dec_hbm,
         arrived,
-        *saved_hbm,
-    ) = refs[:24]
+    ) = refs[:15]
+    saved_hbm = refs[15:28]
     (
         w_query,
         w_key,
@@ -358,6 +368,10 @@
         low_s,
         embed_full,
         qkv_weights,
+        dec_turned,
+        dec_query,
+        dec_key,
+        dec_value,
         move_sems,
         token_slots,
         out_pair,
@@ -373,7 +387,7 @@
         sems,
         swap_sems,
         pair_sems,
-    ) = refs[24:]
+    ) = refs[28:]
     count = lax.axis_size("mp")
     index = lax.axis_index("mp")
     block_rows = images * visible
@@ -392,10 +406,14 @@
                 (w_value_hbm, w_value),
                 (w_up_hbm, w_up),
                 (w_down_hbm, w_down),
+                (dec_hbm[0], dec_query),
+                (dec_hbm[1], dec_key),
+                (dec_hbm[2], dec_value),
             )
         )
     ]
-    saved = [a_s, qkv_s, e_s, inv_s, o_own, c_s, g_s, slope_s, mid_s, low_s, embed_full, qkv_weights]
+    saved = [a_s, qkv_s, e_s, inv_s, o_own, c_s, g_s, slope_s, mid_s, low_s, embed_full]
+    saved += [qkv_weights, dec_turned]
     stores = []
 
     def save(*arrays):
@@ -448,7 +466,11 @@
     for position, weight in enumerate((w_query, w_key, w_value)):
         loads[position].wait()
         qkv_weights[position * columns : (position + 1) * columns, :] = weight[...].T
-    save(qkv_weights)
+    dec_width = dec_query.shape[0]
+    for position, weight in enumerate((dec_query, dec_key, dec_value)):
+        loads[5 + position].wait()
+        dec_turned[position * dec_width : (position + 1) * dec_width, :] = weight[...].T
+    save(qkv_weights, dec_turned)
 
     def attend(step, carry):
         token_gather.arrive_at(step)
@@ -570,7 +592,7 @@
     swap.finish()
 
 
-def encode(tokens, lengths, weights, embed_proj):
+def encode(tokens, lengths, weights, embed_proj, dec_inputs):
     gain_attn, w_query, w_key, w_value, w_out, gain_mlp, w_up, w_down = weights
     model_count = lax.axis_size("mp")
     images, visible, width = tokens.shape
@@ -599,6 +621,7 @@
         ((rows, width), low_type),
         ((width, out_width), low_type),
         ((3 * columns, width), low_type),
+        ((3 * out_width, out_width), low_type),
     ]
     return pl.pallas_call(
         kernel,
@@ -608,7 +631,8 @@
         + [hbm] * 3
         + [vmem] * 2
         + [hbm] * 2
-        + [vmem],
+        + [vmem]
+        + [hbm] * 3,
         out_specs=[vmem] + [hbm] * (len(shapes) - 1),
         scratch_shapes=[
             pltpu.VMEM((width, columns), low_type),
@@ -618,8 +642,9 @@
             pltpu.VMEM((hidden, width), low_type),
         ]
         + [pltpu.VMEM(shape, kind) for shape, kind in shapes[1:]]
+        + [pltpu.VMEM((out_width, out_width), low_type)] * 3
         + [
-            pltpu.SemaphoreType.DMA((5 + len(shapes),)),
+            pltpu.SemaphoreType.DMA((8 + len(shapes),)),
             pltpu.VMEM((model_count, rows, width), low_type),
             pltpu.VMEM((2 * columns, width), low_type),
             pltpu.VMEM((2, 2 * columns, rows), low_type),
@@ -650,146 +675,141 @@
         w_up,
         w_down,
         embed_proj,
+        *dec_inputs,
     )
 
 
 EARLY_DOWN, EARLY_UP, UP_FIRST = True, False, True
 SUM_ORDERS = {
-    "attn": ["crossed"],
-    "dup": ["spread", "spreadz", "all", "spreadz"],
-    "ddn": ["spread", "spread", "spread", "spread"],
-    "pred": ["all"],
-    "emb": ["spread", "spread"],
-    "dn": ["Z", "Y", "Y", "Y"],
-    "up": ["Y", "Y", "Y", "Y"],
+    "attn": ["all"],
+    "dup": ["spread", "all"],
+    "ddn": ["spreadz", "spread", "spread", "spreadz"],
+    "pred": ["spread", "spread"],
+    "emb": ["all"],
+    "dn": ["Y", "Z", "Y", "Y"],
+    "up": ["Y", "Y", "Z", "Y"],
     "oq": ["Y", "Y", "Y", "Y"],
 }
 PLAN = {
     "a3": [
         "pred0",
+        "pred1",
         "ddn0",
         "ddn1",
         "ddn2",
         "ddn3",
         "dup0",
         "dup1",
-        "dup2",
-        "dup3",
     ],
     "a4": [
+        "pred0",
         "ddn0",
-        "dup1",
-        "pred0",
-        "ddn1",
+        "pred1",
     ],
     "a5": [
-        "dup3",
-        "dup2",
+        "ddn3",
+        "dup1",
+        "ddn1",
+        "attn0",
+        "pred0",
         "ddn2",
-        "attn0",
-        "ddn0",
-        "ddn3",
     ],
     "f1": [
-        "ddn1",
-        "dup1",
-        "emb0",
-        "emb1",
-        "dup0",
+        "pred1",
+        "ddn0",
     ],
     "f2": [
-        "pred0",
-        "ddn2",
-        "dup3",
+        "emb0",
     ],
     "f3": [
-        "dup2",
+        "dup0",
+        "ddn1",
         "ddn3",
     ],
     "b0": [
+        "pred0",
+        "ddn2",
+        "dup1",
         "ddn0",
-        "dup1",
+        "pred1",
+        "ddn3",
+    ],
+    "d2": [
+        "dup0",
+    ],
+    "d3": [
         "ddn1",
-        "dup0",
-        "emb0",
-        "pred0",
-        "dup2",
-        "ddn2",
-        "emb1",
-        "dup3",
-        "ddn3",
     ],
     "s2": [
         "attn0",
-        "ddn0",
-        "dup1",
-    ],
-    "s3": [
-        "ddn1",
-        "ddn2",
-        "dup3",
+        "dn0",
     ],
     "b2": [
-        "ddn3",
-        "dn0",
         "dn1",
     ],
     "b4": [
+        "ddn2",
+        "dup1",
+        "emb0",
+        "dn2",
+        "pred0",
+        "ddn0",
+        "pred1",
+        "ddn3",
+        "ddn1",
         "dup0",
-        "emb0",
-        "pred0",
     ],
     "b5": [
-        "dup2",
-        "emb1",
-        "dn2",
+        "dn0",
+        "dn3",
+    ],
+    "t1": [
+        "ddn2",
         "dup0",
+        "dn1",
     ],
     "t2": [
+        "up2",
         "attn0",
-        "dn3",
-        "dn1",
-        "dn0",
+        "dup1",
+        "dn2",
         "up0",
     ],
-    "b6": [
-        "emb0",
-        "emb1",
-        "dn2",
+    "t3": [
+        "dn0",
+        "dn3",
     ],
     "b7": [
         "up1",
     ],
     "tail": [
-        "dn3",
         "attn0",
         "up2",
+        "up3",
+        "dn2",
+        "up0",
+        "emb0",
+        "norm",
         "dn1",
+        "dn3",
+        "up1",
+        "norm",
+        "attn0",
+        "up3",
+        "o",
         "emb0",
         "up0",
-        "emb1",
-        "norm",
-        "up3",
-        "dn2",
-        "up1",
-        "norm",
-        "dn0",
-        "dn3",
-        "up2",
-        "o",
-        "up0",
-        "up3",
         "q",
         "up1",
-        "up2",
+        "up3",
         "o",
         "k",
-        "up3",
+        "emb0",
         "q",
+        "o",
         "v",
-        "o",
         "k",
-        "attn0",
+        "up2",
         "norm",
         "q",
         "v",
@@ -842,7 +862,7 @@
         gain_attn,
         gain_mlp,
     ) = take(10)
-    dec_hbm = take(8)
+    dec_hbm = take(6)
     enc_hbm = take(15)
     decoded, grad_tokens, norm_wide, norm_thin, rows_out, cols_out, dec_out, embed_out = take(8)
     move_sems, decoded_sems = take(2)
@@ -952,19 +972,9 @@
         scaling = float(size) ** -0.5
         place = lax.broadcasted_iota(jnp.int32, (length, visible), 0)
         turn = lax.broadcasted_iota(jnp.int32, (length, visible), 1)
-        out_move = Move(dec_hbm[3], w_out, move_sems.at[3])
-
-        def turned(*inputs):
-            turned_moves = [
-                Move(dec_hbm[position], one, move_sems.at[position])
-                for position, one in enumerate(inputs)
-            ]
-            encoder_barrier(images, ["mp", "dp"])
-            for position, one in enumerate(inputs):
-                turned_moves[position].wait()
-                qkv_weights[position * width : (position + 1) * width, :] = one[...].T
-
-        pl.run_scoped(turned, *scopes[3])
+        arrivals = signal_partners(images, ["mp", "dp"])
+        turned_move = Move(dec_hbm[0], qkv_weights, move_sems.at[0])
+        out_move = Move(dec_hbm[1], w_out, move_sems.at[1])
 
         def picks(image):
             order = jnp.zeros((1, visible), jnp.int32)
@@ -983,14 +993,13 @@
         def dense(w_up, w_down, w_pred, cotangent, mid_s, c_s, g_s, du_s, low_s, dm_s, staged):
             hidden = w_up.shape[1]
             second_moves = [
-                Move(source, target, move_sems.at[4 + position])
+                Move(source, target, move_sems.at[2 + position])
                 for position, (source, target) in enumerate(
-                    zip(dec_hbm[4:], (w_up, w_down, w_pred, cotangent))
+                    zip(dec_hbm[2:], (w_up, w_down, w_pred, cotangent))
                 )
             ]
+            turned_move.wait()
             out_move.wait()
-            for move in second_moves:
-                move.wait()
             small[...] = jnp.zeros_like(small)
 
             def stage_copy(image):
@@ -1046,6 +1055,12 @@
                 mid_s[...] = middle
                 normed, scale = norm_parts(middle)
                 c_s[rows, :] = (normed * dec_gain_mlp[...]).astype(low_type)
+
+                @pl.when(image == 0)
+                def _():
+                    for move in second_moves:
+                        move.wait()
+
                 for first in range(0, hidden, chunk):
                     cols = slice(first, first + chunk)
                     pre = jnp.dot(c_s[rows, :], w_up[:, cols], preferred_element_type=full_type)
@@ -1087,6 +1102,7 @@
             lax.fori_loop(0, images, one_image, 0)
             all_pixels = cotangent[...].reshape(-1, cotangent.shape[2])
             store_dec(6, dot_as(low_s[...], all_pixels, 0, 0))
+            pl.semaphore_wait(pltpu.get_barrier_semaphore(), arrivals)
             start("pred")
             store_dec(5, dot_as(g_s[...], dm_s[...], 0, 0))
             start("ddn")
@@ -1136,9 +1152,9 @@
             grad_arrived[image] = dot_as(
                 pick.astype(low_type), grad_start.astype(low_type), 0, 0
             ).astype(low_type)
+            swap.start_one(image)
             if image == 0:
                 pump("a3")
-        swap.start()
         for position in range(3):
             grads = qkv_s[position * width : (position + 1) * width, :]
             store_dec(position, dot_as(a_s[...], grads, 0, 1))
@@ -1176,7 +1192,7 @@
         scaling = float(size) ** -0.5
         hidden, width = w_down.shape
         moves = {}
-        for position in (13, 2, 10, 1, 9, 11, 8, 12, 0, 4, 5, 6, 7, 14, 3):
+        for position in (12, 13, 9, 2, 10, 1, 11, 8, 0, 4, 5, 6, 7, 14, 3):
             moves[position] = Move(enc_hbm[position], loaded[position], move_sems.at[8 + position])
 
         def ready(*arrays):
@@ -1235,7 +1251,7 @@
                             ].astype(low_type)
         start("emb")
         pump("a5")
-        ready(embed_full, w_down, slope_s)
+        ready(embed_full)
 
         def rows_of(slot):
             return pl.ds(pl.multiple_of(slot * block_rows, block_rows), block_rows)
@@ -1254,6 +1270,11 @@
                 dy_s[...] = grad_out
 
             dm_s[rows, :] = grad_out.astype(low_type)
+            return carry
+
+        def active_back(step, carry):
+            pump_at(step, "d")
+            rows = rows_of(index ^ visit_mask(step, count))
             for first in range(0, hidden, chunk):
                 cols = slice(first, first + chunk)
                 grad_active = dot_as(dm_s[rows, :], w_down[cols, :], 1, 1)
@@ -1298,6 +1319,8 @@
 
         if EARLY_DOWN:
             down_grads()
+        ready(w_down, slope_s)
+        lax.fori_loop(0, count, active_back, 0)
         if EARLY_UP:
             up_grads()
         ready(w_up)
@@ -1476,6 +1499,7 @@
     tokens,
     weights,
     saved,
+    dec_turned,
     embed_proj,
 ):
     gain_attn, w_query, w_key, w_value, w_out, gain_mlp, w_up, w_down = weights
@@ -1508,7 +1532,6 @@
     low = lambda *shape: pltpu.VMEM(shape, low_type)
     full = lambda *shape: pltpu.VMEM(shape, full_type)
     loaded = [w_out, w_up, w_down, *saved]
-    turned_scope = [low(out_width, out_width)] * 3
     attn_scope = [
         low(out_width, out_width),
         full(grid_rows, out_width),
@@ -1550,7 +1573,7 @@
         SIDE,
         pieces,
         embed_pieces[0],
-        (attn_scope, dense_scope, enc_scope, turned_scope),
+        (attn_scope, dense_scope, enc_scope),
     )
 
     def kernel(*refs):
@@ -1602,7 +1625,7 @@
     results = pl.pallas_call(
         kernel,
         out_shape=[jax.ShapeDtypeStruct(shape, kind) for shape, kind in outs],
-        in_specs=[pl.BlockSpec(memory_space=pltpu.SMEM)] + [vmem] * 9 + [hbm] * (8 + len(loaded)),
+        in_specs=[pl.BlockSpec(memory_space=pltpu.SMEM)] + [vmem] * 9 + [hbm] * (6 + len(loaded)),
         out_specs=[hbm] + [vmem] * (len(outs) - 1),
         scratch_shapes=scratch,
         compiler_params=pltpu.CompilerParams(
@@ -1619,9 +1642,7 @@
         tokens.reshape(rows, width),
         gain_attn.reshape(1, -1),
         gain_mlp.reshape(1, -1),
-        dec_query,
-        dec_key,
-        dec_value,
+        dec_turned,
         dec_proj,
         dec_up,
         dec_down,
@@ -2178,7 +2199,8 @@
         )
     enc_weights = (enc_norm, enc_query, enc_key, enc_value, enc_proj, enc_norm2, enc_up, enc_down)
     dec_weights = (dec_norm, dec_query, dec_key, dec_value, dec_proj, dec_norm2, dec_up, dec_down)
-    arrived, *saved = encode(tokens, lengths, enc_weights, embed_proj)
+    dec_inputs = (dec_query, dec_key, dec_value)
+    arrived, *saved, dec_turned = encode(tokens, lengths, enc_weights, embed_proj, dec_inputs)
     decoded, grads = decode_and_back(
         arrived,
         grid_order,
@@ -2191,6 +2213,7 @@
         tokens,
         enc_weights,
         saved,
+        dec_turned,
         embed_proj,
     )
     (

time: 190 us -> 185 us (0.974)
  Pallas kernels: 188 us -> 182 us
    pallas_call x1, Pallas kernels: 143 us -> 136 us  [decode_and_back(): pl.pallas_call(kernel, out_shape=[jax.ShapeDtypeStruct(shape, kind) for s...]
where the time goes in v6:
time: 185 us; the launch traced here: 184 us
  Pallas kernels  182 us (98%)
    pallas_call x1, Pallas kernels, decode_and_back(): pl.pallas_call(kernel, out_shape=[jax.ShapeDtypeStruct(shape, kind) for s...  136 us
    pallas_call x1, Pallas kernels, encode(): pl.pallas_call(kernel, out_shape=[jax.ShapeDtypeStruct(shape, kind) for s...  42.6 us

profile of v6, /device:TPU:0, one launch (start us, length us, event | category | flops | bytes accessed | tf_op | source)
XLA Modules:
  0.0 183.8 jit_solution(8837619786101966358)
XLA Ops:
  0.7 42.6 %shard_map.400 = (bf16[2,64,512]{2,1,0:T(8,128)(2,1)}, bf16[512,1024]{1,0:T(8,128)(2,1)}, bf16[768,512]{1,0:T(8,128)(2,1)}, bf16[16,128,128]{2,1,0:T(8,128)(2,1)...) custom-call(s32[8]{0:T(128)} %refs_0_.2, ...), custom_call_target="tpu_custom_call" | custom-call | tf_op jit(solution)/shard_map/pallas_call | solution.py:626
  43.3 136.3 %shard_map.401 = (f32[2,256,768]{2,1,0:T(8,128)}, f32[128,1024]{1,0:T(8,128)}, f32[2,1024]{1,0:T(2,128)}, f32[3,512]{1,0:T(4,128)}, bf16[128,1792]{1,0:T(8,128)(...) custom-call(f32[2]{0:T(128)} %refs_0_.3, ...), custom_call_target="tpu_custom_call" | custom-call | tf_op jit(solution)/shard_map/pallas_call | solution.py:1625
  179.6 0.0 copy-start
  179.6 3.0 %shard_map.402 = (f32[128,1024]{1,0:T(8,128)}, f32[128,256]{1,0:T(8,128)}, f32[128,256]{1,0:T(8,128)}, f32[128,256]{1,0:T(8,128)}, f32[128,1024]{1,0:T(8,128)}, ...) custom-call(f32[128,1024]{1,0:T(8,128)} %get-tuple-element.78.refs_0, ...), custom_call_target="tpu_custom_call" | custom-call | tf_op jit(solution)/shard_map/pallas_call | solution.py:1669
  182.6 0.0 copy-done
  182.6 1.1 copy.47
Async XLA Ops:
  179.6 3.1 %copy-start = (f32[2,256,768]{2,1,0:T(8,128)S(1)}, f32[2,256,768]{2,1,0:T(8,128)}, u32[]{:S(2)}) copy-start(f32[2,256,768]{2,1,0:T(8,128)} %get-tuple-element.126) | copy-start | bytes 4718596

commit v7 on v6

--- a/solution.py
+++ b/solution.py
@@ -577,9 +577,11 @@
         embed_full[:, slot * width : (slot + 1) * width] = embed_slots[slot]
     scatter.finish(2)
     low_s[...] = (mid_s[...] + total[...]).astype(low_type)
-    out = jnp.dot(low_s[...], embed_full[...], preferred_element_type=full_type)
-    embedded[...] = out.astype(low_type).reshape(embedded.shape)
-    swap.start()
+    for image in range(images):
+        own = low_s[image * visible : (image + 1) * visible, :]
+        out = jnp.dot(own, embed_full[...], preferred_element_type=full_type)
+        embedded[image] = out.astype(low_type)
+        swap.start_one(image)
     save(embed_full, low_s)
     for one in (token_gather, embed_gather, scatter):
         one.drain()
@@ -864,7 +866,7 @@
     ) = take(10)
     dec_hbm = take(6)
     enc_hbm = take(15)
-    decoded, grad_tokens, norm_wide, norm_thin, rows_out, cols_out, dec_out, embed_out = take(8)
+    decoded, tokens_out, norm_wide, norm_thin, rows_out, cols_out, dec_out, embed_out = take(8)
     move_sems, decoded_sems = take(2)
     grad_arrived, dec_packed, small = take(3)
     demb_own, demb_slots, db_s, total = take(4)
@@ -1409,7 +1411,8 @@
         normed, scale = norm_parts(tokens[...].astype(full_type))
         grad_normed = total[...]
         wide_acc[0, 0:1, :] = jnp.sum(grad_normed * normed, axis=0, keepdims=True)
-        grad_tokens[...] = dy_s[...] + norm_back(normed, scale, grad_normed * gain_attn[...])
+        dy_s[...] = dy_s[...] + norm_back(normed, scale, grad_normed * gain_attn[...])
+        tokens_move = Move(dy_s, tokens_out, move_sems.at[0])
 
         def norm_copies(stage):
             peer = partner(*all_stages[stage])[0]
@@ -1453,6 +1456,7 @@
         norm_thin[...] = thin_acc[len(all_stages)]
         for one in (demb_gather, scatter, db_gather, second_scatter):
             one.drain()
+        tokens_move.wait()
 
 
     pl.run_scoped(encoder, *scopes[2])
@@ -1626,7 +1630,7 @@
         kernel,
         out_shape=[jax.ShapeDtypeStruct(shape, kind) for shape, kind in outs],
         in_specs=[pl.BlockSpec(memory_space=pltpu.SMEM)] + [vmem] * 9 + [hbm] * (6 + len(loaded)),
-        out_specs=[hbm] + [vmem] * (len(outs) - 1),
+        out_specs=[hbm] * 2 + [vmem] * (len(outs) - 2),
         scratch_shapes=scratch,
         compiler_params=pltpu.CompilerParams(
             collective_id=2, has_side_effects=True, vmem_limit_bytes=255 * 2**18

time: 185 us -> 184 us (level)
  no operation moved by 1% of the time
where the time goes in v7:
time: 184 us
  Pallas kernels  182 us (99%)
    pallas_call x1, Pallas kernels, decode_and_back(): pl.pallas_call(kernel, out_shape=[jax.ShapeDtypeStruct(shape, kind) for s...  136 us
    pallas_call x1, Pallas kernels, encode(): pl.pallas_call(kernel, out_shape=[jax.ShapeDtypeStruct(shape, kind) for s...  42.6 us

profile of v7, /device:TPU:0, one launch (start us, length us, event | category | flops | bytes accessed | tf_op | source)
XLA Modules:
  0.0 183.6 jit_solution(11906766051674486035)
XLA Ops:
  0.7 42.6 %shard_map.400 = (bf16[2,64,512]{2,1,0:T(8,128)(2,1)}, bf16[512,1024]{1,0:T(8,128)(2,1)}, bf16[768,512]{1,0:T(8,128)(2,1)}, bf16[16,128,128]{2,1,0:T(8,128)(2,1)...) custom-call(s32[8]{0:T(128)} %refs_0_.2, ...), custom_call_target="tpu_custom_call" | custom-call | tf_op jit(solution)/shard_map/pallas_call | solution.py:628
  43.3 136.1 %shard_map.401 = (f32[2,256,768]{2,1,0:T(8,128)}, f32[128,1024]{1,0:T(8,128)}, f32[2,1024]{1,0:T(2,128)}, f32[3,512]{1,0:T(4,128)}, bf16[128,1792]{1,0:T(8,128)(...) custom-call(f32[2]{0:T(128)} %refs_0_.3, ...), custom_call_target="tpu_custom_call" | custom-call | tf_op jit(solution)/shard_map/pallas_call | solution.py:1629
  179.4 0.0 copy-start
  179.4 3.0 %shard_map.402 = (f32[128,1024]{1,0:T(8,128)}, f32[128,256]{1,0:T(8,128)}, f32[128,256]{1,0:T(8,128)}, f32[128,256]{1,0:T(8,128)}, f32[128,1024]{1,0:T(8,128)}, ...) custom-call(f32[128,1024]{1,0:T(8,128)} %get-tuple-element.78.refs_0, ...), custom_call_target="tpu_custom_call" | custom-call | tf_op jit(solution)/shard_map/pallas_call | solution.py:1673
  182.4 0.0 copy-done
  182.4 1.1 copy.47
Async XLA Ops:
  179.4 3.1 %copy-start = (f32[2,256,768]{2,1,0:T(8,128)S(1)}, f32[2,256,768]{2,1,0:T(8,128)}, u32[]{:S(2)}) copy-start(f32[2,256,768]{2,1,0:T(8,128)} %get-tuple-element.126) | copy-start | bytes 4718596
